TPU v7x, 32 devices: a whole 2x2x4 slice. The times are simulated.
32 devices in a mesh: groups: 2 (over x), ctx: 16 (over z, y, core).
Axes of the slice: x: 2, y: 2, z: 4, core: 2. Of those that a mesh axis runs over, the one named last changes fastest.
Arguments:
- residual: bfloat16 [4096, 2048], P(('groups', 'ctx')), parts along dimension 0, may hold values from -200 to 200
- queries: bfloat16 [4096, 2048], P(('groups', 'ctx')), parts along dimension 0, may hold values from -64 to 64
- keys: bfloat16 [4096, 256], P(('groups', 'ctx')), parts along dimension 0, may hold values from -64 to 64
- values: bfloat16 [4096, 256], P(('groups', 'ctx')), parts along dimension 0, may hold values from -6 to 6
- block_order: int32 [32], P('groups'), parts along dimension 0, may hold values from 0 to 3, as said below
- routes: int32 [4096, 8], P(('groups', 'ctx')), parts along dimension 0, may hold values from 0 to 15, as said below
- route_weights: float32 [4096, 8], P(('groups', 'ctx')), parts along dimension 0, may hold values from 0.1 to 1
- out_weight: bfloat16 [2048, 2048], P(None, 'ctx'), may hold values from -0.125 to 0.125
- norm_gain: float32 [2048], replicated, may hold values from 0.5 to 1.5
- w_gate_up: bfloat16 [16, 2048, 1536], P('ctx'), may hold values from -0.125 to 0.125
- w_down: bfloat16 [16, 768, 2048], P('ctx'), may hold values from -0.21875 to 0.21875
Outputs:
- context: bfloat16 [4096, 2048], P(('groups', 'ctx')), parts along dimension 0
- mixed: bfloat16 [4096, 2048], P(('groups', 'ctx')), parts along dimension 0
There are 2 independent parts, one for each index of `groups`. A program takes and returns all parts, laid end to end along the dimension named above; an argument that names none is the same for every part. Nothing has to cross between parts.
Inputs may be any that keep to these rules, and one draw needn't show every extreme that they name: `block_order`: for each i below 4, the entries at the indices congruent to i modulo 4 hold every number from 0 to 3 once. `routes`: each token names 8 different experts. Among the tokens of one device no expert is named more than 72 times, and some expert is named exactly 72 times by the tokens of every device.
All inputs are finite; a program needn't handle non-finite values.
Results may differ from a plain program's by a relative error of at most 0.005.
Values may be sent and summed in bfloat16 or wider, within the bound.
No kernel may reach another device: no remote copies, remote signals or barrier semaphores. Data moves between devices by JAX's collectives and lax.ppermute only.
A program may use at most 128 MiB of HBM per device.

v0:
```python
import jax
import jax.numpy as jnp
from jax import lax
from jax.sharding import PartitionSpec as P

D = 2048
HEAD_SIZE = 128
FF = 768
QUERY_HEADS = 16
KEY_VALUE_HEADS = 2
TOPK = 8
SEQS = 4


def shifted(array, axis, by):
    devices = lax.axis_size(axis)
    return lax.ppermute(array, axis, [(i, (i + by) % devices) for i in range(devices)])


def local(
    residual,
    queries,
    keys,
    values,
    block_order,
    routes,
    route_weights,
    out_weight,
    norm_gain,
    w_gate_up,
    w_down,
):
    device_row_count = queries.shape[0]
    query_group_width = QUERY_HEADS // KEY_VALUE_HEADS
    devices = lax.axis_size("ctx")
    cycle_length = devices // SEQS
    own_index = lax.axis_index("ctx")
    full_weight = lax.all_gather(out_weight, "ctx", axis=1, tiled=True)
    query_position = block_order[own_index]
    query_head_rows = (
        queries.reshape(device_row_count, KEY_VALUE_HEADS, query_group_width, HEAD_SIZE)
        .transpose(1, 2, 0, 3)
        .reshape(KEY_VALUE_HEADS, query_group_width * device_row_count, HEAD_SIZE)
    )
    query_offset = jnp.arange(query_group_width * device_row_count) % device_row_count
    key_offset = jnp.arange(device_row_count)
    scale = HEAD_SIZE ** (-0.5)

    def update(carry, key_value_tuple, key_position):
        summed, running_max, totals = carry
        local_key_block = key_value_tuple[0].reshape(device_row_count, KEY_VALUE_HEADS, HEAD_SIZE)
        local_value_block = key_value_tuple[1].reshape(device_row_count, KEY_VALUE_HEADS, HEAD_SIZE)
        scores = (
            jnp.einsum(
                "hqd,khd->hqk", query_head_rows, local_key_block, preferred_element_type=jnp.float32
            )
            * scale
        )
        visible = (
            key_position * device_row_count + key_offset[None, :]
            <= query_position * device_row_count + query_offset[:, None]
        )
        scores = jnp.where(visible[None], scores, -jnp.inf)
        new_max = jnp.maximum(running_max, jnp.max(scores, axis=-1))
        factor = jnp.exp(running_max - new_max)
        weights = jnp.exp(scores - new_max[..., None])
        totals = totals * factor + jnp.sum(weights, axis=-1)
        summed = summed * factor[..., None] + jnp.einsum(
            "hqk,khd->hqd",
            weights.astype(jnp.bfloat16),
            local_value_block,
            preferred_element_type=jnp.float32,
        )
        return (summed, new_max, totals)

    initial = (
        jnp.zeros((KEY_VALUE_HEADS, query_group_width * device_row_count, HEAD_SIZE), jnp.float32),
        jnp.full((KEY_VALUE_HEADS, query_group_width * device_row_count), -jnp.inf, jnp.float32),
        jnp.zeros((KEY_VALUE_HEADS, query_group_width * device_row_count), jnp.float32),
    )
    local_pair = jnp.stack([keys, values])
    carry = update(initial, local_pair, query_position)

    def advance(step, state):
        current, moving = state
        moving = shifted(moving, "ctx", SEQS)
        anchor = jnp.mod(own_index - SEQS * step, devices)
        key_position = block_order[anchor]
        current = lax.cond(
            key_position <= query_position,
            lambda inner: update(inner, moving, key_position),
            lambda inner: inner,
            current,
        )
        return (current, moving)

    carry, passed = lax.fori_loop(1, cycle_length, advance, (carry, local_pair))
    summed, running_max, totals = carry
    context = (
        (summed / totals[..., None])
        .reshape(KEY_VALUE_HEADS, query_group_width, device_row_count, HEAD_SIZE)
        .transpose(2, 0, 1, 3)
        .reshape(device_row_count, QUERY_HEADS * HEAD_SIZE)
        .astype(jnp.bfloat16)
    )
    projected = jnp.dot(context, full_weight, preferred_element_type=jnp.float32)
    updated = residual.astype(jnp.float32) + projected
    normed = (
        updated * lax.rsqrt(jnp.mean(updated * updated, axis=-1, keepdims=True) + 1e-06) * norm_gain
    ).astype(jnp.bfloat16)
    experts = devices * w_gate_up.shape[0]
    capacity = 9 * device_row_count * TOPK // (8 * experts)
    expert_ids = routes.reshape(-1)
    one_hot = (expert_ids[:, None] == jnp.arange(experts, dtype=jnp.int32)[None, :]).astype(
        jnp.int32
    )
    ranks = jnp.sum(jnp.cumsum(one_hot, axis=0) * one_hot, axis=1) - 1
    target = expert_ids * capacity + ranks
    source_row = jnp.arange(device_row_count * TOPK) // TOPK
    outgoing = (
        jnp.zeros((experts * capacity, D), jnp.bfloat16)
        .at[target]
        .set(normed[source_row])
        .reshape(experts, capacity, D)
    )
    arrived = lax.all_to_all(outgoing, "ctx", split_axis=0, concat_axis=0, tiled=True)
    flat = arrived.reshape(-1, D)
    both = jnp.dot(flat, w_gate_up[0], preferred_element_type=jnp.float32)
    hidden = (jax.nn.silu(both[:, :FF]) * both[:, FF:]).astype(jnp.bfloat16)
    result = (
        jnp.dot(hidden, w_down[0], preferred_element_type=jnp.float32)
        .astype(jnp.bfloat16)
        .reshape(arrived.shape)
    )
    returned = lax.all_to_all(result, "ctx", split_axis=0, concat_axis=0, tiled=True)
    gathered = returned.reshape(-1, D)[target].reshape(device_row_count, TOPK, D)
    gates = route_weights / jnp.sum(route_weights, axis=-1, keepdims=True)
    mixed = updated
    for slot in range(TOPK):
        mixed = mixed + gates[:, slot : slot + 1] * gathered[:, slot].astype(jnp.float32)
    return (context, mixed.astype(jnp.bfloat16))


def solution(mesh):
    placed = (
        P(("groups", "ctx"), None),
        P(("groups", "ctx"), None),
        P(("groups", "ctx"), None),
        P(("groups", "ctx"), None),
        P("groups"),
        P(("groups", "ctx"), None),
        P(("groups", "ctx"), None),
        P(None, "ctx"),
        P(),
        P("ctx", None, None),
        P("ctx", None, None),
    )
    return jax.shard_map(
        local,
        mesh=mesh,
        in_specs=placed,
        out_specs=(P(("groups", "ctx"), None), P(("groups", "ctx"), None)),
        check_vma=False,
    )
```

profile of v0, /device:TPU:15, one launch (start us, length us, event | category | flops | bytes accessed | tf_op | source)
XLA Modules:
  0.0 405.8 jit_solution(8898957640358070973)
XLA Ops:
  7.2 0.0 all-gather.2.cloned.1.call-start
  7.2 0.7 all-gather.2.cloned.1.call-update
  7.9 0.9 copy.32
  8.9 0.1 eq.39
  9.0 0.1 eq.35
  9.1 1.1 copy.58
  10.2 0.9 copy.24
  11.1 0.9 copy.28
  12.1 1.0 copy.29
  13.1 1.3 dynamic_slice.13
  15.1 0.7 pad_maximum_fusion
  15.8 0.1 broadcast_compare_fusion.1
  15.9 1.4 fusion.49
  17.3 0.2 fusion.29
  17.5 1.6 convolution_add_fusion.2
  19.1 42.5 %while.22 = (s32[]{:T(128)}, f32[2,1024,128]{2,1,0:T(8,128)}, f32[2,1024]{1,0:T(2,128)S(1)}, f32[2,1024]{1,0:T(2,128)S(1)}, bf16[2,128,256]{1,2,0:T(8,128)(2,1)S...) while((s32[]{:T(128)}, f32[2,1024,128]{2,1,0:T(8,128)}, ...), condition=%wide.region_7.8_spmd.clone, body=%wide.region_2.7_spmd.clone.sunk | while | flops 136719504 | bytes 7379506 | solution.py:97
  19.1 1.3 collective-permute-start
  20.4 0.6 dynamic_slice.16
  22.4 6.5 %collective-permute-done = bf16[2,128,256]{1,2,0:T(8,128)(2,1)S(1)} collective-permute-done((bf16[2,128,256]{1,2,0:T(8,128)(2,1)S(1)}, bf16[2,128,256]{1,2,0:T(8,128)(2,1)S(1)}, u32[]{:S(2)}, u32[]{:S(2)}) %collective-permute-start) | collective-permute-done | bytes 131104 | tf_op jit(solution)/shard_map/while/body/eval_jaxpr/ppermute | solution.py:17
  28.9 8.3 %collective-permute-start = (bf16[2,128,256]{1,2,0:T(8,128)(2,1)S(1)}, bf16[2,128,256]{1,2,0:T(8,128)(2,1)S(1)}, u32[]{:S(2)}, u32[]{:S(2)}) collective-permute-start(bf16[2,128,256]{1,2,0:T(8,128)(2,1)S(1)} %get-tuple-element.515), channel_id=1, source_target_pairs={{0,4},{1,5},{2,6},{3,7},{4,8},{5,9},{6,10},{7,11},{8,12},{9,13},{1... | collective-permute-start | bytes 393224 | tf_op jit(solution)/shard_map/while/body/eval_jaxpr/ppermute | solution.py:17
  37.3 0.6 dynamic_slice.16
  39.2 4.7 %collective-permute-done = bf16[2,128,256]{1,2,0:T(8,128)(2,1)S(1)} collective-permute-done((bf16[2,128,256]{1,2,0:T(8,128)(2,1)S(1)}, bf16[2,128,256]{1,2,0:T(8,128)(2,1)S(1)}, u32[]{:S(2)}, u32[]{:S(2)}) %collective-permute-start) | collective-permute-done | bytes 131104 | tf_op jit(solution)/shard_map/while/body/eval_jaxpr/ppermute | solution.py:17
  43.9 8.3 %collective-permute-start = (bf16[2,128,256]{1,2,0:T(8,128)(2,1)S(1)}, bf16[2,128,256]{1,2,0:T(8,128)(2,1)S(1)}, u32[]{:S(2)}, u32[]{:S(2)}) collective-permute-start(bf16[2,128,256]{1,2,0:T(8,128)(2,1)S(1)} %get-tuple-element.515), channel_id=1, source_target_pairs={{0,4},{1,5},{2,6},{3,7},{4,8},{5,9},{6,10},{7,11},{8,12},{9,13},{1... | collective-permute-start | bytes 393224 | tf_op jit(solution)/shard_map/while/body/eval_jaxpr/ppermute | solution.py:17
  52.2 0.6 dynamic_slice.16
  54.1 7.4 %collective-permute-done = bf16[2,128,256]{1,2,0:T(8,128)(2,1)S(1)} collective-permute-done((bf16[2,128,256]{1,2,0:T(8,128)(2,1)S(1)}, bf16[2,128,256]{1,2,0:T(8,128)(2,1)S(1)}, u32[]{:S(2)}, u32[]{:S(2)}) %collective-permute-start) | collective-permute-done | bytes 131104 | tf_op jit(solution)/shard_map/while/body/eval_jaxpr/ppermute | solution.py:17
  61.6 1.6 divide_convert_fusion
  63.3 0.3 copy.30
  63.6 0.9 copy.97
  64.5 4.5 %reduce-window.6 = s32[16,8,128]{2,1,0:T(8,128)S(1)} reduce-window(s32[16,8,128]{2,1,0:T(8,128)S(1)} %fusion.39, s32[]{:T(128)} %constant.121.clone.1), window={size=1x1x128 pad=0_0x0_0x127_0}, to_apply=%region_9.10 | reduce-window | flops 2080768 | bytes 131076 | tf_op jit(solution)/shard_map/reduce-window
  69.1 0.1 slice.92
  69.1 0.1 copy.34
  69.3 0.1 copy.35
  69.4 0.1 copy.31
  69.5 0.1 mul.174
  69.6 0.1 broadcast_add_fusion.1
  69.8 21.6 %all-gather.2.cloned.1.call-done = bf16[2048,2048]{1,0:T(8,128)(2,1)} async-done(((bf16[2048,128]{1,0:T(8,128)(2,1)}), bf16[2048,2048]{1,0:T(8,128)(2,1)}) %all-gather.2.cloned.1.call-update) | async-done | bytes 8388624 | tf_op jit(solution)/shard_map/all_gather | solution.py:38
  91.4 5.0 %multiply_reduce_fusion = (f32[128]{0:T(128)S(1)}, f32[128,2048]{1,0:T(8,128)S(1)}) fusion(bf16[128,2048]{1,0:T(8,128)(2,1)} %bitcast.138, bf16[2048,2048]{1,0:T(8,128)(2,1)} %all-gather.2.cloned.1.call-done, bf16[128,2048]{1,0:T(8,128)(2,1)} %param.15), kind=kOutput, calls=%fused_computation.52 | convolution fusion | flops 1074790272 | bytes 10486272 | tf_op jit(solution)/shard_map/dot_general | solution.py:106
  96.4 1.0 copy-done.2
  97.3 0.9 multiply_convert_fusion
  98.3 23.8 %scatter_custom_fusion = bf16[1152,2048]{1,0:T(8,128)(2,1)} fusion(s32[1024]{0:T(1024)S(1)} %bitcast.148, bf16[128,2048]{1,0:T(8,128)(2,1)} %multiply_convert_fusion, s32[1024]{0:T(1024)S(1)} %broadcast_clamp_fusion.1, bf16[]{:T(256)} %constant.129.clone.1), kind=kCustom, calls=%fused_computation.23 | custom fusion | bytes 4719104 | tf_op jit(solution)/shard_map/scatter | solution.py:123
  122.1 113.3 %all_to_all.10 = bf16[16,72,2048]{2,1,0:T(8,128)(2,1)S(1)} all-to-all(bf16[16,72,2048]{2,1,0:T(8,128)(2,1)} %bitcast.133), channel_id=1, replica_groups=mesh['groups'=2,'ctx'=16] {'ctx'}, dimensions={0} | all-to-all | bytes 9437184 | tf_op jit(solution)/shard_map/all_to_all | solution.py:126
  235.3 9.7 %fusion.10 = f32[1152,1536]{1,0:T(8,128)S(1)} fusion(bf16[1152,2048]{1,0:T(8,128)(2,1)S(1)} %bitcast.137, bf16[1,2048,1536]{2,1,0:T(8,128)(2,1)} %param.24), kind=kOutput, calls=%fused_computation.21 | convolution fusion | flops 7247757312 | bytes 18087936 | tf_op jit(solution)/shard_map/dot_general | solution.py:128
  245.0 5.7 %convolution_convert_fusion = bf16[1152,2048]{1,0:T(8,128)(2,1)} fusion(bf16[1,768,2048]{2,1,0:T(8,128)(2,1)S(1)} %copy-done, f32[1152,1536]{1,0:T(8,128)S(1)} %fusion.10), kind=kOutput, calls=%fused_computation.20 | convolution fusion | flops 3631546368 | bytes 14942208 | tf_op jit(solution)/shard_map/dot_general | solution.py:131
  250.7 4.9 %all-to-all-start.1 = ((bf16[16,72,2048]{2,1,0:T(8,128)(2,1)}), bf16[16,72,2048]{2,1,0:T(8,128)(2,1)}, u32[]{:S(2)}, u32[]{:S(2)}) async-start(bf16[16,72,2048]{2,1,0:T(8,128)(2,1)} %bitcast.136), calls=%async_computation.1 | async-start | bytes 9437184 | tf_op jit(solution)/shard_map/all_to_all | solution.py:135
  255.7 103.6 %all-to-all-done.1 = bf16[16,72,2048]{2,1,0:T(8,128)(2,1)} async-done(((bf16[16,72,2048]{2,1,0:T(8,128)(2,1)}), bf16[16,72,2048]{2,1,0:T(8,128)(2,1)}, u32[]{:S(2)}, u32[]{:S(2)}) %all-to-all-start.1) | async-done | bytes 4718624 | tf_op jit(solution)/shard_map/all_to_all | solution.py:135
  359.3 11.8 %gather_fusion = bf16[1024,2048]{1,0:T(8,128)(2,1)} fusion(bf16[1152,2048]{1,0:T(8,128)(2,1)} %bitcast.20, s32[1024]{0:T(1024)S(1)} %broadcast_clamp_fusion), kind=kCustom, calls=%fused_computation.1 | custom fusion | bytes 8392704 | tf_op jit(solution)/shard_map/gather | solution.py:136
  371.1 22.3 %fusion.48 = (bf16[128,1,2048]{2,1,0:T(2,128)(2,1)S(1)}, bf16[128,1,2048]{2,1,0:T(2,128)(2,1)S(1)}, bf16[128,1,2048]{2,1,0:T(2,128)(2,1)S(1)}, bf16[128,1,2048]{...) fusion(bf16[128,8,2048]{2,1,0:T(8,128)(2,1)} %bitcast.130), kind=kLoop, calls=%fused_computation.112 | loop fusion | bytes 8388608 | tf_op jit(solution)/shard_map/slice | solution.py:140
  393.4 5.5 %fusion.21 = bf16[128,2048]{1,0:T(8,128)(2,1)} fusion(f32[128,2048]{1,0:T(8,128)S(1)} %copy-done.3, bf16[128,1,2048]{2,1,0:T(2,128)(2,1)S(1)} %get-tuple-element.415, bf16[128,1,2048]{2,1,0:T(2,128)(2,1)S(1)} %get-tuple-element.409, bf16[128,1,2048]{2,1,0:T(2,128)(2,1)S(1)} %get-tuple-element.410, bf16[128,1,2048]{2,1,0:T(2,128)(2,1)S(1)} %get-tuple-element.411, ...), kind=kLoop, calls=%fused_computation.36 | loop fusion | flops 6553600 | bytes 5771264 | tf_op jit(solution)/shard_map/convert_element_type | solution.py:141
  (51 shorter events, 0.3 us)
Async XLA Ops:
  7.2 237.8 %copy-start = (bf16[1,768,2048]{2,1,0:T(8,128)(2,1)S(1)}, bf16[1,768,2048]{2,1,0:T(8,128)(2,1)}, u32[]{:S(2)}) copy-start(bf16[1,768,2048]{2,1,0:T(8,128)(2,1)} %param.25) | copy-start | bytes 9437188
  7.2 10.3 %copy-start.4 = (bf16[128,256]{1,0:T(8,128)(2,1)S(1)}, bf16[128,256]{1,0:T(8,128)(2,1)}, u32[]{:S(2)}) copy-start(bf16[128,256]{1,0:T(8,128)(2,1)} %param.18) | copy-start | bytes 196612
  7.2 11.9 %copy-start.9 = (s32[16]{0:T(128)S(1)}, s32[16]{0:T(128)}, u32[]{:S(2)}) copy-start(s32[16]{0:T(128)} %param.19) | copy-start | bytes 196
  7.2 84.2 %all-gather.2.cloned.1.call-start = ((), (), s32[]{:S(2)}) async-start(), calls=%async_computation.2 | async-start | bytes 8912896 | tf_op jit(solution)/shard_map/all_gather | solution.py:38
  15.7 3.3 copy-start.5
  19.1 50.3 %copy-start.6 = (s32[128,8]{0,1:T(8,128)S(1)}, s32[128,8]{0,1:T(8,128)}, u32[]{:S(2)}) copy-start(s32[128,8]{0,1:T(8,128)} %param.20) | copy-start | bytes 12292
  19.1 9.8 %collective-permute-start = (bf16[2,128,256]{1,2,0:T(8,128)(2,1)S(1)}, bf16[2,128,256]{1,2,0:T(8,128)(2,1)S(1)}, u32[]{:S(2)}, u32[]{:S(2)}) collective-permute-start(bf16[2,128,256]{1,2,0:T(8,128)(2,1)S(1)} %get-tuple-element.515), channel_id=1, source_target_pairs={{0,4},{1,5},{2,6},{3,7},{4,8},{5,9},{6,10},{7,11},{8,12},{9,13},{1... | collective-permute-start | bytes 393224 | tf_op jit(solution)/shard_map/while/body/eval_jaxpr/ppermute | solution.py:17
  28.9 14.9 %collective-permute-start = (bf16[2,128,256]{1,2,0:T(8,128)(2,1)S(1)}, bf16[2,128,256]{1,2,0:T(8,128)(2,1)S(1)}, u32[]{:S(2)}, u32[]{:S(2)}) collective-permute-start(bf16[2,128,256]{1,2,0:T(8,128)(2,1)S(1)} %get-tuple-element.515), channel_id=1, source_target_pairs={{0,4},{1,5},{2,6},{3,7},{4,8},{5,9},{6,10},{7,11},{8,12},{9,13},{1... | collective-permute-start | bytes 393224 | tf_op jit(solution)/shard_map/while/body/eval_jaxpr/ppermute | solution.py:17
  43.9 17.7 %collective-permute-start = (bf16[2,128,256]{1,2,0:T(8,128)(2,1)S(1)}, bf16[2,128,256]{1,2,0:T(8,128)(2,1)S(1)}, u32[]{:S(2)}, u32[]{:S(2)}) collective-permute-start(bf16[2,128,256]{1,2,0:T(8,128)(2,1)S(1)} %get-tuple-element.515), channel_id=1, source_target_pairs={{0,4},{1,5},{2,6},{3,7},{4,8},{5,9},{6,10},{7,11},{8,12},{9,13},{1... | collective-permute-start | bytes 393224 | tf_op jit(solution)/shard_map/while/body/eval_jaxpr/ppermute | solution.py:17
  91.4 6.0 %copy-start.8 = (f32[2048]{0:T(1024)S(1)}, f32[2048]{0:T(1024)}, u32[]{:S(2)}) copy-start(f32[2048]{0:T(1024)} %param.23) | copy-start | bytes 24580
  96.3 1.0 copy-start.2
  250.7 4.9 %copy-start.7 = (f32[128,8]{0,1:T(8,128)S(1)}, f32[128,8]{0,1:T(8,128)}, u32[]{:S(2)}) copy-start(f32[128,8]{0,1:T(8,128)} %param.21) | copy-start | bytes 12292
  250.7 108.6 %all-to-all-start.1 = ((bf16[16,72,2048]{2,1,0:T(8,128)(2,1)}), bf16[16,72,2048]{2,1,0:T(8,128)(2,1)}, u32[]{:S(2)}, u32[]{:S(2)}) async-start(bf16[16,72,2048]{2,1,0:T(8,128)(2,1)} %bitcast.136), calls=%async_computation.1 | async-start | bytes 9437184 | tf_op jit(solution)/shard_map/all_to_all | solution.py:135
  371.1 22.3 %copy-start.3 = (f32[128,2048]{1,0:T(8,128)S(1)}, f32[128,2048]{1,0:T(8,128)}, u32[]{:S(2)}) copy-start(f32[128,2048]{1,0:T(8,128)} %copy-done.2) | copy-start | bytes 3145732
  393.4 5.5 %copy-start.1 = (bf16[1,768,2048]{2,1,0:T(8,128)(2,1)S(1)}, bf16[1,768,2048]{2,1,0:T(8,128)(2,1)}, u32[]{:S(2)}) copy-start(bf16[1,768,2048]{2,1,0:T(8,128)(2,1)} %param.25) | copy-start | bytes 9437188
Sparse Core Ops, SparseCore 0:
  10.2 81.1 all-gather.1
where the time goes:
time: 407 us; the launch traced here: 406 us
  waiting for transfers between devices  145 us (36%)
  blocking collectives  113 us (28%)
  local copies, waits for them, and re-layouts  68.8 us (17%)
  matrix products  23.3 us (6%)
  starting transfers between devices  23 us (6%)
  between operations  15 us (4%)
  other arithmetic  13.8 us (3%)
  loops' own time  4.07 us (1%)
    all_to_all x1, blocking collectives, local(): lax.all_to_all(outgoing, 'ctx', split_axis=0, concat_axis=0, tiled=True)  113 us
    all_to_all x1, waiting for transfers between devices, local(): lax.all_to_all(result, 'ctx', split_axis=0, concat_axis=0, tiled=True)  104 us
    scatter x1, local copies, waits for them, and re-layouts, local(): outgoing = jnp.zeros((experts * capacity, D), jnp.bfloat16).at[target].se...  23.8 us
    slice x1, local copies, waits for them, and re-layouts, local(): gathered[:, slot].astype(jnp.float32)  22.3 us
    all_gather x1, waiting for transfers between devices, local(): full_weight = lax.all_gather(out_weight, 'ctx', axis=1, tiled=True)  21.6 us
    ppermute x3, waiting for transfers between devices, shifted(): lax.ppermute(array, axis, [(i, (i + by) % devices) for i in range(devices)])  18.6 us
    ppermute x3, starting transfers between devices, shifted(): lax.ppermute(array, axis, [(i, (i + by) % devices) for i in range(devices)])  18 us
    gather x1, local copies, waits for them, and re-layouts, local(): returned.reshape(-1, D)[target].reshape(device_row_count, TOPK, D)  11.8 us
  transfers between devices with their start and end apart: 5, of which 5 were waited for; matrix products, arithmetic and copies ran while one was open for 5% of the time, Pallas kernels for 0%

commit v1 on v0

--- a/solution.py
+++ b/solution.py
@@ -1,7 +1,12 @@
+import functools
+
 import jax
 import jax.numpy as jnp
 from jax import lax
+from jax.experimental import pallas as pl
+from jax.experimental.pallas import tpu as pltpu
 from jax.sharding import PartitionSpec as P
+
 
 D = 2048
 HEAD_SIZE = 128
@@ -10,6 +15,8 @@
 KEY_VALUE_HEADS = 2
 TOPK = 8
 SEQS = 4
+PARTS = 1
+SUM_PARTS = 1
 
 
 def shifted(array, axis, by):
@@ -17,7 +24,7 @@
     return lax.ppermute(array, axis, [(i, (i + by) % devices) for i in range(devices)])
 
 
-def local(
+def exchanged(
     residual,
     queries,
     keys,
@@ -94,8 +101,8 @@
         )
         return (current, moving)
 
-    carry, passed = lax.fori_loop(1, cycle_length, advance, (carry, local_pair))
-    summed, running_max, totals = carry
+    carry, _ = lax.fori_loop(1, cycle_length, advance, (carry, local_pair))
+    summed, _, totals = carry
     context = (
         (summed / totals[..., None])
         .reshape(KEY_VALUE_HEADS, query_group_width, device_row_count, HEAD_SIZE)
@@ -141,6 +148,242 @@
     return (context, mixed.astype(jnp.bfloat16))
 
 
+def ring_order(devices):
+    chips = devices // 2
+    return list(range(0, chips, 2)) + list(range(chips - 1, 0, -2))
+
+
+def ring_tables(devices):
+    order = ring_order(devices)
+    place = {chip: at for at, chip in enumerate(order)}
+    chips = len(order)
+
+    def along(i, by):
+        chip, core = divmod(i, 2)
+        return order[(place[chip] + by) % chips] * 2 + core
+
+    def turned(i, by):
+        return along(i, by if i % 2 == 0 else -by)
+
+    everyone = range(devices)
+    return dict(
+        up=[(i, along(i, 1)) for i in everyone],
+        down=[(i, along(i, -1)) for i in everyone],
+        turned=[(i, turned(i, 1)) for i in everyone],
+        pair=[(i, i ^ 1) for i in everyone],
+        after_up=[[along(i, -s) for s in range(chips)] for i in everyone],
+        after_turned=[[turned(i, -s) for s in range(chips)] for i in everyone],
+    )
+
+
+def attention_kernel(count, table, block_order, q_ref, *refs):
+    key_refs, value_refs, out_ref = refs[:count], refs[count : 2 * count], refs[2 * count]
+    rows = q_ref.shape[0]
+    group = QUERY_HEADS // KEY_VALUE_HEADS
+    row = lax.broadcasted_iota(jnp.int32, (rows, rows), 0)
+    column = lax.broadcasted_iota(jnp.int32, (rows, rows), 1)
+    places = [block_order[table[b]] * rows for b in range(count)]
+    visible = jnp.concatenate([place + column <= places[0] + row for place in places], axis=1)
+    scale = HEAD_SIZE ** (-0.5)
+    for head in range(QUERY_HEADS):
+        of = slice(head // group * HEAD_SIZE, (head // group + 1) * HEAD_SIZE)
+        keys = jnp.concatenate([ref[:, of] for ref in key_refs], axis=0)
+        values = jnp.concatenate([ref[:, of] for ref in value_refs], axis=0)
+        query = q_ref[:, head * HEAD_SIZE : (head + 1) * HEAD_SIZE]
+        scores = (
+            lax.dot_general(
+                query, keys, (((1,), (1,)), ((), ())), preferred_element_type=jnp.float32
+            )
+            * scale
+        )
+        scores = jnp.where(visible, scores, -jnp.inf)
+        weights = jnp.exp(scores - jnp.max(scores, axis=1, keepdims=True))
+        total = jnp.sum(weights, axis=1, keepdims=True)
+        summed = jnp.dot(
+            weights.astype(jnp.bfloat16), values, preferred_element_type=jnp.float32
+        )
+        out_ref[:, head * HEAD_SIZE : (head + 1) * HEAD_SIZE] = (summed / total).astype(
+            jnp.bfloat16
+        )
+
+
+def attention(table, block_order, queries, keys, values):
+    rows, width = queries.shape
+    count = len(keys)
+    return pl.pallas_call(
+        functools.partial(attention_kernel, count),
+        out_shape=jax.ShapeDtypeStruct((rows, width), jnp.bfloat16),
+        in_specs=[pl.BlockSpec(memory_space=pltpu.SMEM)] * 2
+        + [pl.BlockSpec(memory_space=pltpu.VMEM)] * (1 + 2 * count),
+        out_specs=pl.BlockSpec(memory_space=pltpu.VMEM),
+        cost_estimate=pl.CostEstimate(
+            flops=4 * rows * rows * count * width,
+            bytes_accessed=4 * rows * width + 4 * count * keys[0].size,
+            transcendentals=rows * rows * count * QUERY_HEADS,
+        ),
+        name="attention",
+    )(table, block_order, queries, *keys, *values)
+
+
+def partial_kernel(parts, own_ref, other_ref, *refs):
+    mine_ref, theirs_ref = refs[-2:]
+    rows = own_ref.shape[0]
+    out = 0.0
+    done = start = 0
+    for count in parts:
+        blocks = refs[done : done + count]
+        done += count
+        at = slice(start, start + blocks[0].shape[0])
+        start = at.stop
+        context = jnp.concatenate([own_ref[:, at], other_ref[:, at]], axis=0)
+        weight = jnp.concatenate([block[...] for block in blocks], axis=1)
+        out += jnp.dot(context, weight, preferred_element_type=jnp.float32)
+    mine_ref[...] = out[:rows]
+    theirs_ref[...] = out[rows:]
+
+
+def partial_product(own, other, parts):
+    rows, depth = own.shape
+    wide = sum(block.shape[1] for block in parts[0])
+    blocks = [block for part in parts for block in part]
+    return pl.pallas_call(
+        functools.partial(partial_kernel, [len(part) for part in parts]),
+        out_shape=(jax.ShapeDtypeStruct((rows, wide), jnp.float32),) * 2,
+        in_specs=[pl.BlockSpec(memory_space=pltpu.VMEM)] * (2 + len(blocks)),
+        out_specs=(pl.BlockSpec(memory_space=pltpu.VMEM),) * 2,
+        cost_estimate=pl.CostEstimate(
+            flops=4 * rows * depth * wide,
+            bytes_accessed=2 * depth * wide + 4 * rows * depth,
+            transcendentals=0,
+        ),
+        name="partial_product",
+    )(own, other, *blocks)
+
+
+def finish_kernel(wide, parts, skip, table, residual_ref, gain_ref, *refs):
+    piece_refs = refs[: -1 - parts]
+    updated_ref, normed_refs = refs[-1 - parts], refs[-parts:]
+    done = skip
+    for ref in piece_refs:
+        for at in range(0, ref.shape[1], wide):
+            to = pl.ds(pl.multiple_of(table[done] * wide, wide), wide)
+            updated_ref[:, to] = residual_ref[:, to].astype(jnp.float32) + ref[:, at : at + wide]
+            done += 1
+    rows = updated_ref.shape[0] // parts
+    for part, ref in enumerate(normed_refs):
+        updated = updated_ref[part * rows : (part + 1) * rows]
+        mean = jnp.mean(updated * updated, axis=1, keepdims=True)
+        ref[...] = (updated * lax.rsqrt(mean + 1e-06) * gain_ref[...]).astype(jnp.bfloat16)
+
+
+def finish(table, skip, residual, gain, pieces, parts):
+    rows, width = residual.shape
+    return pl.pallas_call(
+        functools.partial(finish_kernel, width // (table.shape[0] - skip), parts, skip),
+        out_shape=(jax.ShapeDtypeStruct((rows, width), jnp.float32),)
+        + (jax.ShapeDtypeStruct((rows // parts, width), jnp.bfloat16),) * parts,
+        in_specs=[pl.BlockSpec(memory_space=pltpu.SMEM)]
+        + [pl.BlockSpec(memory_space=pltpu.VMEM)] * (2 + len(pieces)),
+        out_specs=(pl.BlockSpec(memory_space=pltpu.VMEM),) * (1 + parts),
+        cost_estimate=pl.CostEstimate(
+            flops=6 * rows * width, bytes_accessed=12 * rows * width, transcendentals=rows
+        ),
+        name="finish",
+    )(table, residual, gain.reshape(1, width), *pieces)
+
+
+def ringed(
+    residual,
+    queries,
+    keys,
+    values,
+    block_order,
+    routes,
+    route_weights,
+    out_weight,
+    norm_gain,
+    w_gate_up,
+    w_down,
+):
+    rows = queries.shape[0]
+    devices = lax.axis_size("ctx")
+    own_index = lax.axis_index("ctx")
+    ring = ring_tables(devices)
+    chips = devices // 2
+    half = chips // 2
+    spans = range(devices // SEQS)
+    turns = [0] + [t for s in range(1, half) for t in (s, chips - s)] + [half]
+
+    def sent(array, way):
+        return lax.ppermute(array, "ctx", ring[way])
+
+    table = []
+    for i in range(devices):
+        columns = [ring["after_up"][i][t] for t in turns]
+        table.append([(i - SEQS * s) % devices for s in spans] + columns + [c ^ 1 for c in columns])
+    table = jnp.asarray(table, jnp.int32)[own_index]
+
+    key_blocks = [keys] + [shifted(keys, "ctx", SEQS * s) for s in spans[1:]]
+    value_blocks = [values] + [shifted(values, "ctx", SEQS * s) for s in spans[1:]]
+
+    gates = route_weights / jnp.sum(route_weights, axis=-1, keepdims=True)
+    named = routes[:, :, None] == jnp.arange(devices, dtype=jnp.int32)
+    spread = jnp.sum(jnp.where(named, gates[:, :, None], 0.0), axis=1)
+    arrived = lax.all_to_all(spread.T, "ctx", split_axis=0, concat_axis=0, tiled=True)
+
+    depth = out_weight.shape[0] // 2
+    up = down = whole = (out_weight[:depth], out_weight[depth:])
+    rounds = []
+    for _ in range(1, half):
+        up = tuple(sent(part, "up") for part in up)
+        down = tuple(sent(part, "down") for part in down)
+        rounds.append([up, down])
+    context = attention(table, block_order, queries, key_blocks, value_blocks)
+    rounds.append([(sent(up[0], "up"), sent(down[1], "down"))])
+    other_context = sent(context, "pair")
+    pieces, away = [], []
+    early = [whole] + [block for got in rounds[:-2] for block in got]
+    for got in [early] + rounds[-2:]:
+        mine, theirs = partial_product(context, other_context, list(zip(*got)))
+        pieces.append(mine)
+        away.append(sent(theirs, "pair"))
+    updated, *normed = finish(table, len(spans), residual, norm_gain, pieces + away, PARTS)
+
+    turned = jnp.asarray(ring["after_turned"], jnp.int32)
+    order = jnp.stack([turned[own_index], turned[own_index ^ 1]], axis=1)
+    gate_rows = arrived[order]
+    moving = normed
+    summed = None
+    for step in range(chips):
+        if step > 0:
+            moving = [sent(part, "turned") for part in moving]
+        both = jnp.concatenate([*moving, *[sent(part, "pair") for part in moving]], axis=0)
+        hidden = jnp.dot(both, w_gate_up[0], preferred_element_type=jnp.float32)
+        hidden = (jax.nn.silu(hidden[:, :FF]) * hidden[:, FF:]).astype(jnp.bfloat16)
+        out = jnp.dot(hidden, w_down[0], preferred_element_type=jnp.float32).astype(jnp.bfloat16)
+        gate = gate_rows[step].reshape(2 * rows, 1)
+        out = jnp.where(gate > 0.0, gate * out.astype(jnp.float32), 0.0)
+        theirs = sent(out[rows:].astype(jnp.bfloat16), "pair")
+        total = out[:rows] + theirs.astype(jnp.float32)
+        if step == 0:
+            first = updated + total
+            continue
+        totals = jnp.split(total, SUM_PARTS)
+        if summed is not None:
+            totals = [t + s.astype(jnp.float32) for t, s in zip(totals, summed)]
+        summed = [sent(t.astype(jnp.bfloat16), "turned") for t in totals]
+    mixed = first + jnp.concatenate(summed).astype(jnp.float32)
+    return (context, mixed.astype(jnp.bfloat16))
+
+
+def local(*arrays):
+    devices = lax.axis_size("ctx")
+    held_experts = arrays[9].shape[0]
+    if held_experts == 1 and devices <= 2 * TOPK and devices % (2 * SEQS) == 0:
+        return ringed(*arrays)
+    return exchanged(*arrays)
+
+
 def solution(mesh):
     placed = (
         P(("groups", "ctx"), None),

time: 407 us -> 172 us (0.42)
  the two profiles are of different devices: /device:TPU:15 before, /device:TPU:0 now
where the time goes in v1:
time: 172 us
  waiting for transfers between devices  75.6 us (44%)
  starting transfers between devices  42.6 us (25%)
  matrix products  25.8 us (15%)
  Pallas kernels  17.8 us (10%)
  local copies, waits for them, and re-layouts  5.85 us (3%)
  other arithmetic  3.01 us (2%)
    ppermute x48, waiting for transfers between devices, sent(): return lax.ppermute(array, 'ctx', ring[way])  67.7 us
    ppermute x48, starting transfers between devices, sent(): return lax.ppermute(array, 'ctx', ring[way])  25.3 us
    dot_general x8, matrix products, ringed(): hidden = jnp.dot(both, w_gate_up[0], preferred_element_type=jnp.float32)  17.4 us
    ppermute x6, starting transfers between devices, shifted(): lax.ppermute(array, axis, [(i, (i + by) % devices) for i in range(devices)])  13.6 us
    pallas_call x3, Pallas kernels, partial_product(): pl.pallas_call(functools.partial(partial_kernel, [len(part) for part in p...  8.79 us
    dot_general x8, matrix products, ringed(): jnp.dot(hidden, w_down[0], preferred_element_type=jnp.float32)  8.41 us
    pallas_call x1, Pallas kernels, attention(): pl.pallas_call(functools.partial(attention_kernel, count), out_shape=jax....  6.33 us
    ppermute x6, waiting for transfers between devices, shifted(): lax.ppermute(array, axis, [(i, (i + by) % devices) for i in range(devices)])  5.08 us
  transfers between devices with their start and end apart: 55, of which 21 were waited for; matrix products, arithmetic and copies ran while one was open for 18% of the time, Pallas kernels for 9%

profile of v1, /device:TPU:0, one launch (start us, length us, event | category | flops | bytes accessed | tf_op | source)
XLA Modules:
  0.0 171.8 jit_solution(2150296919994968357)
XLA Ops:
  0.6 1.9 %fusion.211 = (bf16[1024,128]{1,0:T(8,128)(2,1)S(1)}, bf16[1024,128]{1,0:T(8,128)(2,1)}) fusion(bf16[2048,128]{1,0:T(8,128)(2,1)} %param.20), kind=kLoop, calls=%fused_computation.188 | loop fusion | bytes 1048576 | tf_op jit(solution)/shard_map/slice | solution.py:335
  2.6 3.0 %collective-permute-start.12 = (bf16[1024,128]{1,0:T(8,128)(2,1)S(1)}, bf16[1024,128]{1,0:T(8,128)(2,1)}, u32[]{:S(2)}, u32[]{:S(2)}) collective-permute-start(bf16[1024,128]{1,0:T(8,128)(2,1)S(1)} %get-tuple-element.18.refs_5_), channel_id=1, source_target_pairs={{0,2},{1,3},{2,6},{3,7},{4,0},{5,1},{6,10},{7,11},{8,4},{9,5},{10,... | collective-permute-start | bytes 786440 | tf_op jit(solution)/shard_map/ppermute | solution.py:318
  5.6 2.0 %collective-permute-start = (bf16[128,256]{1,0:T(8,128)(2,1)}, bf16[128,256]{1,0:T(8,128)(2,1)S(1)}, u32[]{:S(2)}, u32[]{:S(2)}) collective-permute-start(bf16[128,256]{1,0:T(8,128)(2,1)} %refs_0_.1), channel_id=1, source_target_pairs={{0,4},{1,5},{2,6},{3,7},{4,8},{5,9},{6,10},{7,11},{8,12},{9,13},{1... | collective-permute-start | bytes 196616 | tf_op jit(solution)/shard_map/ppermute | solution.py:24
  7.6 2.6 %collective-permute-start.1 = (bf16[128,256]{1,0:T(8,128)(2,1)}, bf16[128,256]{1,0:T(8,128)(2,1)S(1)}, u32[]{:S(2)}, u32[]{:S(2)}) collective-permute-start(bf16[128,256]{1,0:T(8,128)(2,1)} %refs_0_.1), channel_id=1, source_target_pairs={{0,8},{1,9},{2,10},{3,11},{4,12},{5,13},{6,14},{7,15},{8,0},{9,1},... | collective-permute-start | bytes 196616 | tf_op jit(solution)/shard_map/ppermute | solution.py:24
  11.6 5.1 %collective-permute-done.refs_1_ = bf16[128,256]{1,0:T(8,128)(2,1)S(1)} collective-permute-done((bf16[128,256]{1,0:T(8,128)(2,1)}, bf16[128,256]{1,0:T(8,128)(2,1)S(1)}, u32[]{:S(2)}, u32[]{:S(2)}) %collective-permute-start) | collective-permute-done | bytes 65568 | tf_op jit(solution)/shard_map/ppermute | solution.py:24
  16.7 2.1 %collective-permute-start.3 = (bf16[128,256]{1,0:T(8,128)(2,1)}, bf16[128,256]{1,0:T(8,128)(2,1)S(1)}, u32[]{:S(2)}, u32[]{:S(2)}) collective-permute-start(bf16[128,256]{1,0:T(8,128)(2,1)} %refs_4_.1), channel_id=1, source_target_pairs={{0,4},{1,5},{2,6},{3,7},{4,8},{5,9},{6,10},{7,11},{8,12},{9,13},{1... | collective-permute-start | bytes 196616 | tf_op jit(solution)/shard_map/ppermute | solution.py:24
  18.7 2.7 %collective-permute-start.4 = (bf16[128,256]{1,0:T(8,128)(2,1)}, bf16[128,256]{1,0:T(8,128)(2,1)S(1)}, u32[]{:S(2)}, u32[]{:S(2)}) collective-permute-start(bf16[128,256]{1,0:T(8,128)(2,1)} %refs_4_.1), channel_id=1, source_target_pairs={{0,8},{1,9},{2,10},{3,11},{4,12},{5,13},{6,14},{7,15},{8,0},{9,1},... | collective-permute-start | bytes 196616 | tf_op jit(solution)/shard_map/ppermute | solution.py:24
  21.5 2.8 %collective-permute-start.5 = (bf16[128,256]{1,0:T(8,128)(2,1)}, bf16[128,256]{1,0:T(8,128)(2,1)}, u32[]{:S(2)}, u32[]{:S(2)}) collective-permute-start(bf16[128,256]{1,0:T(8,128)(2,1)} %refs_4_.1), channel_id=1, source_target_pairs={{0,12},{1,13},{2,14},{3,15},{4,0},{5,1},{6,2},{7,3},{8,4},{9,5},{1... | collective-permute-start | bytes 196616 | tf_op jit(solution)/shard_map/ppermute | solution.py:24
  26.3 1.7 %collective-permute-start.11 = (bf16[1024,128]{1,0:T(8,128)(2,1)S(1)}, bf16[1024,128]{1,0:T(8,128)(2,1)}, u32[]{:S(2)}, u32[]{:S(2)}) collective-permute-start(bf16[1024,128]{1,0:T(8,128)(2,1)S(1)} %get-tuple-element.18.refs_5_), channel_id=1, source_target_pairs={{0,4},{1,5},{2,0},{3,1},{4,8},{5,9},{6,2},{7,3},{8,12},{9,13},{10,... | collective-permute-start | bytes 786440 | tf_op jit(solution)/shard_map/ppermute | solution.py:318
  28.4 1.7 collective-permute-start.9
  30.1 6.3 %attention.1.own_ref = bf16[128,2048]{1,0:T(8,128)(2,1)} custom-call(s32[20]{0:T(128)} %fusion.192.table, s32[16]{0:T(128)} %block_order.1, bf16[128,2048]{1,0:T(8,128)(2,1)} %q_ref.1, bf16[128,256]{1,0:T(8,128)(2,1)} %refs_0_.1, bf16[128,256]{1,0:T(8,128)(2,1)} %copy-done.8, bf16[128,256]{1,0:T(8,128)(2,1)} %copy-done.9, ...), custom_call_target="tpu_custom_call" | custom-call | flops 536870912 | bytes 1572864 | tf_op jit(solution)/shard_map/attention/pallas_call | solution.py:213
  36.8 1.7 collective-permute-start.13
  39.1 1.4 collective-permute-start.18
  40.5 5.4 %collective-permute-done.10.refs_4_ = bf16[1024,128]{1,0:T(8,128)(2,1)} collective-permute-done((bf16[1024,128]{1,0:T(8,128)(2,1)}, bf16[1024,128]{1,0:T(8,128)(2,1)}, u32[]{:S(2)}, u32[]{:S(2)}) %collective-permute-start.10) | collective-permute-done | bytes 262176 | tf_op jit(solution)/shard_map/ppermute | solution.py:318
  46.3 1.7 collective-permute-start.17
  48.0 3.9 %collective-permute-done.15.refs_0_ = bf16[1024,128]{1,0:T(8,128)(2,1)} collective-permute-done((bf16[1024,128]{1,0:T(8,128)(2,1)}, bf16[1024,128]{1,0:T(8,128)(2,1)}, u32[]{:S(2)}, u32[]{:S(2)}) %collective-permute-start.15) | collective-permute-done | bytes 262176 | tf_op jit(solution)/shard_map/ppermute | solution.py:318
  51.9 1.7 collective-permute-start.19
  53.9 3.8 %partial_product.3 = (f32[128,640]{1,0:T(8,128)}, f32[128,640]{1,0:T(8,128)}) custom-call(bf16[128,2048]{1,0:T(8,128)(2,1)} %attention.1.own_ref, bf16[128,2048]{1,0:T(8,128)(2,1)} %collective-permute-done.6.other_ref, bf16[1024,128]{1,0:T(8,128)(2,1)} %get-tuple-element.19.refs_0_, bf16[1024,128]{1,0:T(8,128)(2,1)} %collective-permute-done.7.refs_1_, ...), custom_call_target="tpu_custom_call" | custom-call | flops 671088640 | bytes 3670016 | tf_op jit(solution)/shard_map/partial_product/pallas_call | solution.py:249
  57.7 2.6 %partial_product.4 = (f32[128,256]{1,0:T(8,128)}, f32[128,256]{1,0:T(8,128)}) custom-call(bf16[128,2048]{1,0:T(8,128)(2,1)} %attention.1.own_ref, bf16[128,2048]{1,0:T(8,128)(2,1)} %collective-permute-done.6.other_ref, bf16[1024,128]{1,0:T(8,128)(2,1)} %collective-permute-done.15.refs_0_, bf16[1024,128]{1,0:T(8,128)(2,1)} %collective-permute-done.16.refs_1_, ...), custom_call_target="tpu_custom_call" | custom-call | flops 268435456 | bytes 2097152 | tf_op jit(solution)/shard_map/partial_product/pallas_call | solution.py:249
  60.9 1.7 collective-permute-done.19.refs_0_
  62.6 2.4 %partial_product.5 = (f32[128,128]{1,0:T(8,128)}, f32[128,128]{1,0:T(8,128)}) custom-call(bf16[128,2048]{1,0:T(8,128)(2,1)} %attention.1.own_ref, bf16[128,2048]{1,0:T(8,128)(2,1)} %collective-permute-done.6.other_ref, bf16[1024,128]{1,0:T(8,128)(2,1)} %collective-permute-done.19.refs_0_, bf16[1024,128]{1,0:T(8,128)(2,1)} %collective-permute-done.20.refs_1_), custom_call_target="tpu_custom_call" | custom-call | flops 134217728 | bytes 1572864 | tf_op jit(solution)/shard_map/partial_product/pallas_call | solution.py:249
  65.0 1.4 collective-permute-done.23.refs_5_
  67.1 2.7 %finish.1 = (f32[128,2048]{1,0:T(8,128)}, bf16[128,2048]{1,0:T(8,128)(2,1)}) custom-call(s32[20]{0:T(128)} %fusion.192.table, bf16[128,2048]{1,0:T(8,128)(2,1)} %residual_ref.1, f32[1,2048]{1,0:T(1,128)} %bitcast.146, f32[128,640]{1,0:T(8,128)} %get-tuple-element.10.refs_0_, f32[128,256]{1,0:T(8,128)} %get-tuple-element.11.refs_1_, ...), custom_call_target="tpu_custom_call" | custom-call | flops 1572864 | bytes 3145728 | tf_op jit(solution)/shard_map/finish/pallas_call | solution.py:281
  69.8 1.5 collective-permute-start.26
  71.9 3.8 %all-to-all-start = ((f32[16,1,128]{2,1,0:T(1,128)}), f32[16,1,128]{2,1,0:T(1,128)S(1)}, u32[]{:S(2)}, u32[]{:S(2)}) async-start(f32[16,1,128]{2,1,0:T(1,128)} %bitcast.4), calls=%async_computation | async-start | bytes 16384 | tf_op jit(solution)/shard_map/all_to_all | solution.py:332
  76.6 2.7 %collective-permute-done.26 = bf16[128,2048]{1,0:T(8,128)(2,1)} collective-permute-done((bf16[128,2048]{1,0:T(8,128)(2,1)}, bf16[128,2048]{1,0:T(8,128)(2,1)}, u32[]{:S(2)}, u32[]{:S(2)}) %collective-permute-start.26) | collective-permute-done | bytes 524320 | tf_op jit(solution)/shard_map/ppermute | solution.py:318
  79.3 2.8 %all-to-all-done = f32[16,1,128]{2,1,0:T(1,128)S(1)} async-done(((f32[16,1,128]{2,1,0:T(1,128)}), f32[16,1,128]{2,1,0:T(1,128)S(1)}, u32[]{:S(2)}, u32[]{:S(2)}) %all-to-all-start) | async-done | bytes 8224 | tf_op jit(solution)/shard_map/all_to_all | solution.py:332
  83.1 4.9 %fusion = f32[256,1536]{1,0:T(8,128)S(1)} fusion(bf16[1,2048,1536]{2,1,0:T(8,128)(2,1)} %param.22, bf16[128,2048]{1,0:T(8,128)(2,1)} %collective-permute-done.45, bf16[128,2048]{1,0:T(8,128)(2,1)} %collective-permute-done.26), kind=kOutput, calls=%fused_computation.1 | convolution fusion | flops 1612709888 | bytes 8912896 | tf_op jit(solution)/shard_map/dot_general | solution.py:361
  89.2 2.9 %collective-permute-done.27 = bf16[128,2048]{1,0:T(8,128)(2,1)S(1)} collective-permute-done((bf16[128,2048]{1,0:T(8,128)(2,1)}, bf16[128,2048]{1,0:T(8,128)(2,1)S(1)}, u32[]{:S(2)}, u32[]{:S(2)}) %collective-permute-start.27) | collective-permute-done | bytes 524320 | tf_op jit(solution)/shard_map/ppermute | solution.py:318
  94.0 1.8 %fusion.2 = f32[256,1536]{1,0:T(8,128)S(1)} fusion(bf16[1,2048,1536]{2,1,0:T(8,128)(2,1)S(1)} %bitcast.148, bf16[128,2048]{1,0:T(8,128)(2,1)S(1)} %collective-permute-done.43, bf16[128,2048]{1,0:T(8,128)(2,1)S(1)} %collective-permute-done.27), kind=kOutput, calls=%fused_computation.3 | convolution fusion | flops 1612709888 | bytes 8912896 | tf_op jit(solution)/shard_map/dot_general | solution.py:361
  97.1 4.2 %collective-permute-done.28 = bf16[128,2048]{1,0:T(8,128)(2,1)S(1)} collective-permute-done((bf16[128,2048]{1,0:T(8,128)(2,1)S(1)}, bf16[128,2048]{1,0:T(8,128)(2,1)S(1)}, u32[]{:S(2)}, u32[]{:S(2)}) %collective-permute-start.28) | collective-permute-done | bytes 524320 | tf_op jit(solution)/shard_map/ppermute | solution.py:318
  101.7 5.2 %collective-permute-done.47 = bf16[128,2048]{1,0:T(8,128)(2,1)S(1)} collective-permute-done((bf16[128,2048]{1,0:T(8,128)(2,1)S(1)}, bf16[128,2048]{1,0:T(8,128)(2,1)S(1)}, u32[]{:S(2)}, u32[]{:S(2)}) %collective-permute-start.47) | collective-permute-done | bytes 524320 | tf_op jit(solution)/shard_map/ppermute | solution.py:318
  107.5 1.8 %fusion.4 = f32[256,1536]{1,0:T(8,128)S(1)} fusion(bf16[1,2048,1536]{2,1,0:T(8,128)(2,1)S(1)} %bitcast.148, bf16[128,2048]{1,0:T(8,128)(2,1)S(1)} %collective-permute-done.41, bf16[128,2048]{1,0:T(8,128)(2,1)S(1)} %collective-permute-done.28), kind=kOutput, calls=%fused_computation.5 | convolution fusion | flops 1612709888 | bytes 8912896 | tf_op jit(solution)/shard_map/dot_general | solution.py:361
  110.5 2.0 %collective-permute-done.29 = bf16[128,2048]{1,0:T(8,128)(2,1)S(1)} collective-permute-done((bf16[128,2048]{1,0:T(8,128)(2,1)S(1)}, bf16[128,2048]{1,0:T(8,128)(2,1)S(1)}, u32[]{:S(2)}, u32[]{:S(2)}) %collective-permute-start.29) | collective-permute-done | bytes 524320 | tf_op jit(solution)/shard_map/ppermute | solution.py:318
  112.9 5.2 %collective-permute-done.48 = bf16[128,2048]{1,0:T(8,128)(2,1)S(1)} collective-permute-done((bf16[128,2048]{1,0:T(8,128)(2,1)S(1)}, bf16[128,2048]{1,0:T(8,128)(2,1)S(1)}, u32[]{:S(2)}, u32[]{:S(2)}) %collective-permute-start.48) | collective-permute-done | bytes 524320 | tf_op jit(solution)/shard_map/ppermute | solution.py:318
  118.8 1.8 %fusion.6 = f32[256,1536]{1,0:T(8,128)S(1)} fusion(bf16[1,2048,1536]{2,1,0:T(8,128)(2,1)S(1)} %bitcast.148, bf16[128,2048]{1,0:T(8,128)(2,1)S(1)} %collective-permute-done.39, bf16[128,2048]{1,0:T(8,128)(2,1)S(1)} %collective-permute-done.29), kind=kOutput, calls=%fused_computation.7 | convolution fusion | flops 1612709888 | bytes 8912896 | tf_op jit(solution)/shard_map/dot_general | solution.py:361
  121.8 2.0 %collective-permute-done.30 = bf16[128,2048]{1,0:T(8,128)(2,1)S(1)} collective-permute-done((bf16[128,2048]{1,0:T(8,128)(2,1)S(1)}, bf16[128,2048]{1,0:T(8,128)(2,1)S(1)}, u32[]{:S(2)}, u32[]{:S(2)}) %collective-permute-start.30) | collective-permute-done | bytes 524320 | tf_op jit(solution)/shard_map/ppermute | solution.py:318
  124.1 5.2 %collective-permute-done.49 = bf16[128,2048]{1,0:T(8,128)(2,1)S(1)} collective-permute-done((bf16[128,2048]{1,0:T(8,128)(2,1)S(1)}, bf16[128,2048]{1,0:T(8,128)(2,1)S(1)}, u32[]{:S(2)}, u32[]{:S(2)}) %collective-permute-start.49) | collective-permute-done | bytes 524320 | tf_op jit(solution)/shard_map/ppermute | solution.py:318
  130.0 1.8 %fusion.8 = f32[256,1536]{1,0:T(8,128)S(1)} fusion(bf16[1,2048,1536]{2,1,0:T(8,128)(2,1)S(1)} %bitcast.148, bf16[128,2048]{1,0:T(8,128)(2,1)S(1)} %collective-permute-done.37, bf16[128,2048]{1,0:T(8,128)(2,1)S(1)} %collective-permute-done.30), kind=kOutput, calls=%fused_computation.9 | convolution fusion | flops 1612709888 | bytes 8912896 | tf_op jit(solution)/shard_map/dot_general | solution.py:361
  133.0 2.0 %collective-permute-done.31 = bf16[128,2048]{1,0:T(8,128)(2,1)S(1)} collective-permute-done((bf16[128,2048]{1,0:T(8,128)(2,1)S(1)}, bf16[128,2048]{1,0:T(8,128)(2,1)S(1)}, u32[]{:S(2)}, u32[]{:S(2)}) %collective-permute-start.31) | collective-permute-done | bytes 524320 | tf_op jit(solution)/shard_map/ppermute | solution.py:318
  135.4 5.2 %collective-permute-done.50 = bf16[128,2048]{1,0:T(8,128)(2,1)S(1)} collective-permute-done((bf16[128,2048]{1,0:T(8,128)(2,1)S(1)}, bf16[128,2048]{1,0:T(8,128)(2,1)S(1)}, u32[]{:S(2)}, u32[]{:S(2)}) %collective-permute-start.50) | collective-permute-done | bytes 524320 | tf_op jit(solution)/shard_map/ppermute | solution.py:318
  141.5 1.8 %fusion.10 = f32[256,1536]{1,0:T(8,128)S(1)} fusion(bf16[1,2048,1536]{2,1,0:T(8,128)(2,1)S(1)} %bitcast.148, bf16[128,2048]{1,0:T(8,128)(2,1)S(1)} %collective-permute-done.35, bf16[128,2048]{1,0:T(8,128)(2,1)S(1)} %collective-permute-done.31), kind=kOutput, calls=%fused_computation.11 | convolution fusion | flops 1612709888 | bytes 8912896 | tf_op jit(solution)/shard_map/dot_general | solution.py:361
  144.5 1.7 %collective-permute-done.32 = bf16[128,2048]{1,0:T(8,128)(2,1)S(1)} collective-permute-done((bf16[128,2048]{1,0:T(8,128)(2,1)S(1)}, bf16[128,2048]{1,0:T(8,128)(2,1)S(1)}, u32[]{:S(2)}, u32[]{:S(2)}) %collective-permute-start.32) | collective-permute-done | bytes 524320 | tf_op jit(solution)/shard_map/ppermute | solution.py:318
  146.7 5.1 %collective-permute-done.51 = bf16[128,2048]{1,0:T(8,128)(2,1)S(1)} collective-permute-done((bf16[128,2048]{1,0:T(8,128)(2,1)S(1)}, bf16[128,2048]{1,0:T(8,128)(2,1)S(1)}, u32[]{:S(2)}, u32[]{:S(2)}) %collective-permute-start.51) | collective-permute-done | bytes 524320 | tf_op jit(solution)/shard_map/ppermute | solution.py:318
  152.5 1.8 %fusion.12 = f32[256,1536]{1,0:T(8,128)S(1)} fusion(bf16[1,2048,1536]{2,1,0:T(8,128)(2,1)S(1)} %bitcast.148, bf16[128,2048]{1,0:T(8,128)(2,1)S(1)} %collective-permute-done.33, bf16[128,2048]{1,0:T(8,128)(2,1)S(1)} %collective-permute-done.32), kind=kOutput, calls=%fused_computation.13 | convolution fusion | flops 1612709888 | bytes 8912896 | tf_op jit(solution)/shard_map/dot_general | solution.py:361
  155.5 1.8 %fusion.14 = f32[256,1536]{1,0:T(8,128)S(1)} fusion(bf16[1,2048,1536]{2,1,0:T(8,128)(2,1)S(1)} %bitcast.148, bf16[128,2048]{1,0:T(8,128)(2,1)S(1)} %collective-permute-done.24, bf16[128,2048]{1,0:T(8,128)(2,1)S(1)} %copy-done.7), kind=kOutput, calls=%fused_computation.15 | convolution fusion | flops 1612709888 | bytes 8912896 | tf_op jit(solution)/shard_map/dot_general | solution.py:361
  159.0 2.3 %collective-permute-done.52 = bf16[128,2048]{1,0:T(8,128)(2,1)S(1)} collective-permute-done((bf16[128,2048]{1,0:T(8,128)(2,1)S(1)}, bf16[128,2048]{1,0:T(8,128)(2,1)S(1)}, u32[]{:S(2)}, u32[]{:S(2)}) %collective-permute-start.52) | collective-permute-done | bytes 524320 | tf_op jit(solution)/shard_map/ppermute | solution.py:318
  161.9 8.8 %collective-permute-done.53 = bf16[128,2048]{1,0:T(8,128)(2,1)S(1)} collective-permute-done((bf16[128,2048]{1,0:T(8,128)(2,1)S(1)}, bf16[128,2048]{1,0:T(8,128)(2,1)S(1)}, u32[]{:S(2)}, u32[]{:S(2)}) %collective-permute-start.53) | collective-permute-done | bytes 524320 | tf_op jit(solution)/shard_map/ppermute | solution.py:318
  (141 shorter events, 28.2 us)
Async XLA Ops:
  2.6 25.5 %collective-permute-start.12 = (bf16[1024,128]{1,0:T(8,128)(2,1)S(1)}, bf16[1024,128]{1,0:T(8,128)(2,1)}, u32[]{:S(2)}, u32[]{:S(2)}) collective-permute-start(bf16[1024,128]{1,0:T(8,128)(2,1)S(1)} %get-tuple-element.18.refs_5_), channel_id=1, source_target_pairs={{0,2},{1,3},{2,6},{3,7},{4,0},{5,1},{6,10},{7,11},{8,4},{9,5},{10,... | collective-permute-start | bytes 786440 | tf_op jit(solution)/shard_map/ppermute | solution.py:318
  5.6 22.8 %collective-permute-start.7 = (bf16[1024,128]{1,0:T(8,128)(2,1)}, bf16[1024,128]{1,0:T(8,128)(2,1)}, u32[]{:S(2)}, u32[]{:S(2)}) collective-permute-start(bf16[1024,128]{1,0:T(8,128)(2,1)} %get-tuple-element.19.refs_0_), channel_id=1, source_target_pairs={{0,4},{1,5},{2,0},{3,1},{4,8},{5,9},{6,2},{7,3},{8,12},{9,13},{10,... | collective-permute-start | bytes 786440 | tf_op jit(solution)/shard_map/ppermute | solution.py:318
  5.6 11.0 %collective-permute-start = (bf16[128,256]{1,0:T(8,128)(2,1)}, bf16[128,256]{1,0:T(8,128)(2,1)S(1)}, u32[]{:S(2)}, u32[]{:S(2)}) collective-permute-start(bf16[128,256]{1,0:T(8,128)(2,1)} %refs_0_.1), channel_id=1, source_target_pairs={{0,4},{1,5},{2,6},{3,7},{4,8},{5,9},{6,10},{7,11},{8,12},{9,13},{1... | collective-permute-start | bytes 196616 | tf_op jit(solution)/shard_map/ppermute | solution.py:24
  7.6 11.1 %collective-permute-start.1 = (bf16[128,256]{1,0:T(8,128)(2,1)}, bf16[128,256]{1,0:T(8,128)(2,1)S(1)}, u32[]{:S(2)}, u32[]{:S(2)}) collective-permute-start(bf16[128,256]{1,0:T(8,128)(2,1)} %refs_0_.1), channel_id=1, source_target_pairs={{0,8},{1,9},{2,10},{3,11},{4,12},{5,13},{6,14},{7,15},{8,0},{9,1},... | collective-permute-start | bytes 196616 | tf_op jit(solution)/shard_map/ppermute | solution.py:24
  10.2 11.2 %collective-permute-start.2 = (bf16[128,256]{1,0:T(8,128)(2,1)}, bf16[128,256]{1,0:T(8,128)(2,1)}, u32[]{:S(2)}, u32[]{:S(2)}) collective-permute-start(bf16[128,256]{1,0:T(8,128)(2,1)} %refs_0_.1), channel_id=1, source_target_pairs={{0,12},{1,13},{2,14},{3,15},{4,0},{5,1},{6,2},{7,3},{8,4},{9,5},{1... | collective-permute-start | bytes 196616 | tf_op jit(solution)/shard_map/ppermute | solution.py:24
  16.7 8.9 %collective-permute-start.3 = (bf16[128,256]{1,0:T(8,128)(2,1)}, bf16[128,256]{1,0:T(8,128)(2,1)S(1)}, u32[]{:S(2)}, u32[]{:S(2)}) collective-permute-start(bf16[128,256]{1,0:T(8,128)(2,1)} %refs_4_.1), channel_id=1, source_target_pairs={{0,4},{1,5},{2,6},{3,7},{4,8},{5,9},{6,10},{7,11},{8,12},{9,13},{1... | collective-permute-start | bytes 196616 | tf_op jit(solution)/shard_map/ppermute | solution.py:24
  18.7 7.5 %collective-permute-start.4 = (bf16[128,256]{1,0:T(8,128)(2,1)}, bf16[128,256]{1,0:T(8,128)(2,1)S(1)}, u32[]{:S(2)}, u32[]{:S(2)}) collective-permute-start(bf16[128,256]{1,0:T(8,128)(2,1)} %refs_4_.1), channel_id=1, source_target_pairs={{0,8},{1,9},{2,10},{3,11},{4,12},{5,13},{6,14},{7,15},{8,0},{9,1},... | collective-permute-start | bytes 196616 | tf_op jit(solution)/shard_map/ppermute | solution.py:24
  21.5 8.6 %collective-permute-start.5 = (bf16[128,256]{1,0:T(8,128)(2,1)}, bf16[128,256]{1,0:T(8,128)(2,1)}, u32[]{:S(2)}, u32[]{:S(2)}) collective-permute-start(bf16[128,256]{1,0:T(8,128)(2,1)} %refs_4_.1), channel_id=1, source_target_pairs={{0,12},{1,13},{2,14},{3,15},{4,0},{5,1},{6,2},{7,3},{8,4},{9,5},{1... | collective-permute-start | bytes 196616 | tf_op jit(solution)/shard_map/ppermute | solution.py:24
  25.6 10.8 %collective-permute-start.8 = (bf16[1024,128]{1,0:T(8,128)(2,1)}, bf16[1024,128]{1,0:T(8,128)(2,1)}, u32[]{:S(2)}, u32[]{:S(2)}) collective-permute-start(bf16[1024,128]{1,0:T(8,128)(2,1)} %get-tuple-element.19.refs_0_), channel_id=1, source_target_pairs={{0,2},{1,3},{2,6},{3,7},{4,0},{5,1},{6,10},{7,11},{8,4},{9,5},{10,... | collective-permute-start | bytes 786440 | tf_op jit(solution)/shard_map/ppermute | solution.py:318
  26.3 10.5 %collective-permute-start.11 = (bf16[1024,128]{1,0:T(8,128)(2,1)S(1)}, bf16[1024,128]{1,0:T(8,128)(2,1)}, u32[]{:S(2)}, u32[]{:S(2)}) collective-permute-start(bf16[1024,128]{1,0:T(8,128)(2,1)S(1)} %get-tuple-element.18.refs_5_), channel_id=1, source_target_pairs={{0,4},{1,5},{2,0},{3,1},{4,8},{5,9},{6,2},{7,3},{8,12},{9,13},{10,... | collective-permute-start | bytes 786440 | tf_op jit(solution)/shard_map/ppermute | solution.py:318
  28.0 11.1 %collective-permute-start.14 = (bf16[1024,128]{1,0:T(8,128)(2,1)}, bf16[1024,128]{1,0:T(8,128)(2,1)}, u32[]{:S(2)}, u32[]{:S(2)}) collective-permute-start(bf16[1024,128]{1,0:T(8,128)(2,1)} %collective-permute-done.12.refs_7_), channel_id=1, source_target_pairs={{0,2},{1,3},{2,6},{3,7},{4,0},{5,1},{6,10},{7,11},{8,4},{9,5},{10,... | collective-permute-start | bytes 786440 | tf_op jit(solution)/shard_map/ppermute | solution.py:318
  28.4 10.1 %collective-permute-start.9 = (bf16[1024,128]{1,0:T(8,128)(2,1)}, bf16[1024,128]{1,0:T(8,128)(2,1)}, u32[]{:S(2)}, u32[]{:S(2)}) collective-permute-start(bf16[1024,128]{1,0:T(8,128)(2,1)} %collective-permute-done.7.refs_1_), channel_id=1, source_target_pairs={{0,4},{1,5},{2,0},{3,1},{4,8},{5,9},{6,2},{7,3},{8,12},{9,13},{10,... | collective-permute-start | bytes 786440 | tf_op jit(solution)/shard_map/ppermute | solution.py:318
  36.4 17.5 %collective-permute-start.6 = (bf16[128,2048]{1,0:T(8,128)(2,1)}, bf16[128,2048]{1,0:T(8,128)(2,1)}, u32[]{:S(2)}, u32[]{:S(2)}) collective-permute-start(bf16[128,2048]{1,0:T(8,128)(2,1)} %attention.1.own_ref), channel_id=1, source_target_pairs={{0,1},{1,0},{2,3},{3,2},{4,5},{5,4},{6,7},{7,6},{8,9},{9,8},{10,11... | collective-permute-start | bytes 1572872 | tf_op jit(solution)/shard_map/ppermute | solution.py:318
  36.4 9.5 %collective-permute-start.10 = (bf16[1024,128]{1,0:T(8,128)(2,1)}, bf16[1024,128]{1,0:T(8,128)(2,1)}, u32[]{:S(2)}, u32[]{:S(2)}) collective-permute-start(bf16[1024,128]{1,0:T(8,128)(2,1)} %collective-permute-done.8.refs_2_), channel_id=1, source_target_pairs={{0,2},{1,3},{2,6},{3,7},{4,0},{5,1},{6,10},{7,11},{8,4},{9,5},{10,... | collective-permute-start | bytes 786440 | tf_op jit(solution)/shard_map/ppermute | solution.py:318
  36.8 9.5 %collective-permute-start.13 = (bf16[1024,128]{1,0:T(8,128)(2,1)}, bf16[1024,128]{1,0:T(8,128)(2,1)}, u32[]{:S(2)}, u32[]{:S(2)}) collective-permute-start(bf16[1024,128]{1,0:T(8,128)(2,1)} %collective-permute-done.11.refs_6_), channel_id=1, source_target_pairs={{0,4},{1,5},{2,0},{3,1},{4,8},{5,9},{6,2},{7,3},{8,12},{9,13},{10,... | collective-permute-start | bytes 786440 | tf_op jit(solution)/shard_map/ppermute | solution.py:318
  38.5 13.4 %collective-permute-start.15 = (bf16[1024,128]{1,0:T(8,128)(2,1)}, bf16[1024,128]{1,0:T(8,128)(2,1)}, u32[]{:S(2)}, u32[]{:S(2)}) collective-permute-start(bf16[1024,128]{1,0:T(8,128)(2,1)} %collective-permute-done.9.refs_3_), channel_id=1, source_target_pairs={{0,4},{1,5},{2,0},{3,1},{4,8},{5,9},{6,2},{7,3},{8,12},{9,13},{10,... | collective-permute-start | bytes 786440 | tf_op jit(solution)/shard_map/ppermute | solution.py:318
  39.1 14.5 %collective-permute-start.18 = (bf16[1024,128]{1,0:T(8,128)(2,1)}, bf16[1024,128]{1,0:T(8,128)(2,1)}, u32[]{:S(2)}, u32[]{:S(2)}) collective-permute-start(bf16[1024,128]{1,0:T(8,128)(2,1)} %collective-permute-done.14.refs_9_), channel_id=1, source_target_pairs={{0,2},{1,3},{2,6},{3,7},{4,0},{5,1},{6,10},{7,11},{8,4},{9,5},{10,... | collective-permute-start | bytes 786440 | tf_op jit(solution)/shard_map/ppermute | solution.py:318
  46.0 11.8 %collective-permute-start.16 = (bf16[1024,128]{1,0:T(8,128)(2,1)}, bf16[1024,128]{1,0:T(8,128)(2,1)}, u32[]{:S(2)}, u32[]{:S(2)}) collective-permute-start(bf16[1024,128]{1,0:T(8,128)(2,1)} %collective-permute-done.10.refs_4_), channel_id=1, source_target_pairs={{0,2},{1,3},{2,6},{3,7},{4,0},{5,1},{6,10},{7,11},{8,4},{9,5},{10,... | collective-permute-start | bytes 786440 | tf_op jit(solution)/shard_map/ppermute | solution.py:318
  46.3 11.4 %collective-permute-start.17 = (bf16[1024,128]{1,0:T(8,128)(2,1)}, bf16[1024,128]{1,0:T(8,128)(2,1)}, u32[]{:S(2)}, u32[]{:S(2)}) collective-permute-start(bf16[1024,128]{1,0:T(8,128)(2,1)} %collective-permute-done.13.refs_8_), channel_id=1, source_target_pairs={{0,4},{1,5},{2,0},{3,1},{4,8},{5,9},{6,2},{7,3},{8,12},{9,13},{10,... | collective-permute-start | bytes 786440 | tf_op jit(solution)/shard_map/ppermute | solution.py:318
  51.9 10.7 %collective-permute-start.19 = (bf16[1024,128]{1,0:T(8,128)(2,1)}, bf16[1024,128]{1,0:T(8,128)(2,1)}, u32[]{:S(2)}, u32[]{:S(2)}) collective-permute-start(bf16[1024,128]{1,0:T(8,128)(2,1)} %collective-permute-done.15.refs_0_), channel_id=1, source_target_pairs={{0,4},{1,5},{2,0},{3,1},{4,8},{5,9},{6,2},{7,3},{8,12},{9,13},{10,... | collective-permute-start | bytes 786440 | tf_op jit(solution)/shard_map/ppermute | solution.py:318
  53.6 9.0 %collective-permute-start.20 = (bf16[1024,128]{1,0:T(8,128)(2,1)}, bf16[1024,128]{1,0:T(8,128)(2,1)}, u32[]{:S(2)}, u32[]{:S(2)}) collective-permute-start(bf16[1024,128]{1,0:T(8,128)(2,1)} %collective-permute-done.18.refs_3_), channel_id=1, source_target_pairs={{0,2},{1,3},{2,6},{3,7},{4,0},{5,1},{6,10},{7,11},{8,4},{9,5},{10,... | collective-permute-start | bytes 786440 | tf_op jit(solution)/shard_map/ppermute | solution.py:318
  57.7 7.3 %collective-permute-start.21 = (f32[128,640]{1,0:T(8,128)}, f32[128,640]{1,0:T(8,128)S(1)}, u32[]{:S(2)}, u32[]{:S(2)}) collective-permute-start(f32[128,640]{1,0:T(8,128)} %get-tuple-element.13), channel_id=1, source_target_pairs={{0,1},{1,0},{2,3},{3,2},{4,5},{5,4},{6,7},{7,6},{8,9},{9,8},{10,11... | collective-permute-start | bytes 983048 | tf_op jit(solution)/shard_map/ppermute | solution.py:318
  69.8 9.5 %collective-permute-start.26 = (bf16[128,2048]{1,0:T(8,128)(2,1)}, bf16[128,2048]{1,0:T(8,128)(2,1)}, u32[]{:S(2)}, u32[]{:S(2)}) collective-permute-start(bf16[128,2048]{1,0:T(8,128)(2,1)} %get-tuple-element.17), channel_id=1, source_target_pairs={{0,4},{1,3},{2,0},{3,7},{4,8},{5,1},{6,2},{7,11},{8,12},{9,5},{10,... | collective-permute-start | bytes 1572872 | tf_op jit(solution)/shard_map/ppermute | solution.py:318
  71.9 10.2 %all-to-all-start = ((f32[16,1,128]{2,1,0:T(1,128)}), f32[16,1,128]{2,1,0:T(1,128)S(1)}, u32[]{:S(2)}, u32[]{:S(2)}) async-start(f32[16,1,128]{2,1,0:T(1,128)} %bitcast.4), calls=%async_computation | async-start | bytes 16384 | tf_op jit(solution)/shard_map/all_to_all | solution.py:332
  82.7 9.4 %collective-permute-start.27 = (bf16[128,2048]{1,0:T(8,128)(2,1)}, bf16[128,2048]{1,0:T(8,128)(2,1)S(1)}, u32[]{:S(2)}, u32[]{:S(2)}) collective-permute-start(bf16[128,2048]{1,0:T(8,128)(2,1)} %collective-permute-done.26), channel_id=1, source_target_pairs={{0,4},{1,3},{2,0},{3,7},{4,8},{5,1},{6,2},{7,11},{8,12},{9,5},{10,... | collective-permute-start | bytes 1572872 | tf_op jit(solution)/shard_map/ppermute | solution.py:318
  92.1 9.2 %collective-permute-start.28 = (bf16[128,2048]{1,0:T(8,128)(2,1)S(1)}, bf16[128,2048]{1,0:T(8,128)(2,1)S(1)}, u32[]{:S(2)}, u32[]{:S(2)}) collective-permute-start(bf16[128,2048]{1,0:T(8,128)(2,1)S(1)} %collective-permute-done.27), channel_id=1, source_target_pairs={{0,4},{1,3},{2,0},{3,7},{4,8},{5,1},{6,2},{7,11},{8,12},{9,5},{10,... | collective-permute-start | bytes 1572872 | tf_op jit(solution)/shard_map/ppermute | solution.py:318
  92.6 14.3 %collective-permute-start.47 = (bf16[128,2048]{1,0:T(8,128)(2,1)S(1)}, bf16[128,2048]{1,0:T(8,128)(2,1)S(1)}, u32[]{:S(2)}, u32[]{:S(2)}) collective-permute-start(bf16[128,2048]{1,0:T(8,128)(2,1)S(1)} %fusion.128), channel_id=1, source_target_pairs={{0,4},{1,3},{2,0},{3,7},{4,8},{5,1},{6,2},{7,11},{8,12},{9,5},{10,... | collective-permute-start | bytes 1572872 | tf_op jit(solution)/shard_map/ppermute | solution.py:318
  96.9 10.0 %collective-permute-start.44 = (bf16[128,2048]{1,0:T(8,128)(2,1)S(1)}, bf16[128,2048]{1,0:T(8,128)(2,1)S(1)}, u32[]{:S(2)}, u32[]{:S(2)}) collective-permute-start(bf16[128,2048]{1,0:T(8,128)(2,1)S(1)} %slice.347), channel_id=1, source_target_pairs={{0,1},{1,0},{2,3},{3,2},{4,5},{5,4},{6,7},{7,6},{8,9},{9,8},{10,11... | collective-permute-start | bytes 1572872 | tf_op jit(solution)/shard_map/ppermute | solution.py:318
  101.3 6.3 %collective-permute-start.41 = (bf16[128,2048]{1,0:T(8,128)(2,1)S(1)}, bf16[128,2048]{1,0:T(8,128)(2,1)S(1)}, u32[]{:S(2)}, u32[]{:S(2)}) collective-permute-start(bf16[128,2048]{1,0:T(8,128)(2,1)S(1)} %collective-permute-done.28), channel_id=1, source_target_pairs={{0,1},{1,0},{2,3},{3,2},{4,5},{5,4},{6,7},{7,6},{8,9},{9,8},{10,11... | collective-permute-start | bytes 1572872 | tf_op jit(solution)/shard_map/ppermute | solution.py:318
  101.3 11.2 %collective-permute-start.29 = (bf16[128,2048]{1,0:T(8,128)(2,1)S(1)}, bf16[128,2048]{1,0:T(8,128)(2,1)S(1)}, u32[]{:S(2)}, u32[]{:S(2)}) collective-permute-start(bf16[128,2048]{1,0:T(8,128)(2,1)S(1)} %collective-permute-done.28), channel_id=1, source_target_pairs={{0,4},{1,3},{2,0},{3,7},{4,8},{5,1},{6,2},{7,11},{8,12},{9,5},{10,... | collective-permute-start | bytes 1572872 | tf_op jit(solution)/shard_map/ppermute | solution.py:318
  107.1 11.0 %collective-permute-start.48 = (bf16[128,2048]{1,0:T(8,128)(2,1)S(1)}, bf16[128,2048]{1,0:T(8,128)(2,1)S(1)}, u32[]{:S(2)}, u32[]{:S(2)}) collective-permute-start(bf16[128,2048]{1,0:T(8,128)(2,1)S(1)} %fusion.130), channel_id=1, source_target_pairs={{0,4},{1,3},{2,0},{3,7},{4,8},{5,1},{6,2},{7,11},{8,12},{9,5},{10,... | collective-permute-start | bytes 1572872 | tf_op jit(solution)/shard_map/ppermute | solution.py:318
  110.4 7.7 %collective-permute-start.42 = (bf16[128,2048]{1,0:T(8,128)(2,1)S(1)}, bf16[128,2048]{1,0:T(8,128)(2,1)S(1)}, u32[]{:S(2)}, u32[]{:S(2)}) collective-permute-start(bf16[128,2048]{1,0:T(8,128)(2,1)S(1)} %slice.348), channel_id=1, source_target_pairs={{0,1},{1,0},{2,3},{3,2},{4,5},{5,4},{6,7},{7,6},{8,9},{9,8},{10,11... | collective-permute-start | bytes 1572872 | tf_op jit(solution)/shard_map/ppermute | solution.py:318
  112.5 6.3 %collective-permute-start.39 = (bf16[128,2048]{1,0:T(8,128)(2,1)S(1)}, bf16[128,2048]{1,0:T(8,128)(2,1)S(1)}, u32[]{:S(2)}, u32[]{:S(2)}) collective-permute-start(bf16[128,2048]{1,0:T(8,128)(2,1)S(1)} %collective-permute-done.29), channel_id=1, source_target_pairs={{0,1},{1,0},{2,3},{3,2},{4,5},{5,4},{6,7},{7,6},{8,9},{9,8},{10,11... | collective-permute-start | bytes 1572872 | tf_op jit(solution)/shard_map/ppermute | solution.py:318
  112.5 11.2 %collective-permute-start.30 = (bf16[128,2048]{1,0:T(8,128)(2,1)S(1)}, bf16[128,2048]{1,0:T(8,128)(2,1)S(1)}, u32[]{:S(2)}, u32[]{:S(2)}) collective-permute-start(bf16[128,2048]{1,0:T(8,128)(2,1)S(1)} %collective-permute-done.29), channel_id=1, source_target_pairs={{0,4},{1,3},{2,0},{3,7},{4,8},{5,1},{6,2},{7,11},{8,12},{9,5},{10,... | collective-permute-start | bytes 1572872 | tf_op jit(solution)/shard_map/ppermute | solution.py:318
  118.3 11.0 %collective-permute-start.49 = (bf16[128,2048]{1,0:T(8,128)(2,1)S(1)}, bf16[128,2048]{1,0:T(8,128)(2,1)S(1)}, u32[]{:S(2)}, u32[]{:S(2)}) collective-permute-start(bf16[128,2048]{1,0:T(8,128)(2,1)S(1)} %fusion.132), channel_id=1, source_target_pairs={{0,4},{1,3},{2,0},{3,7},{4,8},{5,1},{6,2},{7,11},{8,12},{9,5},{10,... | collective-permute-start | bytes 1572872 | tf_op jit(solution)/shard_map/ppermute | solution.py:318
  121.7 7.7 %collective-permute-start.40 = (bf16[128,2048]{1,0:T(8,128)(2,1)S(1)}, bf16[128,2048]{1,0:T(8,128)(2,1)S(1)}, u32[]{:S(2)}, u32[]{:S(2)}) collective-permute-start(bf16[128,2048]{1,0:T(8,128)(2,1)S(1)} %slice.349), channel_id=1, source_target_pairs={{0,1},{1,0},{2,3},{3,2},{4,5},{5,4},{6,7},{7,6},{8,9},{9,8},{10,11... | collective-permute-start | bytes 1572872 | tf_op jit(solution)/shard_map/ppermute | solution.py:318
  123.8 6.3 %collective-permute-start.37 = (bf16[128,2048]{1,0:T(8,128)(2,1)S(1)}, bf16[128,2048]{1,0:T(8,128)(2,1)S(1)}, u32[]{:S(2)}, u32[]{:S(2)}) collective-permute-start(bf16[128,2048]{1,0:T(8,128)(2,1)S(1)} %collective-permute-done.30), channel_id=1, source_target_pairs={{0,1},{1,0},{2,3},{3,2},{4,5},{5,4},{6,7},{7,6},{8,9},{9,8},{10,11... | collective-permute-start | bytes 1572872 | tf_op jit(solution)/shard_map/ppermute | solution.py:318
  123.8 11.2 %collective-permute-start.31 = (bf16[128,2048]{1,0:T(8,128)(2,1)S(1)}, bf16[128,2048]{1,0:T(8,128)(2,1)S(1)}, u32[]{:S(2)}, u32[]{:S(2)}) collective-permute-start(bf16[128,2048]{1,0:T(8,128)(2,1)S(1)} %collective-permute-done.30), channel_id=1, source_target_pairs={{0,4},{1,3},{2,0},{3,7},{4,8},{5,1},{6,2},{7,11},{8,12},{9,5},{10,... | collective-permute-start | bytes 1572872 | tf_op jit(solution)/shard_map/ppermute | solution.py:318
  129.6 11.0 %collective-permute-start.50 = (bf16[128,2048]{1,0:T(8,128)(2,1)S(1)}, bf16[128,2048]{1,0:T(8,128)(2,1)S(1)}, u32[]{:S(2)}, u32[]{:S(2)}) collective-permute-start(bf16[128,2048]{1,0:T(8,128)(2,1)S(1)} %fusion.134), channel_id=1, source_target_pairs={{0,4},{1,3},{2,0},{3,7},{4,8},{5,1},{6,2},{7,11},{8,12},{9,5},{10,... | collective-permute-start | bytes 1572872 | tf_op jit(solution)/shard_map/ppermute | solution.py:318
  132.9 7.7 %collective-permute-start.38 = (bf16[128,2048]{1,0:T(8,128)(2,1)S(1)}, bf16[128,2048]{1,0:T(8,128)(2,1)S(1)}, u32[]{:S(2)}, u32[]{:S(2)}) collective-permute-start(bf16[128,2048]{1,0:T(8,128)(2,1)S(1)} %slice.350), channel_id=1, source_target_pairs={{0,1},{1,0},{2,3},{3,2},{4,5},{5,4},{6,7},{7,6},{8,9},{9,8},{10,11... | collective-permute-start | bytes 1572872 | tf_op jit(solution)/shard_map/ppermute | solution.py:318
  135.0 6.5 %collective-permute-start.35 = (bf16[128,2048]{1,0:T(8,128)(2,1)S(1)}, bf16[128,2048]{1,0:T(8,128)(2,1)S(1)}, u32[]{:S(2)}, u32[]{:S(2)}) collective-permute-start(bf16[128,2048]{1,0:T(8,128)(2,1)S(1)} %collective-permute-done.31), channel_id=1, source_target_pairs={{0,1},{1,0},{2,3},{3,2},{4,5},{5,4},{6,7},{7,6},{8,9},{9,8},{10,11... | collective-permute-start | bytes 1572872 | tf_op jit(solution)/shard_map/ppermute | solution.py:318
  135.0 11.2 %collective-permute-start.32 = (bf16[128,2048]{1,0:T(8,128)(2,1)S(1)}, bf16[128,2048]{1,0:T(8,128)(2,1)S(1)}, u32[]{:S(2)}, u32[]{:S(2)}) collective-permute-start(bf16[128,2048]{1,0:T(8,128)(2,1)S(1)} %collective-permute-done.31), channel_id=1, source_target_pairs={{0,4},{1,3},{2,0},{3,7},{4,8},{5,1},{6,2},{7,11},{8,12},{9,5},{10,... | collective-permute-start | bytes 1572872 | tf_op jit(solution)/shard_map/ppermute | solution.py:318
  140.8 11.0 %collective-permute-start.51 = (bf16[128,2048]{1,0:T(8,128)(2,1)S(1)}, bf16[128,2048]{1,0:T(8,128)(2,1)S(1)}, u32[]{:S(2)}, u32[]{:S(2)}) collective-permute-start(bf16[128,2048]{1,0:T(8,128)(2,1)S(1)} %fusion.136), channel_id=1, source_target_pairs={{0,4},{1,3},{2,0},{3,7},{4,8},{5,1},{6,2},{7,11},{8,12},{9,5},{10,... | collective-permute-start | bytes 1572872 | tf_op jit(solution)/shard_map/ppermute | solution.py:318
  144.4 7.4 %collective-permute-start.36 = (bf16[128,2048]{1,0:T(8,128)(2,1)S(1)}, bf16[128,2048]{1,0:T(8,128)(2,1)S(1)}, u32[]{:S(2)}, u32[]{:S(2)}) collective-permute-start(bf16[128,2048]{1,0:T(8,128)(2,1)S(1)} %slice.351), channel_id=1, source_target_pairs={{0,1},{1,0},{2,3},{3,2},{4,5},{5,4},{6,7},{7,6},{8,9},{9,8},{10,11... | collective-permute-start | bytes 1572872 | tf_op jit(solution)/shard_map/ppermute | solution.py:318
  146.2 6.3 %collective-permute-start.33 = (bf16[128,2048]{1,0:T(8,128)(2,1)S(1)}, bf16[128,2048]{1,0:T(8,128)(2,1)S(1)}, u32[]{:S(2)}, u32[]{:S(2)}) collective-permute-start(bf16[128,2048]{1,0:T(8,128)(2,1)S(1)} %collective-permute-done.32), channel_id=1, source_target_pairs={{0,1},{1,0},{2,3},{3,2},{4,5},{5,4},{6,7},{7,6},{8,9},{9,8},{10,11... | collective-permute-start | bytes 1572872 | tf_op jit(solution)/shard_map/ppermute | solution.py:318
  146.2 9.3 %collective-permute-start.24 = (bf16[128,2048]{1,0:T(8,128)(2,1)S(1)}, bf16[128,2048]{1,0:T(8,128)(2,1)S(1)}, u32[]{:S(2)}, u32[]{:S(2)}) collective-permute-start(bf16[128,2048]{1,0:T(8,128)(2,1)S(1)} %copy-done.7), channel_id=1, source_target_pairs={{0,1},{1,0},{2,3},{3,2},{4,5},{5,4},{6,7},{7,6},{8,9},{9,8},{10,11... | collective-permute-start | bytes 1572872 | tf_op jit(solution)/shard_map/ppermute | solution.py:318
  152.1 9.2 %collective-permute-start.52 = (bf16[128,2048]{1,0:T(8,128)(2,1)S(1)}, bf16[128,2048]{1,0:T(8,128)(2,1)S(1)}, u32[]{:S(2)}, u32[]{:S(2)}) collective-permute-start(bf16[128,2048]{1,0:T(8,128)(2,1)S(1)} %fusion.138), channel_id=1, source_target_pairs={{0,4},{1,3},{2,0},{3,7},{4,8},{5,1},{6,2},{7,11},{8,12},{9,5},{10,... | collective-permute-start | bytes 1572872 | tf_op jit(solution)/shard_map/ppermute | solution.py:318
  161.5 9.2 %collective-permute-start.53 = (bf16[128,2048]{1,0:T(8,128)(2,1)S(1)}, bf16[128,2048]{1,0:T(8,128)(2,1)S(1)}, u32[]{:S(2)}, u32[]{:S(2)}) collective-permute-start(bf16[128,2048]{1,0:T(8,128)(2,1)S(1)} %fusion.140), channel_id=1, source_target_pairs={{0,4},{1,3},{2,0},{3,7},{4,8},{5,1},{6,2},{7,11},{8,12},{9,5},{10,... | collective-permute-start | bytes 1572872 | tf_op jit(solution)/shard_map/ppermute | solution.py:318
  (21 other events, 240.1 us)

commit v2 on v1

--- a/solution.py
+++ b/solution.py
@@ -16,7 +16,7 @@
 TOPK = 8
 SEQS = 4
 PARTS = 1
-SUM_PARTS = 1
+TAIL = 3
 
 
 def shifted(array, axis, by):
@@ -172,7 +172,6 @@
         turned=[(i, turned(i, 1)) for i in everyone],
         pair=[(i, i ^ 1) for i in everyone],
         after_up=[[along(i, -s) for s in range(chips)] for i in everyone],
-        after_turned=[[turned(i, -s) for s in range(chips)] for i in everyone],
     )
 
 
@@ -260,7 +259,7 @@
     )(own, other, *blocks)
 
 
-def finish_kernel(wide, parts, skip, table, residual_ref, gain_ref, *refs):
+def finish_kernel(wide, parts, skip, table, residual_ref, gain_ref, tags_ref, *refs):
     piece_refs = refs[: -1 - parts]
     updated_ref, normed_refs = refs[-1 - parts], refs[-parts:]
     done = skip
@@ -273,23 +272,26 @@
     for part, ref in enumerate(normed_refs):
         updated = updated_ref[part * rows : (part + 1) * rows]
         mean = jnp.mean(updated * updated, axis=1, keepdims=True)
-        ref[...] = (updated * lax.rsqrt(mean + 1e-06) * gain_ref[...]).astype(jnp.bfloat16)
-
-
-def finish(table, skip, residual, gain, pieces, parts):
+        width = updated.shape[1]
+        ref[:, :width] = (updated * lax.rsqrt(mean + 1e-06) * gain_ref[...]).astype(jnp.bfloat16)
+        ref[:, width:] = tags_ref[part * rows : (part + 1) * rows]
+
+
+def finish(table, skip, residual, gain, tags, pieces, parts):
     rows, width = residual.shape
+    tagged = width + tags.shape[1]
     return pl.pallas_call(
         functools.partial(finish_kernel, width // (table.shape[0] - skip), parts, skip),
         out_shape=(jax.ShapeDtypeStruct((rows, width), jnp.float32),)
-        + (jax.ShapeDtypeStruct((rows // parts, width), jnp.bfloat16),) * parts,
+        + (jax.ShapeDtypeStruct((rows // parts, tagged), jnp.bfloat16),) * parts,
         in_specs=[pl.BlockSpec(memory_space=pltpu.SMEM)]
-        + [pl.BlockSpec(memory_space=pltpu.VMEM)] * (2 + len(pieces)),
+        + [pl.BlockSpec(memory_space=pltpu.VMEM)] * (3 + len(pieces)),
         out_specs=(pl.BlockSpec(memory_space=pltpu.VMEM),) * (1 + parts),
         cost_estimate=pl.CostEstimate(
             flops=6 * rows * width, bytes_accessed=12 * rows * width, transcendentals=rows
         ),
         name="finish",
-    )(table, residual, gain.reshape(1, width), *pieces)
+    )(table, residual, gain.reshape(1, width), tags, *pieces)
 
 
 def ringed(
@@ -328,8 +330,13 @@
 
     gates = route_weights / jnp.sum(route_weights, axis=-1, keepdims=True)
     named = routes[:, :, None] == jnp.arange(devices, dtype=jnp.int32)
-    spread = jnp.sum(jnp.where(named, gates[:, :, None], 0.0), axis=1)
-    arrived = lax.all_to_all(spread.T, "ctx", split_axis=0, concat_axis=0, tiled=True)
+    left = jnp.sum(jnp.where(named, gates[:, :, None], 0.0), axis=1)
+    addends = []
+    for _ in range(3):
+        addends.append(lax.reduce_precision(left, 8, 7))
+        left = left - addends[-1]
+    tags = jnp.concatenate(addends, axis=1).astype(jnp.bfloat16)
+    tags = jnp.pad(tags, ((0, 0), (0, -tags.shape[1] % 128)))
 
     depth = out_weight.shape[0] // 2
     up = down = whole = (out_weight[:depth], out_weight[depth:])
@@ -347,29 +354,33 @@
         mine, theirs = partial_product(context, other_context, list(zip(*got)))
         pieces.append(mine)
         away.append(sent(theirs, "pair"))
-    updated, *normed = finish(table, len(spans), residual, norm_gain, pieces + away, PARTS)
-
-    turned = jnp.asarray(ring["after_turned"], jnp.int32)
-    order = jnp.stack([turned[own_index], turned[own_index ^ 1]], axis=1)
-    gate_rows = arrived[order]
+    updated, *normed = finish(table, len(spans), residual, norm_gain, tags, pieces + away, PARTS)
+
+    lane = jnp.arange(tags.shape[1])
+    own_lane = (lane % devices == own_index) & (lane < 3 * devices)
+    picks = jnp.broadcast_to(own_lane[:, None], (lane.shape[0], 128)).astype(jnp.bfloat16)
     moving = normed
     summed = None
     for step in range(chips):
         if step > 0:
             moving = [sent(part, "turned") for part in moving]
         both = jnp.concatenate([*moving, *[sent(part, "pair") for part in moving]], axis=0)
-        hidden = jnp.dot(both, w_gate_up[0], preferred_element_type=jnp.float32)
+        width = both.shape[1] - lane.shape[0]
+        hidden = jnp.dot(both[:, :width], w_gate_up[0], preferred_element_type=jnp.float32)
         hidden = (jax.nn.silu(hidden[:, :FF]) * hidden[:, FF:]).astype(jnp.bfloat16)
         out = jnp.dot(hidden, w_down[0], preferred_element_type=jnp.float32).astype(jnp.bfloat16)
-        gate = gate_rows[step].reshape(2 * rows, 1)
+        gate = jnp.dot(both[:, width:], picks, preferred_element_type=jnp.float32)[:, :1]
         out = jnp.where(gate > 0.0, gate * out.astype(jnp.float32), 0.0)
         theirs = sent(out[rows:].astype(jnp.bfloat16), "pair")
         total = out[:rows] + theirs.astype(jnp.float32)
         if step == 0:
             first = updated + total
             continue
-        totals = jnp.split(total, SUM_PARTS)
+        cuts = [] if step < chips - TAIL else [5 * rows // 8]
+        totals = jnp.split(total, cuts)
         if summed is not None:
+            if len(summed) < len(totals):
+                summed = jnp.split(summed[0], cuts)
             totals = [t + s.astype(jnp.float32) for t, s in zip(totals, summed)]
         summed = [sent(t.astype(jnp.bfloat16), "turned") for t in totals]
     mixed = first + jnp.concatenate(summed).astype(jnp.float32)

time: 172 us -> 176 us (1.023)
  starting transfers between devices: 42.6 us -> 45.4 us
    ppermute x6, waiting for transfers between devices: 5.08 us -> 21.3 us  [shifted(): lax.ppermute(array, axis, [(i, (i + by) % devices) for i in range(devices)])]
    ppermute x48 -> x51, waiting for transfers between devices: 67.7 us -> 53.7 us  [sent(): return lax.ppermute(array, 'ctx', ring[way])]
    ppermute x48 -> x51, starting transfers between devices: 25.3 us -> 36.1 us  [sent(): return lax.ppermute(array, 'ctx', ring[way])]
    ppermute x6, starting transfers between devices: 13.6 us -> 9.26 us  [shifted(): lax.ppermute(array, axis, [(i, (i + by) % devices) for i in range(devices)])]
    all_to_all x1 -> x0, starting transfers between devices: 3.76 us -> none  [ringed(): lax.all_to_all(spread.T, 'ctx', split_axis=0, concat_axis=0, tiled=True)]
    all_to_all x1 -> x0, waiting for transfers between devices: 2.76 us -> none  [ringed(): lax.all_to_all(spread.T, 'ctx', split_axis=0, concat_axis=0, tiled=True)]
    dot_general x8 -> x16, matrix products: 17.4 us -> 18.8 us  [the longest x8 17.2 us: ringed(): jnp.dot(both[:, :width], w_gate_up[0], preferred_element_type=jnp.float32)]
  transfers between devices with their start and end apart: 55 -> 57, of which waited for: 21 -> 20; matrix products, arithmetic and copies ran while one was open for 18% -> 20% of each run, Pallas kernels for 9% -> 9%
where the time goes in v2:
time: 176 us; the launch traced here: 175 us
  waiting for transfers between devices  75 us (43%)
  starting transfers between devices  45.4 us (26%)
  matrix products  27.3 us (16%)
  Pallas kernels  17.9 us (10%)
  local copies, waits for them, and re-layouts  6.15 us (3%)
  other arithmetic  2.51 us (1%)
    ppermute x51, waiting for transfers between devices, sent(): return lax.ppermute(array, 'ctx', ring[way])  53.7 us
    ppermute x51, starting transfers between devices, sent(): return lax.ppermute(array, 'ctx', ring[way])  36.1 us
    ppermute x6, waiting for transfers between devices, shifted(): lax.ppermute(array, axis, [(i, (i + by) % devices) for i in range(devices)])  21.3 us
    dot_general x8, matrix products, ringed(): jnp.dot(both[:, :width], w_gate_up[0], preferred_element_type=jnp.float32)  17.2 us
    ppermute x6, starting transfers between devices, shifted(): lax.ppermute(array, axis, [(i, (i + by) % devices) for i in range(devices)])  9.26 us
    pallas_call x3, Pallas kernels, partial_product(): pl.pallas_call(functools.partial(partial_kernel, [len(part) for part in p...  8.77 us
    dot_general x8, matrix products, ringed(): jnp.dot(hidden, w_down[0], preferred_element_type=jnp.float32)  8.54 us
    pallas_call x1, Pallas kernels, attention(): pl.pallas_call(functools.partial(attention_kernel, count), out_shape=jax....  6.33 us
  transfers between devices with their start and end apart: 57, of which 20 were waited for; matrix products, arithmetic and copies ran while one was open for 20% of the time, Pallas kernels for 9%

profile of v2, /device:TPU:0, one launch (start us, length us, event | category | flops | bytes accessed | tf_op | source)
XLA Modules:
  0.0 175.4 jit_solution(987908400726310449)
XLA Ops:
  0.7 3.1 %collective-permute-start = (bf16[128,256]{1,0:T(8,128)(2,1)}, bf16[128,256]{1,0:T(8,128)(2,1)S(1)}, u32[]{:S(2)}, u32[]{:S(2)}) collective-permute-start(bf16[128,256]{1,0:T(8,128)(2,1)} %refs_0_.1), channel_id=1, source_target_pairs={{0,4},{1,5},{2,6},{3,7},{4,8},{5,9},{6,10},{7,11},{8,12},{9,13},{1... | collective-permute-start | bytes 196616 | tf_op jit(solution)/shard_map/ppermute | solution.py:24
  3.8 2.6 %collective-permute-start.1 = (bf16[128,256]{1,0:T(8,128)(2,1)}, bf16[128,256]{1,0:T(8,128)(2,1)S(1)}, u32[]{:S(2)}, u32[]{:S(2)}) collective-permute-start(bf16[128,256]{1,0:T(8,128)(2,1)} %refs_0_.1), channel_id=1, source_target_pairs={{0,8},{1,9},{2,10},{3,11},{4,12},{5,13},{6,14},{7,15},{8,0},{9,1},... | collective-permute-start | bytes 196616 | tf_op jit(solution)/shard_map/ppermute | solution.py:24
  6.4 1.8 %fusion.186 = (bf16[1024,128]{1,0:T(8,128)(2,1)S(1)}, bf16[1024,128]{1,0:T(8,128)(2,1)}) fusion(bf16[2048,128]{1,0:T(8,128)(2,1)} %param.19), kind=kLoop, calls=%fused_computation.187 | loop fusion | bytes 1048576 | tf_op jit(solution)/shard_map/slice | solution.py:342
  8.1 1.5 collective-permute-start.8
  10.1 1.5 collective-permute-start.12
  12.2 1.3 collective-permute-start.2
  13.5 10.0 %collective-permute-done.2.refs_3_ = bf16[128,256]{1,0:T(8,128)(2,1)} collective-permute-done((bf16[128,256]{1,0:T(8,128)(2,1)}, bf16[128,256]{1,0:T(8,128)(2,1)}, u32[]{:S(2)}, u32[]{:S(2)}) %collective-permute-start.2) | collective-permute-done | bytes 65568 | tf_op jit(solution)/shard_map/ppermute | solution.py:24
  24.2 5.7 %collective-permute-done.3.refs_5_ = bf16[128,256]{1,0:T(8,128)(2,1)} collective-permute-done((bf16[128,256]{1,0:T(8,128)(2,1)}, bf16[128,256]{1,0:T(8,128)(2,1)}, u32[]{:S(2)}, u32[]{:S(2)}) %collective-permute-start.3) | collective-permute-done | bytes 65568 | tf_op jit(solution)/shard_map/ppermute | solution.py:24
  30.0 5.5 %collective-permute-done.4.refs_6_ = bf16[128,256]{1,0:T(8,128)(2,1)} collective-permute-done((bf16[128,256]{1,0:T(8,128)(2,1)}, bf16[128,256]{1,0:T(8,128)(2,1)}, u32[]{:S(2)}, u32[]{:S(2)}) %collective-permute-start.4) | collective-permute-done | bytes 65568 | tf_op jit(solution)/shard_map/ppermute | solution.py:24
  35.5 1.6 collective-permute-start.5
  37.1 2.0 %collective-permute-start.13 = (bf16[1024,128]{1,0:T(8,128)(2,1)}, bf16[1024,128]{1,0:T(8,128)(2,1)}, u32[]{:S(2)}, u32[]{:S(2)}) collective-permute-start(bf16[1024,128]{1,0:T(8,128)(2,1)} %collective-permute-done.11.refs_6_), channel_id=1, source_target_pairs={{0,4},{1,5},{2,0},{3,1},{4,8},{5,9},{6,2},{7,3},{8,12},{9,13},{10,... | collective-permute-start | bytes 786440 | tf_op jit(solution)/shard_map/ppermute | solution.py:320
  39.1 2.0 %collective-permute-start.9 = (bf16[1024,128]{1,0:T(8,128)(2,1)}, bf16[1024,128]{1,0:T(8,128)(2,1)}, u32[]{:S(2)}, u32[]{:S(2)}) collective-permute-start(bf16[1024,128]{1,0:T(8,128)(2,1)} %collective-permute-done.7.refs_1_), channel_id=1, source_target_pairs={{0,4},{1,5},{2,0},{3,1},{4,8},{5,9},{6,2},{7,3},{8,12},{9,13},{10,... | collective-permute-start | bytes 786440 | tf_op jit(solution)/shard_map/ppermute | solution.py:320
  41.1 1.2 dynamic-slice_bitcast_fusion.table
  42.3 6.3 %attention.1.own_ref = bf16[128,2048]{1,0:T(8,128)(2,1)} custom-call(s32[20]{0:T(128)} %dynamic-slice_bitcast_fusion.table, s32[16]{0:T(128)} %block_order.1, bf16[128,2048]{1,0:T(8,128)(2,1)} %q_ref.1, bf16[128,256]{1,0:T(8,128)(2,1)} %refs_0_.1, bf16[128,256]{1,0:T(8,128)(2,1)} %copy-done.6, bf16[128,256]{1,0:T(8,128)(2,1)} %copy-done.7, ...), custom_call_target="tpu_custom_call" | custom-call | flops 536870912 | bytes 1572864 | tf_op jit(solution)/shard_map/attention/pallas_call | solution.py:212
  49.2 1.6 collective-permute-start.18
  50.8 1.2 collective-permute-start.16
  52.8 5.4 %collective-permute-done.15.refs_0_ = bf16[1024,128]{1,0:T(8,128)(2,1)} collective-permute-done((bf16[1024,128]{1,0:T(8,128)(2,1)}, bf16[1024,128]{1,0:T(8,128)(2,1)}, u32[]{:S(2)}, u32[]{:S(2)}) %collective-permute-start.15) | collective-permute-done | bytes 262176 | tf_op jit(solution)/shard_map/ppermute | solution.py:320
  58.7 1.6 collective-permute-start.20
  60.3 3.8 %partial_product.3 = (f32[128,640]{1,0:T(8,128)}, f32[128,640]{1,0:T(8,128)}) custom-call(bf16[128,2048]{1,0:T(8,128)(2,1)} %attention.1.own_ref, bf16[128,2048]{1,0:T(8,128)(2,1)} %collective-permute-done.6.other_ref, bf16[1024,128]{1,0:T(8,128)(2,1)} %get-tuple-element.19.refs_0_, bf16[1024,128]{1,0:T(8,128)(2,1)} %collective-permute-done.7.refs_1_, ...), custom_call_target="tpu_custom_call" | custom-call | flops 671088640 | bytes 3670016 | tf_op jit(solution)/shard_map/partial_product/pallas_call | solution.py:248
  64.3 2.6 %partial_product.4 = (f32[128,256]{1,0:T(8,128)}, f32[128,256]{1,0:T(8,128)}) custom-call(bf16[128,2048]{1,0:T(8,128)(2,1)} %attention.1.own_ref, bf16[128,2048]{1,0:T(8,128)(2,1)} %collective-permute-done.6.other_ref, bf16[1024,128]{1,0:T(8,128)(2,1)} %collective-permute-done.15.refs_0_, bf16[1024,128]{1,0:T(8,128)(2,1)} %collective-permute-done.16.refs_1_, ...), custom_call_target="tpu_custom_call" | custom-call | flops 268435456 | bytes 2097152 | tf_op jit(solution)/shard_map/partial_product/pallas_call | solution.py:248
  67.2 1.8 %collective-permute-done.19.refs_0_ = bf16[1024,128]{1,0:T(8,128)(2,1)} collective-permute-done((bf16[1024,128]{1,0:T(8,128)(2,1)}, bf16[1024,128]{1,0:T(8,128)(2,1)}, u32[]{:S(2)}, u32[]{:S(2)}) %collective-permute-start.19) | collective-permute-done | bytes 262176 | tf_op jit(solution)/shard_map/ppermute | solution.py:320
  69.2 2.4 %partial_product.5 = (f32[128,128]{1,0:T(8,128)}, f32[128,128]{1,0:T(8,128)}) custom-call(bf16[128,2048]{1,0:T(8,128)(2,1)} %attention.1.own_ref, bf16[128,2048]{1,0:T(8,128)(2,1)} %collective-permute-done.6.other_ref, bf16[1024,128]{1,0:T(8,128)(2,1)} %collective-permute-done.19.refs_0_, bf16[1024,128]{1,0:T(8,128)(2,1)} %collective-permute-done.20.refs_1_), custom_call_target="tpu_custom_call" | custom-call | flops 134217728 | bytes 1572864 | tf_op jit(solution)/shard_map/partial_product/pallas_call | solution.py:248
  73.2 2.8 %finish.1 = (f32[128,2048]{1,0:T(8,128)}, bf16[128,2176]{1,0:T(8,128)(2,1)}) custom-call(s32[20]{0:T(128)} %dynamic-slice_bitcast_fusion.table, bf16[128,2048]{1,0:T(8,128)(2,1)} %residual_ref.1, f32[1,2048]{1,0:T(1,128)} %bitcast.101, bf16[128,128]{1,0:T(8,128)(2,1)} %pad.4.tags_ref, f32[128,640]{1,0:T(8,128)} %get-tuple-element.10.refs_0_, ...), custom_call_target="tpu_custom_call" | custom-call | flops 1572864 | bytes 3145728 | tf_op jit(solution)/shard_map/finish/pallas_call | solution.py:283
  78.9 6.8 %collective-permute-done.26 = bf16[128,2176]{1,0:T(8,128)(2,1)S(1)} collective-permute-done((bf16[128,2176]{1,0:T(8,128)(2,1)}, bf16[128,2176]{1,0:T(8,128)(2,1)S(1)}, u32[]{:S(2)}, u32[]{:S(2)}) %collective-permute-start.26) | collective-permute-done | bytes 557088 | tf_op jit(solution)/shard_map/ppermute | solution.py:320
  86.6 1.1 collective-permute-done.45
  87.7 4.7 %fusion = f32[256,1536]{1,0:T(8,128)S(1)} fusion(bf16[1,2048,1536]{2,1,0:T(8,128)(2,1)} %param.21, bf16[256,2176]{1,0:T(8,128)(2,1)S(1)} %constant_dynamic-update-slice_fusion.14), kind=kOutput, calls=%fused_computation | convolution fusion | flops 1610612736 | bytes 8912896 | tf_op jit(solution)/shard_map/dot_general | solution.py:369
  94.0 1.8 %fusion.14 = f32[256,1536]{1,0:T(8,128)S(1)} fusion(bf16[1,2048,1536]{2,1,0:T(8,128)(2,1)S(1)} %bitcast.111, bf16[256,2176]{1,0:T(8,128)(2,1)S(1)} %constant_dynamic-update-slice_fusion), kind=kOutput, calls=%fused_computation.14 | convolution fusion | flops 1610612736 | bytes 8912896 | tf_op jit(solution)/shard_map/dot_general | solution.py:369
  97.2 2.0 %collective-permute-start.47 = (bf16[128,2048]{1,0:T(8,128)(2,1)S(1)}, bf16[128,2048]{1,0:T(8,128)(2,1)S(1)}, u32[]{:S(2)}, u32[]{:S(2)}) collective-permute-start(bf16[128,2048]{1,0:T(8,128)(2,1)S(1)} %fusion.80), channel_id=1, source_target_pairs={{0,4},{1,3},{2,0},{3,7},{4,8},{5,1},{6,2},{7,11},{8,12},{9,5},{10,... | collective-permute-start | bytes 1572872 | tf_op jit(solution)/shard_map/ppermute | solution.py:320
  99.3 1.8 %fusion.2 = f32[256,1536]{1,0:T(8,128)S(1)} fusion(bf16[1,2048,1536]{2,1,0:T(8,128)(2,1)S(1)} %bitcast.111, bf16[256,2176]{1,0:T(8,128)(2,1)S(1)} %constant_dynamic-update-slice_fusion.12), kind=kOutput, calls=%fused_computation.2 | convolution fusion | flops 1610612736 | bytes 8912896 | tf_op jit(solution)/shard_map/dot_general | solution.py:369
  102.7 3.2 %collective-permute-done.28 = bf16[128,2176]{1,0:T(8,128)(2,1)S(1)} collective-permute-done((bf16[128,2176]{1,0:T(8,128)(2,1)S(1)}, bf16[128,2176]{1,0:T(8,128)(2,1)S(1)}, u32[]{:S(2)}, u32[]{:S(2)}) %collective-permute-start.28) | collective-permute-done | bytes 557088 | tf_op jit(solution)/shard_map/ppermute | solution.py:320
  106.7 4.8 %collective-permute-done.47 = bf16[128,2048]{1,0:T(8,128)(2,1)S(1)} collective-permute-done((bf16[128,2048]{1,0:T(8,128)(2,1)S(1)}, bf16[128,2048]{1,0:T(8,128)(2,1)S(1)}, u32[]{:S(2)}, u32[]{:S(2)}) %collective-permute-start.47) | collective-permute-done | bytes 524320 | tf_op jit(solution)/shard_map/ppermute | solution.py:320
  112.6 1.8 %fusion.4 = f32[256,1536]{1,0:T(8,128)S(1)} fusion(bf16[1,2048,1536]{2,1,0:T(8,128)(2,1)S(1)} %bitcast.111, bf16[256,2176]{1,0:T(8,128)(2,1)S(1)} %constant_dynamic-update-slice_fusion.10), kind=kOutput, calls=%fused_computation.4 | convolution fusion | flops 1610612736 | bytes 8912896 | tf_op jit(solution)/shard_map/dot_general | solution.py:369
  117.6 1.8 %collective-permute-start.30 = (bf16[128,2176]{1,0:T(8,128)(2,1)S(1)}, bf16[128,2176]{1,0:T(8,128)(2,1)S(1)}, u32[]{:S(2)}, u32[]{:S(2)}) collective-permute-start(bf16[128,2176]{1,0:T(8,128)(2,1)S(1)} %collective-permute-done.29), channel_id=1, source_target_pairs={{0,4},{1,3},{2,0},{3,7},{4,8},{5,1},{6,2},{7,11},{8,12},{9,5},{10,... | collective-permute-start | bytes 1671176 | tf_op jit(solution)/shard_map/ppermute | solution.py:320
  119.4 3.7 %collective-permute-done.48 = bf16[128,2048]{1,0:T(8,128)(2,1)S(1)} collective-permute-done((bf16[128,2048]{1,0:T(8,128)(2,1)S(1)}, bf16[128,2048]{1,0:T(8,128)(2,1)S(1)}, u32[]{:S(2)}, u32[]{:S(2)}) %collective-permute-start.48) | collective-permute-done | bytes 524320 | tf_op jit(solution)/shard_map/ppermute | solution.py:320
  124.4 1.8 %fusion.6 = f32[256,1536]{1,0:T(8,128)S(1)} fusion(bf16[1,2048,1536]{2,1,0:T(8,128)(2,1)S(1)} %bitcast.111, bf16[256,2176]{1,0:T(8,128)(2,1)S(1)} %constant_dynamic-update-slice_fusion.8), kind=kOutput, calls=%fused_computation.6 | convolution fusion | flops 1610612736 | bytes 8912896 | tf_op jit(solution)/shard_map/dot_general | solution.py:369
  126.1 2.9 %collective-permute-done.30 = bf16[128,2176]{1,0:T(8,128)(2,1)S(1)} collective-permute-done((bf16[128,2176]{1,0:T(8,128)(2,1)S(1)}, bf16[128,2176]{1,0:T(8,128)(2,1)S(1)}, u32[]{:S(2)}, u32[]{:S(2)}) %collective-permute-start.30) | collective-permute-done | bytes 557088 | tf_op jit(solution)/shard_map/ppermute | solution.py:320
  131.6 1.8 %fusion.8 = f32[256,1536]{1,0:T(8,128)S(1)} fusion(bf16[1,2048,1536]{2,1,0:T(8,128)(2,1)S(1)} %bitcast.111, bf16[256,2176]{1,0:T(8,128)(2,1)S(1)} %constant_dynamic-update-slice_fusion.6), kind=kOutput, calls=%fused_computation.8 | convolution fusion | flops 1610612736 | bytes 8912896 | tf_op jit(solution)/shard_map/dot_general | solution.py:369
  135.7 1.2 collective-permute-start.50
  136.9 3.8 %collective-permute-done.31 = bf16[128,2176]{1,0:T(8,128)(2,1)S(1)} collective-permute-done((bf16[128,2176]{1,0:T(8,128)(2,1)S(1)}, bf16[128,2176]{1,0:T(8,128)(2,1)S(1)}, u32[]{:S(2)}, u32[]{:S(2)}) %collective-permute-start.31) | collective-permute-done | bytes 557088 | tf_op jit(solution)/shard_map/ppermute | solution.py:320
  141.7 4.6 %collective-permute-done.50 = bf16[128,2048]{1,0:T(8,128)(2,1)S(1)} collective-permute-done((bf16[128,2048]{1,0:T(8,128)(2,1)S(1)}, bf16[128,2048]{1,0:T(8,128)(2,1)S(1)}, u32[]{:S(2)}, u32[]{:S(2)}) %collective-permute-start.50) | collective-permute-done | bytes 524320 | tf_op jit(solution)/shard_map/ppermute | solution.py:320
  147.4 1.8 %fusion.10 = f32[256,1536]{1,0:T(8,128)S(1)} fusion(bf16[1,2048,1536]{2,1,0:T(8,128)(2,1)S(1)} %bitcast.111, bf16[256,2176]{1,0:T(8,128)(2,1)S(1)} %constant_dynamic-update-slice_fusion.4), kind=kOutput, calls=%fused_computation.10 | convolution fusion | flops 1610612736 | bytes 8912896 | tf_op jit(solution)/shard_map/dot_general | solution.py:369
  150.7 1.8 %collective-permute-start.54 = (bf16[48,2048]{1,0:T(8,128)(2,1)S(1)}, bf16[48,2048]{1,0:T(8,128)(2,1)S(1)}, u32[]{:S(2)}, u32[]{:S(2)}) collective-permute-start(bf16[48,2048]{1,0:T(8,128)(2,1)S(1)} %fusion.149), channel_id=1, source_target_pairs={{0,4},{1,3},{2,0},{3,7},{4,8},{5,1},{6,2},{7,11},{8,12},{9,5},{10,... | collective-permute-start | bytes 589832 | tf_op jit(solution)/shard_map/ppermute | solution.py:320
  152.7 1.8 %collective-permute-done.33 = bf16[128,2176]{1,0:T(8,128)(2,1)S(1)} collective-permute-done((bf16[128,2176]{1,0:T(8,128)(2,1)S(1)}, bf16[128,2176]{1,0:T(8,128)(2,1)S(1)}, u32[]{:S(2)}, u32[]{:S(2)}) %collective-permute-start.33) | collective-permute-done | bytes 557088 | tf_op jit(solution)/shard_map/ppermute | solution.py:320
  154.5 1.8 %fusion.12 = f32[256,1536]{1,0:T(8,128)S(1)} fusion(bf16[1,2048,1536]{2,1,0:T(8,128)(2,1)S(1)} %bitcast.111, bf16[256,2176]{1,0:T(8,128)(2,1)S(1)} %constant_dynamic-update-slice_fusion.2), kind=kOutput, calls=%fused_computation.12 | convolution fusion | flops 1610612736 | bytes 8912896 | tf_op jit(solution)/shard_map/dot_general | solution.py:369
  158.6 1.7 collective-permute-start.55
  160.5 4.6 %collective-permute-done.52 = bf16[80,2048]{1,0:T(8,128)(2,1)S(1)} collective-permute-done((bf16[80,2048]{1,0:T(8,128)(2,1)S(1)}, bf16[80,2048]{1,0:T(8,128)(2,1)S(1)}, u32[]{:S(2)}, u32[]{:S(2)}) %collective-permute-start.52) | collective-permute-done | bytes 327712 | tf_op jit(solution)/shard_map/ppermute | solution.py:320
  165.8 1.3 collective-permute-done.55
  167.9 6.5 %collective-permute-done.56 = bf16[48,2048]{1,0:T(8,128)(2,1)S(1)} collective-permute-done((bf16[48,2048]{1,0:T(8,128)(2,1)S(1)}, bf16[48,2048]{1,0:T(8,128)(2,1)S(1)}, u32[]{:S(2)}, u32[]{:S(2)}) %collective-permute-start.56) | collective-permute-done | bytes 196640 | tf_op jit(solution)/shard_map/ppermute | solution.py:320
  (165 shorter events, 34.1 us)
Async XLA Ops:
  0.7 11.0 %collective-permute-start = (bf16[128,256]{1,0:T(8,128)(2,1)}, bf16[128,256]{1,0:T(8,128)(2,1)S(1)}, u32[]{:S(2)}, u32[]{:S(2)}) collective-permute-start(bf16[128,256]{1,0:T(8,128)(2,1)} %refs_0_.1), channel_id=1, source_target_pairs={{0,4},{1,5},{2,6},{3,7},{4,8},{5,9},{6,10},{7,11},{8,12},{9,13},{1... | collective-permute-start | bytes 196616 | tf_op jit(solution)/shard_map/ppermute | solution.py:24
  3.8 8.4 %collective-permute-start.1 = (bf16[128,256]{1,0:T(8,128)(2,1)}, bf16[128,256]{1,0:T(8,128)(2,1)S(1)}, u32[]{:S(2)}, u32[]{:S(2)}) collective-permute-start(bf16[128,256]{1,0:T(8,128)(2,1)} %refs_0_.1), channel_id=1, source_target_pairs={{0,8},{1,9},{2,10},{3,11},{4,12},{5,13},{6,14},{7,15},{8,0},{9,1},... | collective-permute-start | bytes 196616 | tf_op jit(solution)/shard_map/ppermute | solution.py:24
  8.1 28.9 %collective-permute-start.8 = (bf16[1024,128]{1,0:T(8,128)(2,1)}, bf16[1024,128]{1,0:T(8,128)(2,1)}, u32[]{:S(2)}, u32[]{:S(2)}) collective-permute-start(bf16[1024,128]{1,0:T(8,128)(2,1)} %get-tuple-element.19.refs_0_), channel_id=1, source_target_pairs={{0,2},{1,3},{2,6},{3,7},{4,0},{5,1},{6,10},{7,11},{8,4},{9,5},{10,... | collective-permute-start | bytes 786440 | tf_op jit(solution)/shard_map/ppermute | solution.py:320
  9.6 27.4 %collective-permute-start.11 = (bf16[1024,128]{1,0:T(8,128)(2,1)S(1)}, bf16[1024,128]{1,0:T(8,128)(2,1)}, u32[]{:S(2)}, u32[]{:S(2)}) collective-permute-start(bf16[1024,128]{1,0:T(8,128)(2,1)S(1)} %get-tuple-element.18.refs_5_), channel_id=1, source_target_pairs={{0,4},{1,5},{2,0},{3,1},{4,8},{5,9},{6,2},{7,3},{8,12},{9,13},{10,... | collective-permute-start | bytes 786440 | tf_op jit(solution)/shard_map/ppermute | solution.py:320
  10.1 28.9 %collective-permute-start.12 = (bf16[1024,128]{1,0:T(8,128)(2,1)S(1)}, bf16[1024,128]{1,0:T(8,128)(2,1)}, u32[]{:S(2)}, u32[]{:S(2)}) collective-permute-start(bf16[1024,128]{1,0:T(8,128)(2,1)S(1)} %get-tuple-element.18.refs_5_), channel_id=1, source_target_pairs={{0,2},{1,3},{2,6},{3,7},{4,0},{5,1},{6,10},{7,11},{8,4},{9,5},{10,... | collective-permute-start | bytes 786440 | tf_op jit(solution)/shard_map/ppermute | solution.py:320
  11.7 27.5 %collective-permute-start.7 = (bf16[1024,128]{1,0:T(8,128)(2,1)}, bf16[1024,128]{1,0:T(8,128)(2,1)}, u32[]{:S(2)}, u32[]{:S(2)}) collective-permute-start(bf16[1024,128]{1,0:T(8,128)(2,1)} %get-tuple-element.19.refs_0_), channel_id=1, source_target_pairs={{0,4},{1,5},{2,0},{3,1},{4,8},{5,9},{6,2},{7,3},{8,12},{9,13},{10,... | collective-permute-start | bytes 786440 | tf_op jit(solution)/shard_map/ppermute | solution.py:320
  12.2 11.4 %collective-permute-start.2 = (bf16[128,256]{1,0:T(8,128)(2,1)}, bf16[128,256]{1,0:T(8,128)(2,1)}, u32[]{:S(2)}, u32[]{:S(2)}) collective-permute-start(bf16[128,256]{1,0:T(8,128)(2,1)} %refs_0_.1), channel_id=1, source_target_pairs={{0,12},{1,13},{2,14},{3,15},{4,0},{5,1},{6,2},{7,3},{8,4},{9,5},{1... | collective-permute-start | bytes 196616 | tf_op jit(solution)/shard_map/ppermute | solution.py:24
  23.6 6.4 %collective-permute-start.3 = (bf16[128,256]{1,0:T(8,128)(2,1)}, bf16[128,256]{1,0:T(8,128)(2,1)}, u32[]{:S(2)}, u32[]{:S(2)}) collective-permute-start(bf16[128,256]{1,0:T(8,128)(2,1)} %refs_4_.1), channel_id=1, source_target_pairs={{0,4},{1,5},{2,6},{3,7},{4,8},{5,9},{6,10},{7,11},{8,12},{9,13},{1... | collective-permute-start | bytes 196616 | tf_op jit(solution)/shard_map/ppermute | solution.py:24
  30.0 5.5 %collective-permute-start.4 = (bf16[128,256]{1,0:T(8,128)(2,1)}, bf16[128,256]{1,0:T(8,128)(2,1)}, u32[]{:S(2)}, u32[]{:S(2)}) collective-permute-start(bf16[128,256]{1,0:T(8,128)(2,1)} %refs_4_.1), channel_id=1, source_target_pairs={{0,8},{1,9},{2,10},{3,11},{4,12},{5,13},{6,14},{7,15},{8,0},{9,1},... | collective-permute-start | bytes 196616 | tf_op jit(solution)/shard_map/ppermute | solution.py:24
  35.5 6.8 %collective-permute-start.5 = (bf16[128,256]{1,0:T(8,128)(2,1)}, bf16[128,256]{1,0:T(8,128)(2,1)}, u32[]{:S(2)}, u32[]{:S(2)}) collective-permute-start(bf16[128,256]{1,0:T(8,128)(2,1)} %refs_4_.1), channel_id=1, source_target_pairs={{0,12},{1,13},{2,14},{3,15},{4,0},{5,1},{6,2},{7,3},{8,4},{9,5},{1... | collective-permute-start | bytes 196616 | tf_op jit(solution)/shard_map/ppermute | solution.py:24
  37.0 13.7 %collective-permute-start.10 = (bf16[1024,128]{1,0:T(8,128)(2,1)}, bf16[1024,128]{1,0:T(8,128)(2,1)}, u32[]{:S(2)}, u32[]{:S(2)}) collective-permute-start(bf16[1024,128]{1,0:T(8,128)(2,1)} %collective-permute-done.8.refs_2_), channel_id=1, source_target_pairs={{0,2},{1,3},{2,6},{3,7},{4,0},{5,1},{6,10},{7,11},{8,4},{9,5},{10,... | collective-permute-start | bytes 786440 | tf_op jit(solution)/shard_map/ppermute | solution.py:320
  37.1 15.0 %collective-permute-start.13 = (bf16[1024,128]{1,0:T(8,128)(2,1)}, bf16[1024,128]{1,0:T(8,128)(2,1)}, u32[]{:S(2)}, u32[]{:S(2)}) collective-permute-start(bf16[1024,128]{1,0:T(8,128)(2,1)} %collective-permute-done.11.refs_6_), channel_id=1, source_target_pairs={{0,4},{1,5},{2,0},{3,1},{4,8},{5,9},{6,2},{7,3},{8,12},{9,13},{10,... | collective-permute-start | bytes 786440 | tf_op jit(solution)/shard_map/ppermute | solution.py:320
  39.1 10.1 %collective-permute-start.14 = (bf16[1024,128]{1,0:T(8,128)(2,1)}, bf16[1024,128]{1,0:T(8,128)(2,1)}, u32[]{:S(2)}, u32[]{:S(2)}) collective-permute-start(bf16[1024,128]{1,0:T(8,128)(2,1)} %collective-permute-done.12.refs_7_), channel_id=1, source_target_pairs={{0,2},{1,3},{2,6},{3,7},{4,0},{5,1},{6,10},{7,11},{8,4},{9,5},{10,... | collective-permute-start | bytes 786440 | tf_op jit(solution)/shard_map/ppermute | solution.py:320
  39.1 9.6 %collective-permute-start.9 = (bf16[1024,128]{1,0:T(8,128)(2,1)}, bf16[1024,128]{1,0:T(8,128)(2,1)}, u32[]{:S(2)}, u32[]{:S(2)}) collective-permute-start(bf16[1024,128]{1,0:T(8,128)(2,1)} %collective-permute-done.7.refs_1_), channel_id=1, source_target_pairs={{0,4},{1,5},{2,0},{3,1},{4,8},{5,9},{6,2},{7,3},{8,12},{9,13},{10,... | collective-permute-start | bytes 786440 | tf_op jit(solution)/shard_map/ppermute | solution.py:320
  48.7 11.6 %collective-permute-start.6 = (bf16[128,2048]{1,0:T(8,128)(2,1)}, bf16[128,2048]{1,0:T(8,128)(2,1)}, u32[]{:S(2)}, u32[]{:S(2)}) collective-permute-start(bf16[128,2048]{1,0:T(8,128)(2,1)} %attention.1.own_ref), channel_id=1, source_target_pairs={{0,1},{1,0},{2,3},{3,2},{4,5},{5,4},{6,7},{7,6},{8,9},{9,8},{10,11... | collective-permute-start | bytes 1572872 | tf_op jit(solution)/shard_map/ppermute | solution.py:320
  48.7 9.5 %collective-permute-start.15 = (bf16[1024,128]{1,0:T(8,128)(2,1)}, bf16[1024,128]{1,0:T(8,128)(2,1)}, u32[]{:S(2)}, u32[]{:S(2)}) collective-permute-start(bf16[1024,128]{1,0:T(8,128)(2,1)} %collective-permute-done.9.refs_3_), channel_id=1, source_target_pairs={{0,4},{1,5},{2,0},{3,1},{4,8},{5,9},{6,2},{7,3},{8,12},{9,13},{10,... | collective-permute-start | bytes 786440 | tf_op jit(solution)/shard_map/ppermute | solution.py:320
  49.2 9.5 %collective-permute-start.18 = (bf16[1024,128]{1,0:T(8,128)(2,1)}, bf16[1024,128]{1,0:T(8,128)(2,1)}, u32[]{:S(2)}, u32[]{:S(2)}) collective-permute-start(bf16[1024,128]{1,0:T(8,128)(2,1)} %collective-permute-done.14.refs_9_), channel_id=1, source_target_pairs={{0,2},{1,3},{2,6},{3,7},{4,0},{5,1},{6,10},{7,11},{8,4},{9,5},{10,... | collective-permute-start | bytes 786440 | tf_op jit(solution)/shard_map/ppermute | solution.py:320
  50.8 13.5 %collective-permute-start.16 = (bf16[1024,128]{1,0:T(8,128)(2,1)}, bf16[1024,128]{1,0:T(8,128)(2,1)}, u32[]{:S(2)}, u32[]{:S(2)}) collective-permute-start(bf16[1024,128]{1,0:T(8,128)(2,1)} %collective-permute-done.10.refs_4_), channel_id=1, source_target_pairs={{0,2},{1,3},{2,6},{3,7},{4,0},{5,1},{6,10},{7,11},{8,4},{9,5},{10,... | collective-permute-start | bytes 786440 | tf_op jit(solution)/shard_map/ppermute | solution.py:320
  52.0 12.3 %collective-permute-start.17 = (bf16[1024,128]{1,0:T(8,128)(2,1)}, bf16[1024,128]{1,0:T(8,128)(2,1)}, u32[]{:S(2)}, u32[]{:S(2)}) collective-permute-start(bf16[1024,128]{1,0:T(8,128)(2,1)} %collective-permute-done.13.refs_8_), channel_id=1, source_target_pairs={{0,4},{1,5},{2,0},{3,1},{4,8},{5,9},{6,2},{7,3},{8,12},{9,13},{10,... | collective-permute-start | bytes 786440 | tf_op jit(solution)/shard_map/ppermute | solution.py:320
  58.2 10.8 %collective-permute-start.19 = (bf16[1024,128]{1,0:T(8,128)(2,1)}, bf16[1024,128]{1,0:T(8,128)(2,1)}, u32[]{:S(2)}, u32[]{:S(2)}) collective-permute-start(bf16[1024,128]{1,0:T(8,128)(2,1)} %collective-permute-done.15.refs_0_), channel_id=1, source_target_pairs={{0,4},{1,5},{2,0},{3,1},{4,8},{5,9},{6,2},{7,3},{8,12},{9,13},{10,... | collective-permute-start | bytes 786440 | tf_op jit(solution)/shard_map/ppermute | solution.py:320
  58.7 10.5 %collective-permute-start.20 = (bf16[1024,128]{1,0:T(8,128)(2,1)}, bf16[1024,128]{1,0:T(8,128)(2,1)}, u32[]{:S(2)}, u32[]{:S(2)}) collective-permute-start(bf16[1024,128]{1,0:T(8,128)(2,1)} %collective-permute-done.18.refs_3_), channel_id=1, source_target_pairs={{0,2},{1,3},{2,6},{3,7},{4,0},{5,1},{6,10},{7,11},{8,4},{9,5},{10,... | collective-permute-start | bytes 786440 | tf_op jit(solution)/shard_map/ppermute | solution.py:320
  64.0 8.3 %collective-permute-start.21 = (f32[128,640]{1,0:T(8,128)}, f32[128,640]{1,0:T(8,128)S(1)}, u32[]{:S(2)}, u32[]{:S(2)}) collective-permute-start(f32[128,640]{1,0:T(8,128)} %get-tuple-element.13), channel_id=1, source_target_pairs={{0,1},{1,0},{2,3},{3,2},{4,5},{5,4},{6,7},{7,6},{8,9},{9,8},{10,11... | collective-permute-start | bytes 983048 | tf_op jit(solution)/shard_map/ppermute | solution.py:320
  66.9 5.4 %collective-permute-start.22 = (f32[128,256]{1,0:T(8,128)}, f32[128,256]{1,0:T(8,128)}, u32[]{:S(2)}, u32[]{:S(2)}) collective-permute-start(f32[128,256]{1,0:T(8,128)} %get-tuple-element.14), channel_id=1, source_target_pairs={{0,1},{1,0},{2,3},{3,2},{4,5},{5,4},{6,7},{7,6},{8,9},{9,8},{10,11... | collective-permute-start | bytes 393224 | tf_op jit(solution)/shard_map/ppermute | solution.py:320
  76.0 9.7 %collective-permute-start.26 = (bf16[128,2176]{1,0:T(8,128)(2,1)}, bf16[128,2176]{1,0:T(8,128)(2,1)S(1)}, u32[]{:S(2)}, u32[]{:S(2)}) collective-permute-start(bf16[128,2176]{1,0:T(8,128)(2,1)} %get-tuple-element.17), channel_id=1, source_target_pairs={{0,4},{1,3},{2,0},{3,7},{4,8},{5,1},{6,2},{7,11},{8,12},{9,5},{10,... | collective-permute-start | bytes 1671176 | tf_op jit(solution)/shard_map/ppermute | solution.py:320
  76.8 9.7 %collective-permute-start.24 = (bf16[128,2176]{1,0:T(8,128)(2,1)}, bf16[128,2176]{1,0:T(8,128)(2,1)S(1)}, u32[]{:S(2)}, u32[]{:S(2)}) collective-permute-start(bf16[128,2176]{1,0:T(8,128)(2,1)} %get-tuple-element.17), channel_id=1, source_target_pairs={{0,1},{1,0},{2,3},{3,2},{4,5},{5,4},{6,7},{7,6},{8,9},{9,8},{10,11... | collective-permute-start | bytes 1671176 | tf_op jit(solution)/shard_map/ppermute | solution.py:320
  85.7 10.1 %collective-permute-start.27 = (bf16[128,2176]{1,0:T(8,128)(2,1)S(1)}, bf16[128,2176]{1,0:T(8,128)(2,1)S(1)}, u32[]{:S(2)}, u32[]{:S(2)}) collective-permute-start(bf16[128,2176]{1,0:T(8,128)(2,1)S(1)} %collective-permute-done.26), channel_id=1, source_target_pairs={{0,4},{1,3},{2,0},{3,7},{4,8},{5,1},{6,2},{7,11},{8,12},{9,5},{10,... | collective-permute-start | bytes 1671176 | tf_op jit(solution)/shard_map/ppermute | solution.py:320
  96.3 9.6 %collective-permute-start.28 = (bf16[128,2176]{1,0:T(8,128)(2,1)S(1)}, bf16[128,2176]{1,0:T(8,128)(2,1)S(1)}, u32[]{:S(2)}, u32[]{:S(2)}) collective-permute-start(bf16[128,2176]{1,0:T(8,128)(2,1)S(1)} %collective-permute-done.27), channel_id=1, source_target_pairs={{0,4},{1,3},{2,0},{3,7},{4,8},{5,1},{6,2},{7,11},{8,12},{9,5},{10,... | collective-permute-start | bytes 1671176 | tf_op jit(solution)/shard_map/ppermute | solution.py:320
  97.2 14.3 %collective-permute-start.47 = (bf16[128,2048]{1,0:T(8,128)(2,1)S(1)}, bf16[128,2048]{1,0:T(8,128)(2,1)S(1)}, u32[]{:S(2)}, u32[]{:S(2)}) collective-permute-start(bf16[128,2048]{1,0:T(8,128)(2,1)S(1)} %fusion.80), channel_id=1, source_target_pairs={{0,4},{1,3},{2,0},{3,7},{4,8},{5,1},{6,2},{7,11},{8,12},{9,5},{10,... | collective-permute-start | bytes 1572872 | tf_op jit(solution)/shard_map/ppermute | solution.py:320
  102.4 9.1 %collective-permute-start.44 = (bf16[128,2048]{1,0:T(8,128)(2,1)S(1)}, bf16[128,2048]{1,0:T(8,128)(2,1)S(1)}, u32[]{:S(2)}, u32[]{:S(2)}) collective-permute-start(bf16[128,2048]{1,0:T(8,128)(2,1)S(1)} %slice.453), channel_id=1, source_target_pairs={{0,1},{1,0},{2,3},{3,2},{4,5},{5,4},{6,7},{7,6},{8,9},{9,8},{10,11... | collective-permute-start | bytes 1572872 | tf_op jit(solution)/shard_map/ppermute | solution.py:320
  105.9 6.6 %collective-permute-start.41 = (bf16[128,2176]{1,0:T(8,128)(2,1)S(1)}, bf16[128,2176]{1,0:T(8,128)(2,1)S(1)}, u32[]{:S(2)}, u32[]{:S(2)}) collective-permute-start(bf16[128,2176]{1,0:T(8,128)(2,1)S(1)} %collective-permute-done.28), channel_id=1, source_target_pairs={{0,1},{1,0},{2,3},{3,2},{4,5},{5,4},{6,7},{7,6},{8,9},{9,8},{10,11... | collective-permute-start | bytes 1671176 | tf_op jit(solution)/shard_map/ppermute | solution.py:320
  105.9 11.5 %collective-permute-start.29 = (bf16[128,2176]{1,0:T(8,128)(2,1)S(1)}, bf16[128,2176]{1,0:T(8,128)(2,1)S(1)}, u32[]{:S(2)}, u32[]{:S(2)}) collective-permute-start(bf16[128,2176]{1,0:T(8,128)(2,1)S(1)} %collective-permute-done.28), channel_id=1, source_target_pairs={{0,4},{1,3},{2,0},{3,7},{4,8},{5,1},{6,2},{7,11},{8,12},{9,5},{10,... | collective-permute-start | bytes 1671176 | tf_op jit(solution)/shard_map/ppermute | solution.py:320
  111.7 11.4 %collective-permute-start.48 = (bf16[128,2048]{1,0:T(8,128)(2,1)S(1)}, bf16[128,2048]{1,0:T(8,128)(2,1)S(1)}, u32[]{:S(2)}, u32[]{:S(2)}) collective-permute-start(bf16[128,2048]{1,0:T(8,128)(2,1)S(1)} %fusion.83), channel_id=1, source_target_pairs={{0,4},{1,3},{2,0},{3,7},{4,8},{5,1},{6,2},{7,11},{8,12},{9,5},{10,... | collective-permute-start | bytes 1572872 | tf_op jit(solution)/shard_map/ppermute | solution.py:320
  115.7 7.4 %collective-permute-start.42 = (bf16[128,2048]{1,0:T(8,128)(2,1)S(1)}, bf16[128,2048]{1,0:T(8,128)(2,1)S(1)}, u32[]{:S(2)}, u32[]{:S(2)}) collective-permute-start(bf16[128,2048]{1,0:T(8,128)(2,1)S(1)} %slice.454), channel_id=1, source_target_pairs={{0,1},{1,0},{2,3},{3,2},{4,5},{5,4},{6,7},{7,6},{8,9},{9,8},{10,11... | collective-permute-start | bytes 1572872 | tf_op jit(solution)/shard_map/ppermute | solution.py:320
  116.9 51.0 %collective-permute-start.25 = (bf16[128,2048]{1,0:T(8,128)(2,1)S(1)}, bf16[128,2048]{1,0:T(8,128)(2,1)S(1)}, u32[]{:S(2)}, u32[]{:S(2)}) collective-permute-start(bf16[128,2048]{1,0:T(8,128)(2,1)S(1)} %slice.459), channel_id=1, source_target_pairs={{0,1},{1,0},{2,3},{3,2},{4,5},{5,4},{6,7},{7,6},{8,9},{9,8},{10,11... | collective-permute-start | bytes 1572872 | tf_op jit(solution)/shard_map/ppermute | solution.py:320
  117.5 6.6 %collective-permute-start.39 = (bf16[128,2176]{1,0:T(8,128)(2,1)S(1)}, bf16[128,2176]{1,0:T(8,128)(2,1)S(1)}, u32[]{:S(2)}, u32[]{:S(2)}) collective-permute-start(bf16[128,2176]{1,0:T(8,128)(2,1)S(1)} %collective-permute-done.29), channel_id=1, source_target_pairs={{0,1},{1,0},{2,3},{3,2},{4,5},{5,4},{6,7},{7,6},{8,9},{9,8},{10,11... | collective-permute-start | bytes 1671176 | tf_op jit(solution)/shard_map/ppermute | solution.py:320
  117.6 11.4 %collective-permute-start.30 = (bf16[128,2176]{1,0:T(8,128)(2,1)S(1)}, bf16[128,2176]{1,0:T(8,128)(2,1)S(1)}, u32[]{:S(2)}, u32[]{:S(2)}) collective-permute-start(bf16[128,2176]{1,0:T(8,128)(2,1)S(1)} %collective-permute-done.29), channel_id=1, source_target_pairs={{0,4},{1,3},{2,0},{3,7},{4,8},{5,1},{6,2},{7,11},{8,12},{9,5},{10,... | collective-permute-start | bytes 1671176 | tf_op jit(solution)/shard_map/ppermute | solution.py:320
  123.3 12.2 %collective-permute-start.49 = (bf16[128,2048]{1,0:T(8,128)(2,1)S(1)}, bf16[128,2048]{1,0:T(8,128)(2,1)S(1)}, u32[]{:S(2)}, u32[]{:S(2)}) collective-permute-start(bf16[128,2048]{1,0:T(8,128)(2,1)S(1)} %fusion.86), channel_id=1, source_target_pairs={{0,4},{1,3},{2,0},{3,7},{4,8},{5,1},{6,2},{7,11},{8,12},{9,5},{10,... | collective-permute-start | bytes 1572872 | tf_op jit(solution)/shard_map/ppermute | solution.py:320
  130.8 9.9 %collective-permute-start.31 = (bf16[128,2176]{1,0:T(8,128)(2,1)S(1)}, bf16[128,2176]{1,0:T(8,128)(2,1)S(1)}, u32[]{:S(2)}, u32[]{:S(2)}) collective-permute-start(bf16[128,2176]{1,0:T(8,128)(2,1)S(1)} %collective-permute-done.30), channel_id=1, source_target_pairs={{0,4},{1,3},{2,0},{3,7},{4,8},{5,1},{6,2},{7,11},{8,12},{9,5},{10,... | collective-permute-start | bytes 1671176 | tf_op jit(solution)/shard_map/ppermute | solution.py:320
  134.8 6.8 %collective-permute-start.38 = (bf16[128,2048]{1,0:T(8,128)(2,1)S(1)}, bf16[128,2048]{1,0:T(8,128)(2,1)S(1)}, u32[]{:S(2)}, u32[]{:S(2)}) collective-permute-start(bf16[128,2048]{1,0:T(8,128)(2,1)S(1)} %slice.456), channel_id=1, source_target_pairs={{0,1},{1,0},{2,3},{3,2},{4,5},{5,4},{6,7},{7,6},{8,9},{9,8},{10,11... | collective-permute-start | bytes 1572872 | tf_op jit(solution)/shard_map/ppermute | solution.py:320
  135.7 10.6 %collective-permute-start.50 = (bf16[128,2048]{1,0:T(8,128)(2,1)S(1)}, bf16[128,2048]{1,0:T(8,128)(2,1)S(1)}, u32[]{:S(2)}, u32[]{:S(2)}) collective-permute-start(bf16[128,2048]{1,0:T(8,128)(2,1)S(1)} %fusion.89), channel_id=1, source_target_pairs={{0,4},{1,3},{2,0},{3,7},{4,8},{5,1},{6,2},{7,11},{8,12},{9,5},{10,... | collective-permute-start | bytes 1572872 | tf_op jit(solution)/shard_map/ppermute | solution.py:320
  140.7 6.6 %collective-permute-start.35 = (bf16[128,2176]{1,0:T(8,128)(2,1)S(1)}, bf16[128,2176]{1,0:T(8,128)(2,1)S(1)}, u32[]{:S(2)}, u32[]{:S(2)}) collective-permute-start(bf16[128,2176]{1,0:T(8,128)(2,1)S(1)} %collective-permute-done.31), channel_id=1, source_target_pairs={{0,1},{1,0},{2,3},{3,2},{4,5},{5,4},{6,7},{7,6},{8,9},{9,8},{10,11... | collective-permute-start | bytes 1671176 | tf_op jit(solution)/shard_map/ppermute | solution.py:320
  140.8 11.7 %collective-permute-start.32 = (bf16[128,2176]{1,0:T(8,128)(2,1)S(1)}, bf16[128,2176]{1,0:T(8,128)(2,1)S(1)}, u32[]{:S(2)}, u32[]{:S(2)}) collective-permute-start(bf16[128,2176]{1,0:T(8,128)(2,1)S(1)} %collective-permute-done.31), channel_id=1, source_target_pairs={{0,4},{1,3},{2,0},{3,7},{4,8},{5,1},{6,2},{7,11},{8,12},{9,5},{10,... | collective-permute-start | bytes 1671176 | tf_op jit(solution)/shard_map/ppermute | solution.py:320
  146.3 11.5 %collective-permute-start.51 = (bf16[80,2048]{1,0:T(8,128)(2,1)S(1)}, bf16[80,2048]{1,0:T(8,128)(2,1)S(1)}, u32[]{:S(2)}, u32[]{:S(2)}) collective-permute-start(bf16[80,2048]{1,0:T(8,128)(2,1)S(1)} %fusion.106), channel_id=1, source_target_pairs={{0,4},{1,3},{2,0},{3,7},{4,8},{5,1},{6,2},{7,11},{8,12},{9,5},{10,... | collective-permute-start | bytes 983048 | tf_op jit(solution)/shard_map/ppermute | solution.py:320
  150.7 7.9 %collective-permute-start.54 = (bf16[48,2048]{1,0:T(8,128)(2,1)S(1)}, bf16[48,2048]{1,0:T(8,128)(2,1)S(1)}, u32[]{:S(2)}, u32[]{:S(2)}) collective-permute-start(bf16[48,2048]{1,0:T(8,128)(2,1)S(1)} %fusion.149), channel_id=1, source_target_pairs={{0,4},{1,3},{2,0},{3,7},{4,8},{5,1},{6,2},{7,11},{8,12},{9,5},{10,... | collective-permute-start | bytes 589832 | tf_op jit(solution)/shard_map/ppermute | solution.py:320
  157.9 7.1 %collective-permute-start.52 = (bf16[80,2048]{1,0:T(8,128)(2,1)S(1)}, bf16[80,2048]{1,0:T(8,128)(2,1)S(1)}, u32[]{:S(2)}, u32[]{:S(2)}) collective-permute-start(bf16[80,2048]{1,0:T(8,128)(2,1)S(1)} %fusion.107), channel_id=1, source_target_pairs={{0,4},{1,3},{2,0},{3,7},{4,8},{5,1},{6,2},{7,11},{8,12},{9,5},{10,... | collective-permute-start | bytes 983048 | tf_op jit(solution)/shard_map/ppermute | solution.py:320
  158.6 8.5 %collective-permute-start.55 = (bf16[48,2048]{1,0:T(8,128)(2,1)S(1)}, bf16[48,2048]{1,0:T(8,128)(2,1)S(1)}, u32[]{:S(2)}, u32[]{:S(2)}) collective-permute-start(bf16[48,2048]{1,0:T(8,128)(2,1)S(1)} %fusion.150), channel_id=1, source_target_pairs={{0,4},{1,3},{2,0},{3,7},{4,8},{5,1},{6,2},{7,11},{8,12},{9,5},{10,... | collective-permute-start | bytes 589832 | tf_op jit(solution)/shard_map/ppermute | solution.py:320
  165.1 9.2 %collective-permute-start.53 = (bf16[80,2048]{1,0:T(8,128)(2,1)S(1)}, bf16[80,2048]{1,0:T(8,128)(2,1)S(1)}, u32[]{:S(2)}, u32[]{:S(2)}) collective-permute-start(bf16[80,2048]{1,0:T(8,128)(2,1)S(1)} %fusion.108), channel_id=1, source_target_pairs={{0,4},{1,3},{2,0},{3,7},{4,8},{5,1},{6,2},{7,11},{8,12},{9,5},{10,... | collective-permute-start | bytes 983048 | tf_op jit(solution)/shard_map/ppermute | solution.py:320
  167.2 7.2 %collective-permute-start.56 = (bf16[48,2048]{1,0:T(8,128)(2,1)S(1)}, bf16[48,2048]{1,0:T(8,128)(2,1)S(1)}, u32[]{:S(2)}, u32[]{:S(2)}) collective-permute-start(bf16[48,2048]{1,0:T(8,128)(2,1)S(1)} %fusion.151), channel_id=1, source_target_pairs={{0,4},{1,3},{2,0},{3,7},{4,8},{5,1},{6,2},{7,11},{8,12},{9,5},{10,... | collective-permute-start | bytes 589832 | tf_op jit(solution)/shard_map/ppermute | solution.py:320
  (19 other events, 359.0 us)

commit v3 on v2

--- a/solution.py
+++ b/solution.py
@@ -15,6 +15,7 @@
 KEY_VALUE_HEADS = 2
 TOPK = 8
 SEQS = 4
+KERNEL_BYTES = 16 << 20
 PARTS = 1
 TAIL = 3
 
@@ -220,6 +221,7 @@
             bytes_accessed=4 * rows * width + 4 * count * keys[0].size,
             transcendentals=rows * rows * count * QUERY_HEADS,
         ),
+        compiler_params=pltpu.CompilerParams(vmem_limit_bytes=KERNEL_BYTES),
         name="attention",
     )(table, block_order, queries, *keys, *values)
 
@@ -290,6 +292,7 @@
         cost_estimate=pl.CostEstimate(
             flops=6 * rows * width, bytes_accessed=12 * rows * width, transcendentals=rows
         ),
+        compiler_params=pltpu.CompilerParams(vmem_limit_bytes=KERNEL_BYTES),
         name="finish",
     )(table, residual, gain.reshape(1, width), tags, *pieces)
 
@@ -350,8 +353,17 @@
     other_context = sent(context, "pair")
     pieces, away = [], []
     early = [whole] + [block for got in rounds[:-2] for block in got]
-    for got in [early] + rounds[-2:]:
-        mine, theirs = partial_product(context, other_context, list(zip(*got)))
+    for step, got in enumerate([early] + rounds[-2:]):
+        if step < half - 2:
+            mine, theirs = partial_product(context, other_context, list(zip(*got)))
+        else:
+            both = jnp.concatenate([context, other_context], axis=0)
+            product, start = 0.0, 0
+            for part in got[0]:
+                rows_in = both[:, start : start + part.shape[0]]
+                product += jnp.dot(rows_in, part, preferred_element_type=jnp.float32)
+                start += part.shape[0]
+            mine, theirs = product[:rows], product[rows:]
         pieces.append(mine)
         away.append(sent(theirs, "pair"))
     updated, *normed = finish(table, len(spans), residual, norm_gain, tags, pieces + away, PARTS)

time: 176 us -> 184 us (1.045)
  local copies, waits for them, and re-layouts: 6.15 us -> 12.9 us
  Pallas kernels: 17.9 us -> 13.6 us
  other arithmetic: 2.51 us -> 5.55 us
  matrix products: 27.3 us -> 30.1 us
    ppermute x51, starting transfers between devices: 36.1 us -> 41.7 us  [sent(): return lax.ppermute(array, 'ctx', ring[way])]
    unnamed x28 -> x42, local copies, waits for them, and re-layouts: 1.42 us -> 6.4 us
    ppermute x6, starting transfers between devices: 9.26 us -> 4.45 us  [shifted(): lax.ppermute(array, axis, [(i, (i + by) % devices) for i in range(devices)])]
    dot_general x0 -> x2, matrix products: none -> 2.78 us  [ringed(): product += jnp.dot(rows_in, part, preferred_element_type=jnp.float32)]
    pallas_call x3 -> x2, Pallas kernels: 8.77 us -> 6.38 us  [partial_product(): pl.pallas_call(functools.partial(partial_kernel, [len(part) for part in p...]
  transfers between devices with their start and end apart: 57 -> 57, of which waited for: 20 -> 23; matrix products, arithmetic and copies ran while one was open for 20% -> 21% of each run, Pallas kernels for 9% -> 7%
where the time goes in v3:
time: 184 us
  waiting for transfers between devices  74.3 us (40%)
  starting transfers between devices  46.2 us (25%)
  matrix products  30.1 us (16%)
  Pallas kernels  13.6 us (7%)
  local copies, waits for them, and re-layouts  12.9 us (7%)
  other arithmetic  5.55 us (3%)
    ppermute x51, waiting for transfers between devices, sent(): return lax.ppermute(array, 'ctx', ring[way])  53.3 us
    ppermute x51, starting transfers between devices, sent(): return lax.ppermute(array, 'ctx', ring[way])  41.7 us
    ppermute x6, waiting for transfers between devices, shifted(): lax.ppermute(array, axis, [(i, (i + by) % devices) for i in range(devices)])  21 us
    dot_general x8, matrix products, ringed(): jnp.dot(both[:, :width], w_gate_up[0], preferred_element_type=jnp.float32)  17.2 us
    dot_general x8, matrix products, ringed(): jnp.dot(hidden, w_down[0], preferred_element_type=jnp.float32)  8.53 us
    unnamed x42, local copies, waits for them, and re-layouts  6.4 us
    pallas_call x2, Pallas kernels, partial_product(): pl.pallas_call(functools.partial(partial_kernel, [len(part) for part in p...  6.38 us
    pallas_call x1, Pallas kernels, attention(): pl.pallas_call(functools.partial(attention_kernel, count), out_shape=jax....  5.7 us
  transfers between devices with their start and end apart: 57, of which 23 were waited for; matrix products, arithmetic and copies ran while one was open for 21% of the time, Pallas kernels for 7%

profile of v3, /device:TPU:0, one launch (start us, length us, event | category | flops | bytes accessed | tf_op | source)
XLA Modules:
  0.0 183.9 jit_solution(4050324161418600042)
XLA Ops:
  0.7 2.0 %fusion.192 = (bf16[1024,128]{1,0:T(8,128)(2,1)}, bf16[1024,128]{1,0:T(8,128)(2,1)}) fusion(bf16[2048,128]{1,0:T(8,128)(2,1)} %param.19), kind=kLoop, calls=%fused_computation.196 | loop fusion | bytes 1048576 | tf_op jit(solution)/shard_map/slice | solution.py:345
  2.7 3.0 %collective-permute-start.12 = (bf16[1024,128]{1,0:T(8,128)(2,1)}, bf16[1024,128]{1,0:T(8,128)(2,1)}, u32[]{:S(2)}, u32[]{:S(2)}) collective-permute-start(bf16[1024,128]{1,0:T(8,128)(2,1)} %get-tuple-element.14.refs_5_), channel_id=1, source_target_pairs={{0,2},{1,3},{2,6},{3,7},{4,0},{5,1},{6,10},{7,11},{8,4},{9,5},{10,... | collective-permute-start | bytes 786440 | tf_op jit(solution)/shard_map/ppermute | solution.py:323
  5.7 3.0 %collective-permute-start.1 = (bf16[128,256]{1,0:T(8,128)(2,1)}, bf16[128,256]{1,0:T(8,128)(2,1)S(1)}, u32[]{:S(2)}, u32[]{:S(2)}) collective-permute-start(bf16[128,256]{1,0:T(8,128)(2,1)} %refs_0_.1), channel_id=1, source_target_pairs={{0,8},{1,9},{2,10},{3,11},{4,12},{5,13},{6,14},{7,15},{8,0},{9,1},... | collective-permute-start | bytes 196616 | tf_op jit(solution)/shard_map/ppermute | solution.py:25
  8.8 1.3 collective-permute-start.2
  10.8 6.2 %collective-permute-done.refs_1_ = bf16[128,256]{1,0:T(8,128)(2,1)S(1)} collective-permute-done((bf16[128,256]{1,0:T(8,128)(2,1)}, bf16[128,256]{1,0:T(8,128)(2,1)S(1)}, u32[]{:S(2)}, u32[]{:S(2)}) %collective-permute-start) | collective-permute-done | bytes 65568 | tf_op jit(solution)/shard_map/ppermute | solution.py:25
  17.0 1.5 collective-permute-done.1.refs_2_
  18.4 1.5 collective-permute-start.8
  20.5 2.0 %collective-permute-start.14 = (bf16[1024,128]{1,0:T(8,128)(2,1)}, bf16[1024,128]{1,0:T(8,128)(2,1)}, u32[]{:S(2)}, u32[]{:S(2)}) collective-permute-start(bf16[1024,128]{1,0:T(8,128)(2,1)} %collective-permute-done.12.refs_7_), channel_id=1, source_target_pairs={{0,2},{1,3},{2,6},{3,7},{4,0},{5,1},{6,10},{7,11},{8,4},{9,5},{10,... | collective-permute-start | bytes 786440 | tf_op jit(solution)/shard_map/ppermute | solution.py:323
  22.5 1.5 collective-permute-done.3.refs_5_
  25.2 10.1 %collective-permute-done.4.refs_6_ = bf16[128,256]{1,0:T(8,128)(2,1)S(1)} collective-permute-done((bf16[128,256]{1,0:T(8,128)(2,1)}, bf16[128,256]{1,0:T(8,128)(2,1)S(1)}, u32[]{:S(2)}, u32[]{:S(2)}) %collective-permute-start.4) | collective-permute-done | bytes 65568 | tf_op jit(solution)/shard_map/ppermute | solution.py:25
  36.0 2.0 %collective-permute-start.9 = (bf16[1024,128]{1,0:T(8,128)(2,1)}, bf16[1024,128]{1,0:T(8,128)(2,1)S(1)}, u32[]{:S(2)}, u32[]{:S(2)}) collective-permute-start(bf16[1024,128]{1,0:T(8,128)(2,1)} %collective-permute-done.7.refs_1_), channel_id=1, source_target_pairs={{0,4},{1,5},{2,0},{3,1},{4,8},{5,9},{6,2},{7,3},{8,12},{9,13},{10,... | collective-permute-start | bytes 786440 | tf_op jit(solution)/shard_map/ppermute | solution.py:323
  38.0 1.8 collective-permute-done.5.refs_7_
  43.2 5.7 %attention.1.own_ref = bf16[128,2048]{1,0:T(8,128)(2,1)} custom-call(s32[20]{0:T(128)S(1)} %dynamic-slice_bitcast_fusion.table, s32[16]{0:T(128)S(1)} %copy-done.8, bf16[128,2048]{1,0:T(8,128)(2,1)S(1)} %copy-done.5, bf16[128,256]{1,0:T(8,128)(2,1)S(1)} %copy-done.6, bf16[128,256]{1,0:T(8,128)(2,1)S(1)} %collective-permute-done.refs_1_, ...), custom_call_target="tpu_custom_call" | custom-call | flops 536870912 | bytes 1572864 | tf_op jit(solution)/shard_map/attention/pallas_call | solution.py:213
  54.3 3.9 %collective-permute-done.10.refs_4_ = bf16[1024,128]{1,0:T(8,128)(2,1)S(1)} collective-permute-done((bf16[1024,128]{1,0:T(8,128)(2,1)}, bf16[1024,128]{1,0:T(8,128)(2,1)S(1)}, u32[]{:S(2)}, u32[]{:S(2)}) %collective-permute-start.10) | collective-permute-done | bytes 262176 | tf_op jit(solution)/shard_map/ppermute | solution.py:323
  60.4 3.6 %collective-permute-done.18.refs_3_ = bf16[1024,128]{1,0:T(8,128)(2,1)} collective-permute-done((bf16[1024,128]{1,0:T(8,128)(2,1)}, bf16[1024,128]{1,0:T(8,128)(2,1)}, u32[]{:S(2)}, u32[]{:S(2)}) %collective-permute-start.18) | collective-permute-done | bytes 262176 | tf_op jit(solution)/shard_map/ppermute | solution.py:323
  66.6 3.8 %partial_product.2 = (f32[128,640]{1,0:T(8,128)}, f32[128,640]{1,0:T(8,128)}) custom-call(bf16[128,2048]{1,0:T(8,128)(2,1)} %attention.1.own_ref, bf16[128,2048]{1,0:T(8,128)(2,1)} %collective-permute-done.6.other_ref, bf16[1024,128]{1,0:T(8,128)(2,1)} %get-tuple-element.15.refs_0_, bf16[1024,128]{1,0:T(8,128)(2,1)} %collective-permute-done.7.refs_1_, ...), custom_call_target="tpu_custom_call" | custom-call | flops 671088640 | bytes 3670016 | tf_op jit(solution)/shard_map/partial_product/pallas_call | solution.py:250
  70.5 2.6 %partial_product.3 = (f32[128,256]{1,0:T(8,128)}, f32[128,256]{1,0:T(8,128)}) custom-call(bf16[128,2048]{1,0:T(8,128)(2,1)} %attention.1.own_ref, bf16[128,2048]{1,0:T(8,128)(2,1)} %collective-permute-done.6.other_ref, bf16[1024,128]{1,0:T(8,128)(2,1)} %collective-permute-done.15.refs_0_, bf16[1024,128]{1,0:T(8,128)(2,1)} %collective-permute-done.16.refs_1_, ...), custom_call_target="tpu_custom_call" | custom-call | flops 268435456 | bytes 2097152 | tf_op jit(solution)/shard_map/partial_product/pallas_call | solution.py:250
  74.8 1.4 fusion.111
  76.2 1.4 convolution_add_fusion
  78.8 1.4 copy.19
  83.0 1.5 finish.1
  85.9 8.2 %collective-permute-done.26 = bf16[128,2176]{1,0:T(8,128)(2,1)S(1)} collective-permute-done((bf16[128,2176]{1,0:T(8,128)(2,1)S(1)}, bf16[128,2176]{1,0:T(8,128)(2,1)S(1)}, u32[]{:S(2)}, u32[]{:S(2)}) %collective-permute-start.26) | collective-permute-done | bytes 557088 | tf_op jit(solution)/shard_map/ppermute | solution.py:323
  94.6 1.5 collective-permute-done.45
  96.1 4.7 %fusion = f32[256,1536]{1,0:T(8,128)S(1)} fusion(bf16[1,2048,1536]{2,1,0:T(8,128)(2,1)} %param.21, bf16[256,2176]{1,0:T(8,128)(2,1)S(1)} %constant_dynamic-update-slice_fusion.14), kind=kOutput, calls=%fused_computation | convolution fusion | flops 1610612736 | bytes 8912896 | tf_op jit(solution)/shard_map/dot_general | solution.py:381
  102.4 1.8 fusion.14
  105.2 2.5 %collective-permute-start.47 = (bf16[128,2048]{1,0:T(8,128)(2,1)S(1)}, bf16[128,2048]{1,0:T(8,128)(2,1)S(1)}, u32[]{:S(2)}, u32[]{:S(2)}) collective-permute-start(bf16[128,2048]{1,0:T(8,128)(2,1)S(1)} %fusion.80), channel_id=1, source_target_pairs={{0,4},{1,3},{2,0},{3,7},{4,8},{5,1},{6,2},{7,11},{8,12},{9,5},{10,... | collective-permute-start | bytes 1572872 | tf_op jit(solution)/shard_map/ppermute | solution.py:323
  107.7 1.8 fusion.2
  111.1 3.1 %collective-permute-done.28 = bf16[128,2176]{1,0:T(8,128)(2,1)S(1)} collective-permute-done((bf16[128,2176]{1,0:T(8,128)(2,1)S(1)}, bf16[128,2176]{1,0:T(8,128)(2,1)S(1)}, u32[]{:S(2)}, u32[]{:S(2)}) %collective-permute-start.28) | collective-permute-done | bytes 557088 | tf_op jit(solution)/shard_map/ppermute | solution.py:323
  114.7 5.2 %collective-permute-done.47 = bf16[128,2048]{1,0:T(8,128)(2,1)S(1)} collective-permute-done((bf16[128,2048]{1,0:T(8,128)(2,1)S(1)}, bf16[128,2048]{1,0:T(8,128)(2,1)S(1)}, u32[]{:S(2)}, u32[]{:S(2)}) %collective-permute-start.47) | collective-permute-done | bytes 524320 | tf_op jit(solution)/shard_map/ppermute | solution.py:323
  120.6 1.8 fusion.4
  125.9 2.0 %collective-permute-start.30 = (bf16[128,2176]{1,0:T(8,128)(2,1)S(1)}, bf16[128,2176]{1,0:T(8,128)(2,1)S(1)}, u32[]{:S(2)}, u32[]{:S(2)}) collective-permute-start(bf16[128,2176]{1,0:T(8,128)(2,1)S(1)} %collective-permute-done.29), channel_id=1, source_target_pairs={{0,4},{1,3},{2,0},{3,7},{4,8},{5,1},{6,2},{7,11},{8,12},{9,5},{10,... | collective-permute-start | bytes 1671176 | tf_op jit(solution)/shard_map/ppermute | solution.py:323
  127.9 3.6 %collective-permute-done.48 = bf16[128,2048]{1,0:T(8,128)(2,1)S(1)} collective-permute-done((bf16[128,2048]{1,0:T(8,128)(2,1)S(1)}, bf16[128,2048]{1,0:T(8,128)(2,1)S(1)}, u32[]{:S(2)}, u32[]{:S(2)}) %collective-permute-start.48) | collective-permute-done | bytes 524320 | tf_op jit(solution)/shard_map/ppermute | solution.py:323
  132.4 1.8 fusion.6
  134.2 3.3 %collective-permute-done.30 = bf16[128,2176]{1,0:T(8,128)(2,1)S(1)} collective-permute-done((bf16[128,2176]{1,0:T(8,128)(2,1)S(1)}, bf16[128,2176]{1,0:T(8,128)(2,1)S(1)}, u32[]{:S(2)}, u32[]{:S(2)}) %collective-permute-start.30) | collective-permute-done | bytes 557088 | tf_op jit(solution)/shard_map/ppermute | solution.py:323
  139.6 1.8 fusion.8
  143.4 1.9 %collective-permute-start.50 = (bf16[128,2048]{1,0:T(8,128)(2,1)S(1)}, bf16[128,2048]{1,0:T(8,128)(2,1)S(1)}, u32[]{:S(2)}, u32[]{:S(2)}) collective-permute-start(bf16[128,2048]{1,0:T(8,128)(2,1)S(1)} %fusion.89), channel_id=1, source_target_pairs={{0,4},{1,3},{2,0},{3,7},{4,8},{5,1},{6,2},{7,11},{8,12},{9,5},{10,... | collective-permute-start | bytes 1572872 | tf_op jit(solution)/shard_map/ppermute | solution.py:323
  145.3 3.7 %collective-permute-done.31 = bf16[128,2176]{1,0:T(8,128)(2,1)S(1)} collective-permute-done((bf16[128,2176]{1,0:T(8,128)(2,1)S(1)}, bf16[128,2176]{1,0:T(8,128)(2,1)S(1)}, u32[]{:S(2)}, u32[]{:S(2)}) %collective-permute-start.31) | collective-permute-done | bytes 557088 | tf_op jit(solution)/shard_map/ppermute | solution.py:323
  149.7 5.0 %collective-permute-done.50 = bf16[128,2048]{1,0:T(8,128)(2,1)S(1)} collective-permute-done((bf16[128,2048]{1,0:T(8,128)(2,1)S(1)}, bf16[128,2048]{1,0:T(8,128)(2,1)S(1)}, u32[]{:S(2)}, u32[]{:S(2)}) %collective-permute-start.50) | collective-permute-done | bytes 524320 | tf_op jit(solution)/shard_map/ppermute | solution.py:323
  155.4 1.8 fusion.10
  158.7 2.3 %collective-permute-start.54 = (bf16[48,2048]{1,0:T(8,128)(2,1)S(1)}, bf16[48,2048]{1,0:T(8,128)(2,1)S(1)}, u32[]{:S(2)}, u32[]{:S(2)}) collective-permute-start(bf16[48,2048]{1,0:T(8,128)(2,1)S(1)} %fusion.153), channel_id=1, source_target_pairs={{0,4},{1,3},{2,0},{3,7},{4,8},{5,1},{6,2},{7,11},{8,12},{9,5},{10,... | collective-permute-start | bytes 589832 | tf_op jit(solution)/shard_map/ppermute | solution.py:323
  161.1 1.8 collective-permute-done.33
  163.0 1.8 fusion.12
  166.4 1.9 %collective-permute-start.52 = (bf16[80,2048]{1,0:T(8,128)(2,1)S(1)}, bf16[80,2048]{1,0:T(8,128)(2,1)S(1)}, u32[]{:S(2)}, u32[]{:S(2)}) collective-permute-start(bf16[80,2048]{1,0:T(8,128)(2,1)S(1)} %fusion.107), channel_id=1, source_target_pairs={{0,4},{1,3},{2,0},{3,7},{4,8},{5,1},{6,2},{7,11},{8,12},{9,5},{10,... | collective-permute-start | bytes 983048 | tf_op jit(solution)/shard_map/ppermute | solution.py:323
  168.3 1.8 collective-permute-start.55
  170.2 3.3 %collective-permute-done.52 = bf16[80,2048]{1,0:T(8,128)(2,1)S(1)} collective-permute-done((bf16[80,2048]{1,0:T(8,128)(2,1)S(1)}, bf16[80,2048]{1,0:T(8,128)(2,1)S(1)}, u32[]{:S(2)}, u32[]{:S(2)}) %collective-permute-start.52) | collective-permute-done | bytes 327712 | tf_op jit(solution)/shard_map/ppermute | solution.py:323
  173.6 1.9 %collective-permute-start.53 = (bf16[80,2048]{1,0:T(8,128)(2,1)S(1)}, bf16[80,2048]{1,0:T(8,128)(2,1)S(1)}, u32[]{:S(2)}, u32[]{:S(2)}) collective-permute-start(bf16[80,2048]{1,0:T(8,128)(2,1)S(1)} %fusion.108), channel_id=1, source_target_pairs={{0,4},{1,3},{2,0},{3,7},{4,8},{5,1},{6,2},{7,11},{8,12},{9,5},{10,... | collective-permute-start | bytes 983048 | tf_op jit(solution)/shard_map/ppermute | solution.py:323
  175.7 1.9 %collective-permute-start.56 = (bf16[48,2048]{1,0:T(8,128)(2,1)S(1)}, bf16[48,2048]{1,0:T(8,128)(2,1)S(1)}, u32[]{:S(2)}, u32[]{:S(2)}) collective-permute-start(bf16[48,2048]{1,0:T(8,128)(2,1)S(1)} %fusion.155), channel_id=1, source_target_pairs={{0,4},{1,3},{2,0},{3,7},{4,8},{5,1},{6,2},{7,11},{8,12},{9,5},{10,... | collective-permute-start | bytes 589832 | tf_op jit(solution)/shard_map/ppermute | solution.py:323
  177.5 5.3 %collective-permute-done.56 = bf16[48,2048]{1,0:T(8,128)(2,1)S(1)} collective-permute-done((bf16[48,2048]{1,0:T(8,128)(2,1)S(1)}, bf16[48,2048]{1,0:T(8,128)(2,1)S(1)}, u32[]{:S(2)}, u32[]{:S(2)}) %collective-permute-start.56) | collective-permute-done | bytes 196640 | tf_op jit(solution)/shard_map/ppermute | solution.py:323
  (181 shorter events, 44.4 us)
Async XLA Ops:
  2.7 17.8 %collective-permute-start.12 = (bf16[1024,128]{1,0:T(8,128)(2,1)}, bf16[1024,128]{1,0:T(8,128)(2,1)}, u32[]{:S(2)}, u32[]{:S(2)}) collective-permute-start(bf16[1024,128]{1,0:T(8,128)(2,1)} %get-tuple-element.14.refs_5_), channel_id=1, source_target_pairs={{0,2},{1,3},{2,6},{3,7},{4,0},{5,1},{6,10},{7,11},{8,4},{9,5},{10,... | collective-permute-start | bytes 786440 | tf_op jit(solution)/shard_map/ppermute | solution.py:323
  5.7 11.3 %collective-permute-start = (bf16[128,256]{1,0:T(8,128)(2,1)}, bf16[128,256]{1,0:T(8,128)(2,1)S(1)}, u32[]{:S(2)}, u32[]{:S(2)}) collective-permute-start(bf16[128,256]{1,0:T(8,128)(2,1)} %refs_0_.1), channel_id=1, source_target_pairs={{0,4},{1,5},{2,6},{3,7},{4,8},{5,9},{6,10},{7,11},{8,12},{9,13},{1... | collective-permute-start | bytes 196616 | tf_op jit(solution)/shard_map/ppermute | solution.py:25
  5.7 12.7 %collective-permute-start.1 = (bf16[128,256]{1,0:T(8,128)(2,1)}, bf16[128,256]{1,0:T(8,128)(2,1)S(1)}, u32[]{:S(2)}, u32[]{:S(2)}) collective-permute-start(bf16[128,256]{1,0:T(8,128)(2,1)} %refs_0_.1), channel_id=1, source_target_pairs={{0,8},{1,9},{2,10},{3,11},{4,12},{5,13},{6,14},{7,15},{8,0},{9,1},... | collective-permute-start | bytes 196616 | tf_op jit(solution)/shard_map/ppermute | solution.py:25
  8.8 11.1 %collective-permute-start.2 = (bf16[128,256]{1,0:T(8,128)(2,1)}, bf16[128,256]{1,0:T(8,128)(2,1)S(1)}, u32[]{:S(2)}, u32[]{:S(2)}) collective-permute-start(bf16[128,256]{1,0:T(8,128)(2,1)} %refs_0_.1), channel_id=1, source_target_pairs={{0,12},{1,13},{2,14},{3,15},{4,0},{5,1},{6,2},{7,3},{8,4},{9,5},{1... | collective-permute-start | bytes 196616 | tf_op jit(solution)/shard_map/ppermute | solution.py:25
  10.1 25.9 %collective-permute-start.7 = (bf16[1024,128]{1,0:T(8,128)(2,1)}, bf16[1024,128]{1,0:T(8,128)(2,1)}, u32[]{:S(2)}, u32[]{:S(2)}) collective-permute-start(bf16[1024,128]{1,0:T(8,128)(2,1)} %get-tuple-element.15.refs_0_), channel_id=1, source_target_pairs={{0,4},{1,5},{2,0},{3,1},{4,8},{5,9},{6,2},{7,3},{8,12},{9,13},{10,... | collective-permute-start | bytes 786440 | tf_op jit(solution)/shard_map/ppermute | solution.py:323
  17.0 7.0 %collective-permute-start.3 = (bf16[128,256]{1,0:T(8,128)(2,1)}, bf16[128,256]{1,0:T(8,128)(2,1)S(1)}, u32[]{:S(2)}, u32[]{:S(2)}) collective-permute-start(bf16[128,256]{1,0:T(8,128)(2,1)} %refs_4_.1), channel_id=1, source_target_pairs={{0,4},{1,5},{2,6},{3,7},{4,8},{5,9},{6,10},{7,11},{8,12},{9,13},{1... | collective-permute-start | bytes 196616 | tf_op jit(solution)/shard_map/ppermute | solution.py:25
  18.4 30.4 %collective-permute-start.8 = (bf16[1024,128]{1,0:T(8,128)(2,1)}, bf16[1024,128]{1,0:T(8,128)(2,1)}, u32[]{:S(2)}, u32[]{:S(2)}) collective-permute-start(bf16[1024,128]{1,0:T(8,128)(2,1)} %get-tuple-element.15.refs_0_), channel_id=1, source_target_pairs={{0,2},{1,3},{2,6},{3,7},{4,0},{5,1},{6,10},{7,11},{8,4},{9,5},{10,... | collective-permute-start | bytes 786440 | tf_op jit(solution)/shard_map/ppermute | solution.py:323
  19.9 29.9 %collective-permute-start.11 = (bf16[1024,128]{1,0:T(8,128)(2,1)}, bf16[1024,128]{1,0:T(8,128)(2,1)}, u32[]{:S(2)}, u32[]{:S(2)}) collective-permute-start(bf16[1024,128]{1,0:T(8,128)(2,1)} %get-tuple-element.14.refs_5_), channel_id=1, source_target_pairs={{0,4},{1,5},{2,0},{3,1},{4,8},{5,9},{6,2},{7,3},{8,12},{9,13},{10,... | collective-permute-start | bytes 786440 | tf_op jit(solution)/shard_map/ppermute | solution.py:323
  20.5 30.4 %collective-permute-start.14 = (bf16[1024,128]{1,0:T(8,128)(2,1)}, bf16[1024,128]{1,0:T(8,128)(2,1)}, u32[]{:S(2)}, u32[]{:S(2)}) collective-permute-start(bf16[1024,128]{1,0:T(8,128)(2,1)} %collective-permute-done.12.refs_7_), channel_id=1, source_target_pairs={{0,2},{1,3},{2,6},{3,7},{4,0},{5,1},{6,10},{7,11},{8,4},{9,5},{10,... | collective-permute-start | bytes 786440 | tf_op jit(solution)/shard_map/ppermute | solution.py:323
  24.0 11.3 %collective-permute-start.4 = (bf16[128,256]{1,0:T(8,128)(2,1)}, bf16[128,256]{1,0:T(8,128)(2,1)S(1)}, u32[]{:S(2)}, u32[]{:S(2)}) collective-permute-start(bf16[128,256]{1,0:T(8,128)(2,1)} %refs_4_.1), channel_id=1, source_target_pairs={{0,8},{1,9},{2,10},{3,11},{4,12},{5,13},{6,14},{7,15},{8,0},{9,1},... | collective-permute-start | bytes 196616 | tf_op jit(solution)/shard_map/ppermute | solution.py:25
  36.0 16.5 %collective-permute-start.9 = (bf16[1024,128]{1,0:T(8,128)(2,1)}, bf16[1024,128]{1,0:T(8,128)(2,1)S(1)}, u32[]{:S(2)}, u32[]{:S(2)}) collective-permute-start(bf16[1024,128]{1,0:T(8,128)(2,1)} %collective-permute-done.7.refs_1_), channel_id=1, source_target_pairs={{0,4},{1,5},{2,0},{3,1},{4,8},{5,9},{6,2},{7,3},{8,12},{9,13},{10,... | collective-permute-start | bytes 786440 | tf_op jit(solution)/shard_map/ppermute | solution.py:323
  48.9 17.8 %collective-permute-start.6 = (bf16[128,2048]{1,0:T(8,128)(2,1)}, bf16[128,2048]{1,0:T(8,128)(2,1)}, u32[]{:S(2)}, u32[]{:S(2)}) collective-permute-start(bf16[128,2048]{1,0:T(8,128)(2,1)} %attention.1.own_ref), channel_id=1, source_target_pairs={{0,1},{1,0},{2,3},{3,2},{4,5},{5,4},{6,7},{7,6},{8,9},{9,8},{10,11... | collective-permute-start | bytes 1572872 | tf_op jit(solution)/shard_map/ppermute | solution.py:323
  48.9 9.4 %collective-permute-start.10 = (bf16[1024,128]{1,0:T(8,128)(2,1)}, bf16[1024,128]{1,0:T(8,128)(2,1)S(1)}, u32[]{:S(2)}, u32[]{:S(2)}) collective-permute-start(bf16[1024,128]{1,0:T(8,128)(2,1)} %collective-permute-done.8.refs_2_), channel_id=1, source_target_pairs={{0,2},{1,3},{2,6},{3,7},{4,0},{5,1},{6,10},{7,11},{8,4},{9,5},{10,... | collective-permute-start | bytes 786440 | tf_op jit(solution)/shard_map/ppermute | solution.py:323
  49.8 9.5 %collective-permute-start.13 = (bf16[1024,128]{1,0:T(8,128)(2,1)}, bf16[1024,128]{1,0:T(8,128)(2,1)}, u32[]{:S(2)}, u32[]{:S(2)}) collective-permute-start(bf16[1024,128]{1,0:T(8,128)(2,1)} %collective-permute-done.11.refs_6_), channel_id=1, source_target_pairs={{0,4},{1,5},{2,0},{3,1},{4,8},{5,9},{6,2},{7,3},{8,12},{9,13},{10,... | collective-permute-start | bytes 786440 | tf_op jit(solution)/shard_map/ppermute | solution.py:323
  50.9 13.1 %collective-permute-start.18 = (bf16[1024,128]{1,0:T(8,128)(2,1)}, bf16[1024,128]{1,0:T(8,128)(2,1)}, u32[]{:S(2)}, u32[]{:S(2)}) collective-permute-start(bf16[1024,128]{1,0:T(8,128)(2,1)} %collective-permute-done.14.refs_9_), channel_id=1, source_target_pairs={{0,2},{1,3},{2,6},{3,7},{4,0},{5,1},{6,10},{7,11},{8,4},{9,5},{10,... | collective-permute-start | bytes 786440 | tf_op jit(solution)/shard_map/ppermute | solution.py:323
  53.2 12.3 %collective-permute-start.15 = (bf16[1024,128]{1,0:T(8,128)(2,1)S(1)}, bf16[1024,128]{1,0:T(8,128)(2,1)}, u32[]{:S(2)}, u32[]{:S(2)}) collective-permute-start(bf16[1024,128]{1,0:T(8,128)(2,1)S(1)} %collective-permute-done.9.refs_3_), channel_id=1, source_target_pairs={{0,4},{1,5},{2,0},{3,1},{4,8},{5,9},{6,2},{7,3},{8,12},{9,13},{10,... | collective-permute-start | bytes 786440 | tf_op jit(solution)/shard_map/ppermute | solution.py:323
  58.3 12.1 %collective-permute-start.16 = (bf16[1024,128]{1,0:T(8,128)(2,1)S(1)}, bf16[1024,128]{1,0:T(8,128)(2,1)}, u32[]{:S(2)}, u32[]{:S(2)}) collective-permute-start(bf16[1024,128]{1,0:T(8,128)(2,1)S(1)} %collective-permute-done.10.refs_4_), channel_id=1, source_target_pairs={{0,2},{1,3},{2,6},{3,7},{4,0},{5,1},{6,10},{7,11},{8,4},{9,5},{10,... | collective-permute-start | bytes 786440 | tf_op jit(solution)/shard_map/ppermute | solution.py:323
  59.3 11.2 %collective-permute-start.17 = (bf16[1024,128]{1,0:T(8,128)(2,1)}, bf16[1024,128]{1,0:T(8,128)(2,1)}, u32[]{:S(2)}, u32[]{:S(2)}) collective-permute-start(bf16[1024,128]{1,0:T(8,128)(2,1)} %collective-permute-done.13.refs_8_), channel_id=1, source_target_pairs={{0,4},{1,5},{2,0},{3,1},{4,8},{5,9},{6,2},{7,3},{8,12},{9,13},{10,... | collective-permute-start | bytes 786440 | tf_op jit(solution)/shard_map/ppermute | solution.py:323
  64.0 10.8 %collective-permute-start.20 = (bf16[1024,128]{1,0:T(8,128)(2,1)}, bf16[1024,128]{1,0:T(8,128)(2,1)}, u32[]{:S(2)}, u32[]{:S(2)}) collective-permute-start(bf16[1024,128]{1,0:T(8,128)(2,1)} %collective-permute-done.18.refs_3_), channel_id=1, source_target_pairs={{0,2},{1,3},{2,6},{3,7},{4,0},{5,1},{6,10},{7,11},{8,4},{9,5},{10,... | collective-permute-start | bytes 786440 | tf_op jit(solution)/shard_map/ppermute | solution.py:323
  65.5 10.6 %collective-permute-start.19 = (bf16[1024,128]{1,0:T(8,128)(2,1)}, bf16[1024,128]{1,0:T(8,128)(2,1)}, u32[]{:S(2)}, u32[]{:S(2)}) collective-permute-start(bf16[1024,128]{1,0:T(8,128)(2,1)} %collective-permute-done.15.refs_0_), channel_id=1, source_target_pairs={{0,4},{1,5},{2,0},{3,1},{4,8},{5,9},{6,2},{7,3},{8,12},{9,13},{10,... | collective-permute-start | bytes 786440 | tf_op jit(solution)/shard_map/ppermute | solution.py:323
  70.4 10.6 %collective-permute-start.21 = (f32[128,640]{1,0:T(8,128)}, f32[128,640]{1,0:T(8,128)}, u32[]{:S(2)}, u32[]{:S(2)}) collective-permute-start(f32[128,640]{1,0:T(8,128)} %get-tuple-element.10), channel_id=1, source_target_pairs={{0,1},{1,0},{2,3},{3,2},{4,5},{5,4},{6,7},{7,6},{8,9},{9,8},{10,11... | collective-permute-start | bytes 983048 | tf_op jit(solution)/shard_map/ppermute | solution.py:323
  73.2 7.8 %collective-permute-start.22 = (f32[128,256]{1,0:T(8,128)}, f32[128,256]{1,0:T(8,128)}, u32[]{:S(2)}, u32[]{:S(2)}) collective-permute-start(f32[128,256]{1,0:T(8,128)} %get-tuple-element.11), channel_id=1, source_target_pairs={{0,1},{1,0},{2,3},{3,2},{4,5},{5,4},{6,7},{7,6},{8,9},{9,8},{10,11... | collective-permute-start | bytes 393224 | tf_op jit(solution)/shard_map/ppermute | solution.py:323
  84.5 9.6 %collective-permute-start.26 = (bf16[128,2176]{1,0:T(8,128)(2,1)S(1)}, bf16[128,2176]{1,0:T(8,128)(2,1)S(1)}, u32[]{:S(2)}, u32[]{:S(2)}) collective-permute-start(bf16[128,2176]{1,0:T(8,128)(2,1)S(1)} %get-tuple-element.13), channel_id=1, source_target_pairs={{0,4},{1,3},{2,0},{3,7},{4,8},{5,1},{6,2},{7,11},{8,12},{9,5},{10,... | collective-permute-start | bytes 1671176 | tf_op jit(solution)/shard_map/ppermute | solution.py:323
  85.0 9.5 %collective-permute-start.24 = (bf16[128,2176]{1,0:T(8,128)(2,1)S(1)}, bf16[128,2176]{1,0:T(8,128)(2,1)S(1)}, u32[]{:S(2)}, u32[]{:S(2)}) collective-permute-start(bf16[128,2176]{1,0:T(8,128)(2,1)S(1)} %get-tuple-element.13), channel_id=1, source_target_pairs={{0,1},{1,0},{2,3},{3,2},{4,5},{5,4},{6,7},{7,6},{8,9},{9,8},{10,11... | collective-permute-start | bytes 1671176 | tf_op jit(solution)/shard_map/ppermute | solution.py:323
  94.1 10.1 %collective-permute-start.27 = (bf16[128,2176]{1,0:T(8,128)(2,1)S(1)}, bf16[128,2176]{1,0:T(8,128)(2,1)S(1)}, u32[]{:S(2)}, u32[]{:S(2)}) collective-permute-start(bf16[128,2176]{1,0:T(8,128)(2,1)S(1)} %collective-permute-done.26), channel_id=1, source_target_pairs={{0,4},{1,3},{2,0},{3,7},{4,8},{5,1},{6,2},{7,11},{8,12},{9,5},{10,... | collective-permute-start | bytes 1671176 | tf_op jit(solution)/shard_map/ppermute | solution.py:323
  104.7 9.6 %collective-permute-start.28 = (bf16[128,2176]{1,0:T(8,128)(2,1)S(1)}, bf16[128,2176]{1,0:T(8,128)(2,1)S(1)}, u32[]{:S(2)}, u32[]{:S(2)}) collective-permute-start(bf16[128,2176]{1,0:T(8,128)(2,1)S(1)} %collective-permute-done.27), channel_id=1, source_target_pairs={{0,4},{1,3},{2,0},{3,7},{4,8},{5,1},{6,2},{7,11},{8,12},{9,5},{10,... | collective-permute-start | bytes 1671176 | tf_op jit(solution)/shard_map/ppermute | solution.py:323
  105.2 14.7 %collective-permute-start.47 = (bf16[128,2048]{1,0:T(8,128)(2,1)S(1)}, bf16[128,2048]{1,0:T(8,128)(2,1)S(1)}, u32[]{:S(2)}, u32[]{:S(2)}) collective-permute-start(bf16[128,2048]{1,0:T(8,128)(2,1)S(1)} %fusion.80), channel_id=1, source_target_pairs={{0,4},{1,3},{2,0},{3,7},{4,8},{5,1},{6,2},{7,11},{8,12},{9,5},{10,... | collective-permute-start | bytes 1572872 | tf_op jit(solution)/shard_map/ppermute | solution.py:323
  110.9 9.0 %collective-permute-start.44 = (bf16[128,2048]{1,0:T(8,128)(2,1)S(1)}, bf16[128,2048]{1,0:T(8,128)(2,1)S(1)}, u32[]{:S(2)}, u32[]{:S(2)}) collective-permute-start(bf16[128,2048]{1,0:T(8,128)(2,1)S(1)} %slice.481), channel_id=1, source_target_pairs={{0,1},{1,0},{2,3},{3,2},{4,5},{5,4},{6,7},{7,6},{8,9},{9,8},{10,11... | collective-permute-start | bytes 1572872 | tf_op jit(solution)/shard_map/ppermute | solution.py:323
  114.3 6.3 %collective-permute-start.41 = (bf16[128,2176]{1,0:T(8,128)(2,1)S(1)}, bf16[128,2176]{1,0:T(8,128)(2,1)S(1)}, u32[]{:S(2)}, u32[]{:S(2)}) collective-permute-start(bf16[128,2176]{1,0:T(8,128)(2,1)S(1)} %collective-permute-done.28), channel_id=1, source_target_pairs={{0,1},{1,0},{2,3},{3,2},{4,5},{5,4},{6,7},{7,6},{8,9},{9,8},{10,11... | collective-permute-start | bytes 1671176 | tf_op jit(solution)/shard_map/ppermute | solution.py:323
  114.3 11.5 %collective-permute-start.29 = (bf16[128,2176]{1,0:T(8,128)(2,1)S(1)}, bf16[128,2176]{1,0:T(8,128)(2,1)S(1)}, u32[]{:S(2)}, u32[]{:S(2)}) collective-permute-start(bf16[128,2176]{1,0:T(8,128)(2,1)S(1)} %collective-permute-done.28), channel_id=1, source_target_pairs={{0,4},{1,3},{2,0},{3,7},{4,8},{5,1},{6,2},{7,11},{8,12},{9,5},{10,... | collective-permute-start | bytes 1671176 | tf_op jit(solution)/shard_map/ppermute | solution.py:323
  120.1 11.4 %collective-permute-start.48 = (bf16[128,2048]{1,0:T(8,128)(2,1)S(1)}, bf16[128,2048]{1,0:T(8,128)(2,1)S(1)}, u32[]{:S(2)}, u32[]{:S(2)}) collective-permute-start(bf16[128,2048]{1,0:T(8,128)(2,1)S(1)} %fusion.83), channel_id=1, source_target_pairs={{0,4},{1,3},{2,0},{3,7},{4,8},{5,1},{6,2},{7,11},{8,12},{9,5},{10,... | collective-permute-start | bytes 1572872 | tf_op jit(solution)/shard_map/ppermute | solution.py:323
  123.7 7.8 %collective-permute-start.42 = (bf16[128,2048]{1,0:T(8,128)(2,1)S(1)}, bf16[128,2048]{1,0:T(8,128)(2,1)S(1)}, u32[]{:S(2)}, u32[]{:S(2)}) collective-permute-start(bf16[128,2048]{1,0:T(8,128)(2,1)S(1)} %slice.482), channel_id=1, source_target_pairs={{0,1},{1,0},{2,3},{3,2},{4,5},{5,4},{6,7},{7,6},{8,9},{9,8},{10,11... | collective-permute-start | bytes 1572872 | tf_op jit(solution)/shard_map/ppermute | solution.py:323
  124.9 52.6 %collective-permute-start.25 = (bf16[128,2048]{1,0:T(8,128)(2,1)S(1)}, bf16[128,2048]{1,0:T(8,128)(2,1)S(1)}, u32[]{:S(2)}, u32[]{:S(2)}) collective-permute-start(bf16[128,2048]{1,0:T(8,128)(2,1)S(1)} %slice.487), channel_id=1, source_target_pairs={{0,1},{1,0},{2,3},{3,2},{4,5},{5,4},{6,7},{7,6},{8,9},{9,8},{10,11... | collective-permute-start | bytes 1572872 | tf_op jit(solution)/shard_map/ppermute | solution.py:323
  125.9 6.3 %collective-permute-start.39 = (bf16[128,2176]{1,0:T(8,128)(2,1)S(1)}, bf16[128,2176]{1,0:T(8,128)(2,1)S(1)}, u32[]{:S(2)}, u32[]{:S(2)}) collective-permute-start(bf16[128,2176]{1,0:T(8,128)(2,1)S(1)} %collective-permute-done.29), channel_id=1, source_target_pairs={{0,1},{1,0},{2,3},{3,2},{4,5},{5,4},{6,7},{7,6},{8,9},{9,8},{10,11... | collective-permute-start | bytes 1671176 | tf_op jit(solution)/shard_map/ppermute | solution.py:323
  125.9 11.5 %collective-permute-start.30 = (bf16[128,2176]{1,0:T(8,128)(2,1)S(1)}, bf16[128,2176]{1,0:T(8,128)(2,1)S(1)}, u32[]{:S(2)}, u32[]{:S(2)}) collective-permute-start(bf16[128,2176]{1,0:T(8,128)(2,1)S(1)} %collective-permute-done.29), channel_id=1, source_target_pairs={{0,4},{1,3},{2,0},{3,7},{4,8},{5,1},{6,2},{7,11},{8,12},{9,5},{10,... | collective-permute-start | bytes 1671176 | tf_op jit(solution)/shard_map/ppermute | solution.py:323
  131.7 11.5 %collective-permute-start.49 = (bf16[128,2048]{1,0:T(8,128)(2,1)S(1)}, bf16[128,2048]{1,0:T(8,128)(2,1)S(1)}, u32[]{:S(2)}, u32[]{:S(2)}) collective-permute-start(bf16[128,2048]{1,0:T(8,128)(2,1)S(1)} %fusion.86), channel_id=1, source_target_pairs={{0,4},{1,3},{2,0},{3,7},{4,8},{5,1},{6,2},{7,11},{8,12},{9,5},{10,... | collective-permute-start | bytes 1572872 | tf_op jit(solution)/shard_map/ppermute | solution.py:323
  138.6 4.6 %collective-permute-start.40 = (bf16[128,2048]{1,0:T(8,128)(2,1)S(1)}, bf16[128,2048]{1,0:T(8,128)(2,1)S(1)}, u32[]{:S(2)}, u32[]{:S(2)}) collective-permute-start(bf16[128,2048]{1,0:T(8,128)(2,1)S(1)} %slice.483), channel_id=1, source_target_pairs={{0,1},{1,0},{2,3},{3,2},{4,5},{5,4},{6,7},{7,6},{8,9},{9,8},{10,11... | collective-permute-start | bytes 1572872 | tf_op jit(solution)/shard_map/ppermute | solution.py:323
  139.2 9.9 %collective-permute-start.31 = (bf16[128,2176]{1,0:T(8,128)(2,1)S(1)}, bf16[128,2176]{1,0:T(8,128)(2,1)S(1)}, u32[]{:S(2)}, u32[]{:S(2)}) collective-permute-start(bf16[128,2176]{1,0:T(8,128)(2,1)S(1)} %collective-permute-done.30), channel_id=1, source_target_pairs={{0,4},{1,3},{2,0},{3,7},{4,8},{5,1},{6,2},{7,11},{8,12},{9,5},{10,... | collective-permute-start | bytes 1671176 | tf_op jit(solution)/shard_map/ppermute | solution.py:323
  142.8 6.8 %collective-permute-start.38 = (bf16[128,2048]{1,0:T(8,128)(2,1)S(1)}, bf16[128,2048]{1,0:T(8,128)(2,1)S(1)}, u32[]{:S(2)}, u32[]{:S(2)}) collective-permute-start(bf16[128,2048]{1,0:T(8,128)(2,1)S(1)} %slice.484), channel_id=1, source_target_pairs={{0,1},{1,0},{2,3},{3,2},{4,5},{5,4},{6,7},{7,6},{8,9},{9,8},{10,11... | collective-permute-start | bytes 1572872 | tf_op jit(solution)/shard_map/ppermute | solution.py:323
  143.4 11.2 %collective-permute-start.50 = (bf16[128,2048]{1,0:T(8,128)(2,1)S(1)}, bf16[128,2048]{1,0:T(8,128)(2,1)S(1)}, u32[]{:S(2)}, u32[]{:S(2)}) collective-permute-start(bf16[128,2048]{1,0:T(8,128)(2,1)S(1)} %fusion.89), channel_id=1, source_target_pairs={{0,4},{1,3},{2,0},{3,7},{4,8},{5,1},{6,2},{7,11},{8,12},{9,5},{10,... | collective-permute-start | bytes 1572872 | tf_op jit(solution)/shard_map/ppermute | solution.py:323
  149.1 6.3 %collective-permute-start.35 = (bf16[128,2176]{1,0:T(8,128)(2,1)S(1)}, bf16[128,2176]{1,0:T(8,128)(2,1)S(1)}, u32[]{:S(2)}, u32[]{:S(2)}) collective-permute-start(bf16[128,2176]{1,0:T(8,128)(2,1)S(1)} %collective-permute-done.31), channel_id=1, source_target_pairs={{0,1},{1,0},{2,3},{3,2},{4,5},{5,4},{6,7},{7,6},{8,9},{9,8},{10,11... | collective-permute-start | bytes 1671176 | tf_op jit(solution)/shard_map/ppermute | solution.py:323
  149.2 11.8 %collective-permute-start.32 = (bf16[128,2176]{1,0:T(8,128)(2,1)S(1)}, bf16[128,2176]{1,0:T(8,128)(2,1)S(1)}, u32[]{:S(2)}, u32[]{:S(2)}) collective-permute-start(bf16[128,2176]{1,0:T(8,128)(2,1)S(1)} %collective-permute-done.31), channel_id=1, source_target_pairs={{0,4},{1,3},{2,0},{3,7},{4,8},{5,1},{6,2},{7,11},{8,12},{9,5},{10,... | collective-permute-start | bytes 1671176 | tf_op jit(solution)/shard_map/ppermute | solution.py:323
  154.7 11.6 %collective-permute-start.51 = (bf16[80,2048]{1,0:T(8,128)(2,1)S(1)}, bf16[80,2048]{1,0:T(8,128)(2,1)S(1)}, u32[]{:S(2)}, u32[]{:S(2)}) collective-permute-start(bf16[80,2048]{1,0:T(8,128)(2,1)S(1)} %fusion.106), channel_id=1, source_target_pairs={{0,4},{1,3},{2,0},{3,7},{4,8},{5,1},{6,2},{7,11},{8,12},{9,5},{10,... | collective-permute-start | bytes 983048 | tf_op jit(solution)/shard_map/ppermute | solution.py:323
  158.7 9.6 %collective-permute-start.54 = (bf16[48,2048]{1,0:T(8,128)(2,1)S(1)}, bf16[48,2048]{1,0:T(8,128)(2,1)S(1)}, u32[]{:S(2)}, u32[]{:S(2)}) collective-permute-start(bf16[48,2048]{1,0:T(8,128)(2,1)S(1)} %fusion.153), channel_id=1, source_target_pairs={{0,4},{1,3},{2,0},{3,7},{4,8},{5,1},{6,2},{7,11},{8,12},{9,5},{10,... | collective-permute-start | bytes 589832 | tf_op jit(solution)/shard_map/ppermute | solution.py:323
  166.4 7.1 %collective-permute-start.52 = (bf16[80,2048]{1,0:T(8,128)(2,1)S(1)}, bf16[80,2048]{1,0:T(8,128)(2,1)S(1)}, u32[]{:S(2)}, u32[]{:S(2)}) collective-permute-start(bf16[80,2048]{1,0:T(8,128)(2,1)S(1)} %fusion.107), channel_id=1, source_target_pairs={{0,4},{1,3},{2,0},{3,7},{4,8},{5,1},{6,2},{7,11},{8,12},{9,5},{10,... | collective-permute-start | bytes 983048 | tf_op jit(solution)/shard_map/ppermute | solution.py:323
  168.3 7.3 %collective-permute-start.55 = (bf16[48,2048]{1,0:T(8,128)(2,1)S(1)}, bf16[48,2048]{1,0:T(8,128)(2,1)S(1)}, u32[]{:S(2)}, u32[]{:S(2)}) collective-permute-start(bf16[48,2048]{1,0:T(8,128)(2,1)S(1)} %fusion.154), channel_id=1, source_target_pairs={{0,4},{1,3},{2,0},{3,7},{4,8},{5,1},{6,2},{7,11},{8,12},{9,5},{10,... | collective-permute-start | bytes 589832 | tf_op jit(solution)/shard_map/ppermute | solution.py:323
  173.6 9.2 %collective-permute-start.53 = (bf16[80,2048]{1,0:T(8,128)(2,1)S(1)}, bf16[80,2048]{1,0:T(8,128)(2,1)S(1)}, u32[]{:S(2)}, u32[]{:S(2)}) collective-permute-start(bf16[80,2048]{1,0:T(8,128)(2,1)S(1)} %fusion.108), channel_id=1, source_target_pairs={{0,4},{1,3},{2,0},{3,7},{4,8},{5,1},{6,2},{7,11},{8,12},{9,5},{10,... | collective-permute-start | bytes 983048 | tf_op jit(solution)/shard_map/ppermute | solution.py:323
  175.7 7.2 %collective-permute-start.56 = (bf16[48,2048]{1,0:T(8,128)(2,1)S(1)}, bf16[48,2048]{1,0:T(8,128)(2,1)S(1)}, u32[]{:S(2)}, u32[]{:S(2)}) collective-permute-start(bf16[48,2048]{1,0:T(8,128)(2,1)S(1)} %fusion.155), channel_id=1, source_target_pairs={{0,4},{1,3},{2,0},{3,7},{4,8},{5,1},{6,2},{7,11},{8,12},{9,5},{10,... | collective-permute-start | bytes 589832 | tf_op jit(solution)/shard_map/ppermute | solution.py:323
  (26 other events, 284.3 us)
